TPU v7x, 512 devices: a whole 4x8x8 slice. The times are simulated.
512 devices in a mesh: vocab: 16 (over y, core), rows: 8 (over z), seq: 4 (over x).
Axes of the slice: x: 4, y: 8, z: 8, core: 2. Of those that a mesh axis runs over, the one named last changes fastest.
Arguments:
- hidden: bfloat16 [1024, 16384], P(('vocab', 'seq'), 'rows'), may hold values from -7 to 7
- head_weight: bfloat16 [16384, 65536], P('rows', ('vocab', 'seq')), may hold values from -0.1 to 0.1
- tokens: int32 [1024], P(('rows', 'seq')), may hold values from 0 to 65535
Outputs:
- logprobs: float32 [1024, 65536], P(('rows', 'seq'), 'vocab')
- target_logp: float32 [1024], P(('rows', 'seq'))
All inputs are finite; a program needn't handle non-finite values.
Results may differ from a plain program's by a relative error of at most 0.0003.
Values may be sent and summed in bfloat16 or wider, within the bound.
No kernel may reach another device: no remote copies, remote signals or barrier semaphores. Data moves between devices by JAX's collectives and lax.ppermute only.
A program may use at most 64 MiB of HBM per device.

v0:
```python
import jax
import jax.numpy as jnp
from jax import lax
from jax.sharding import PartitionSpec as P


def local(hidden, head_weight, tokens):
    partial_value = jnp.dot(
        lax.all_gather(hidden, ("vocab", "seq"), axis=0, tiled=True),
        head_weight,
        preferred_element_type=jnp.float32,
    )
    logits = lax.psum_scatter(partial_value, "rows", scatter_dimension=0, tiled=True)
    local_peak = jnp.max(logits, axis=1)
    row_peak = lax.pmax(local_peak, ("vocab", "seq"))
    local_total = jnp.sum(jnp.exp(logits - row_peak[:, None]), axis=1)
    row_total = lax.psum(local_total, ("vocab", "seq"))
    payload = logits - row_peak[:, None] - jnp.log(row_total)[:, None]
    arrived = lax.all_to_all(payload, "seq", split_axis=0, concat_axis=1, tiled=True)
    width = arrived.shape[1]
    column = lax.axis_index("vocab") * width + lax.broadcasted_iota(jnp.int32, arrived.shape, 1)
    picked = jnp.sum(jnp.where(column == tokens[:, None], arrived, 0.0), axis=1)
    target_logp = lax.psum(picked, "vocab")
    return (arrived, target_logp)


def solution(mesh):
    in_specs = (P(("vocab", "seq"), "rows"), P("rows", ("vocab", "seq")), P(("rows", "seq")))
    out_specs = (P(("rows", "seq"), "vocab"), P(("rows", "seq")))
    return jax.shard_map(local, mesh=mesh, in_specs=in_specs, out_specs=out_specs, check_vma=False)
```

profile of v0, /device:TPU:1, one launch (start us, length us, event | category | flops | bytes accessed | tf_op | source)
XLA Modules:
  0.0 468.1 jit_solution(14702957354153405713)
XLA Ops:
  7.2 0.0 all-gather.2.cloned.1.call-start
  7.2 0.7 all-gather.2.cloned.1.call-update
  7.9 0.0 reduce-scatter.2.cloned.1.call-start
  7.9 93.7 %all-gather.2.cloned.1.call-done = bf16[1024,2048]{1,0:T(8,128)(2,1)} async-done(((bf16[16,2048]{1,0:T(8,128)(2,1)}), bf16[1024,2048]{1,0:T(8,128)(2,1)}) %all-gather.2.cloned.1.call-update) | async-done | bytes 4194320 | tf_op jit(solution)/shard_map/all_gather | solution.py:9
  101.6 9.9 %fusion.1 = f32[1024,1024]{1,0:T(8,128)} fusion(bf16[1024,2048]{1,0:T(8,128)(2,1)} %all-gather.2.cloned.1.call-done, bf16[2048,1024]{1,0:T(8,128)(2,1)} %param.4), kind=kOutput, calls=%fused_computation.5 | convolution fusion | flops 4294967296 | bytes 12582912 | tf_op jit(solution)/shard_map/dot_general | solution.py:8
  111.5 0.0 copy-start
  111.5 0.0 reduce-scatter.2.cloned.1.call-update
  111.5 56.0 %reduce-scatter.2.cloned.1.call-done = f32[128,1024]{1,0:T(8,128)} async-done(((f32[1024,1024]{1,0:T(8,128)}), f32[128,1024]{1,0:T(8,128)}) %reduce-scatter.2.cloned.1.call-update) | async-done | bytes 524304 | tf_op jit(solution)/shard_map/reduce_scatter | solution.py:13
  167.5 1.2 reduce_max.9
  168.7 124.1 %pmax.7 = f32[128]{0:T(128)S(1)} all-reduce(f32[128]{0:T(128)S(1)} %reduce_max.9), channel_id=1, replica_groups=mesh['vocab'=16,'rows'=8,'seq'=4] {'vocab','seq'}, use_global_device_ids=true, to_apply=%region_2.0 | all-reduce | flops 128 | bytes 1024 | tf_op jit(solution)/shard_map/pmax | solution.py:15
  292.8 1.3 exponential_reduce_fusion
  294.1 124.1 %psum.14 = f32[128]{0:T(128)S(1)} all-reduce(f32[128]{0:T(128)S(1)} %exponential_reduce_fusion), channel_id=1, replica_groups=mesh['vocab'=16,'rows'=8,'seq'=4] {'vocab','seq'}, use_global_device_ids=true, to_apply=%region_4.0 | all-reduce | flops 128 | bytes 1024 | tf_op jit(solution)/shard_map/psum | solution.py:17
  418.1 2.0 subtract_subtract_fusion
  420.1 3.5 all-to-all-start
  423.6 6.9 %all-to-all-done = f32[4,32,1024]{2,1,0:T(8,128)S(1)} async-done(((f32[4,32,1024]{2,1,0:T(8,128)}), f32[4,32,1024]{2,1,0:T(8,128)S(1)}, u32[]{:S(2)}, u32[]{:S(2)}) %all-to-all-start) | async-done | bytes 524320 | tf_op jit(solution)/shard_map/all_to_all | solution.py:19
  430.5 0.8 copy.6
  431.3 0.0 copy-done
  431.3 0.2 fusion
  431.6 29.7 %psum.15 = f32[32]{0:T(128)} all-reduce(f32[32]{0:T(128)S(1)} %fusion), channel_id=1, replica_groups=mesh['vocab'=16,'rows'=8,'seq'=4] {'vocab'}, use_global_device_ids=true, to_apply=%region_6.7 | all-reduce | flops 32 | bytes 256 | tf_op jit(solution)/shard_map/psum | solution.py:23
  (2 shorter events, 0.0 us)
Async XLA Ops:
  7.2 94.4 %all-gather.2.cloned.1.call-start = ((), (), s32[]{:S(2)}) async-start(), calls=%async_computation.2 | async-start | bytes 4259840 | tf_op jit(solution)/shard_map/all_gather | solution.py:9
  7.9 159.6 %reduce-scatter.2.cloned.1.call-start = ((), (), s32[]{:S(2)}) async-start(), calls=%async_computation.3 | async-start | bytes 4718592 | tf_op jit(solution)/shard_map/reduce_scatter | solution.py:13
  111.5 319.8 %copy-start = (s32[32]{0:T(128)S(1)}, s32[32]{0:T(128)}, u32[]{:S(2)}) copy-start(s32[32]{0:T(128)} %param.5) | copy-start | bytes 388
  420.1 10.4 %all-to-all-start = ((f32[4,32,1024]{2,1,0:T(8,128)}), f32[4,32,1024]{2,1,0:T(8,128)S(1)}, u32[]{:S(2)}, u32[]{:S(2)}) async-start(f32[4,32,1024]{2,1,0:T(8,128)} %bitcast), calls=%async_computation.1 | async-start | bytes 1048576 | tf_op jit(solution)/shard_map/all_to_all | solution.py:19
Sparse Core Ops, SparseCore 0:
  11.3 90.2 all-gather.1
  111.6 55.8 reduce-scatter.1
where the time goes:
time: 468 us
  blocking collectives  278 us (59%)
  waiting for transfers between devices  157 us (34%)
  between operations  14.1 us (3%)
  matrix products  9.88 us (2%)
    pmax x1, blocking collectives, local(): row_peak = lax.pmax(local_peak, ('vocab', 'seq'))  124 us
    psum x1, blocking collectives, local(): row_total = lax.psum(local_total, ('vocab', 'seq'))  124 us
    all_gather x1, waiting for transfers between devices, local(): lax.all_gather(hidden, ('vocab', 'seq'), axis=0, tiled=True)  93.7 us
    reduce_scatter x1, waiting for transfers between devices, local(): lax.psum_scatter(partial_value, 'rows', scatter_dimension=0, tiled=True)  56 us
    psum x1, blocking collectives, local(): target_logp = lax.psum(picked, 'vocab')  29.7 us
    dot_general x1, matrix products, local(): jnp.dot(lax.all_gather(hidden, ('vocab', 'seq'), axis=0, tiled=True), hea...  9.88 us
  transfers between devices with their start and end apart: 3, of which 3 were waited for; matrix products, arithmetic and copies ran while one was open for 0% of the time, Pallas kernels for 0%

commit v1 on v0

v1 whole, which is shorter than its diff:
```python
import jax
import jax.numpy as jnp
from jax import lax
from jax.sharding import Mesh, PartitionSpec as P

F16 = jnp.float16
F32 = jnp.float32


def spread(x, axis, size):
    return lax.all_to_all(jnp.broadcast_to(x[None], (size,) + x.shape), axis, split_axis=0, concat_axis=0, tiled=True)


def local(ny, nz, nx, hidden, head_weight, tokens):
    n, k = hidden.shape
    cols = head_weight.shape[1]
    core = lax.axis_index("core")
    mine = spread(spread(hidden, "y", ny), "x", nx)
    mine = jnp.swapaxes(mine, 0, 1).reshape(ny * nx * n, k)
    other = lax.ppermute(mine, "core", [(0, 1), (1, 0)])

    def reduced(rows):
        part = jnp.dot(rows, head_weight, preferred_element_type=F32).astype(F16)
        part = lax.all_to_all(part.reshape(nz, nx * n, cols), "rows", split_axis=0, concat_axis=0, tiled=True)
        return jnp.sum(part.astype(F32), axis=0)

    first, second = reduced(mine), reduced(other)
    both = jnp.where(core == 0, jnp.stack([first, second]), jnp.stack([second, first]))
    both = both.astype(F16).reshape(nx, 2 * n, cols)
    logits = lax.all_to_all(both, "x", split_axis=0, concat_axis=0, tiled=True)
    logits = jnp.swapaxes(logits, 0, 1).reshape(2 * n, nx * cols).astype(F32)

    width = logits.shape[1]
    column = lax.axis_index(("y", "core")) * width + lax.broadcasted_iota(jnp.int32, logits.shape, 1)
    peak = jnp.max(logits, axis=1)
    total = jnp.sum(jnp.exp(logits - peak[:, None]), axis=1)
    picked = jnp.sum(jnp.where(column == tokens[:, None], logits, 0.0), axis=1)
    stats = spread(jnp.concatenate([peak, total, picked]), ("y", "core"), 2 * ny)
    peaks, totals, picks = jnp.split(stats, 3, axis=1)
    row_peak = jnp.max(peaks, axis=0)
    row_total = jnp.sum(totals * jnp.exp(peaks - row_peak), axis=0)
    shift = jnp.log(row_total)
    logprobs = logits - row_peak[:, None] - shift[:, None]
    target_logp = jnp.sum(picks, axis=0) - row_peak - shift
    return (logprobs, target_logp)


def solution(mesh):
    nv, nz, nx = mesh.devices.shape
    ny = nv // 2
    split = Mesh(mesh.devices.reshape(ny, 2, nz, nx), ("y", "core", "rows", "x"))
    in_specs = (P(("y", "core", "x"), "rows"), P("rows", ("y", "core", "x")), P(("rows", "x")))
    out_specs = (P(("rows", "x"), ("y", "core")), P(("rows", "x")))

    def body(*args):
        return local(ny, nz, nx, *args)

    return jax.shard_map(body, mesh=split, in_specs=in_specs, out_specs=out_specs, check_vma=False)
```

time: 468 us -> 159 us (0.34)
  blocking collectives: 278 us -> 50.6 us
  waiting for transfers between devices: 157 us -> 64.9 us
  starting transfers between devices: 3.55 us -> 28 us
  between operations: 14.1 us -> 0.75 us
    psum x2 -> x0, blocking collectives: 154 us -> none  [the longest x1 124 us: local(): row_total = lax.psum(local_total, ('vocab', 'seq'))]
    pmax x1 -> x0, blocking collectives: 124 us -> none  [local(): row_peak = lax.pmax(local_peak, ('vocab', 'seq'))]
    all_gather x1 -> x0, waiting for transfers between devices: 93.7 us -> none  [local(): lax.all_gather(hidden, ('vocab', 'seq'), axis=0, tiled=True)]
    all_to_all x1 -> x4, waiting for transfers between devices: 6.88 us -> 64.9 us  [the longest x2 52.1 us: reduced(): lax.all_to_all(part.reshape(nz, nx * n, cols), 'rows', split_axis=0, conc...]
    reduce_scatter x1 -> x0, waiting for transfers between devices: 56 us -> none  [local(): lax.psum_scatter(partial_value, 'rows', scatter_dimension=0, tiled=True)]
    all_to_all x0 -> x2, blocking collectives: none -> 50.6 us  [spread(): lax.all_to_all(jnp.broadcast_to(x[None], (size,) + x.shape), axis, split_...]
    all_to_all x1 -> x4, starting transfers between devices: 3.47 us -> 21.9 us  [the longest x2 13.6 us: reduced(): lax.all_to_all(part.reshape(nz, nx * n, cols), 'rows', split_axis=0, conc...]
    ppermute x0 -> x1, starting transfers between devices: none -> 6.12 us  [local(): other = lax.ppermute(mine, 'core', [(0, 1), (1, 0)])]
  transfers between devices with their start and end apart: 3 -> 5, of which waited for: 3 -> 4; matrix products, arithmetic and copies ran while one was open for 0% -> 6% of each run, Pallas kernels for 0% -> 0%
where the time goes in v1:
time: 159 us
  waiting for transfers between devices  64.9 us (41%)
  blocking collectives  50.6 us (32%)
  starting transfers between devices  28 us (18%)
  matrix products  9.5 us (6%)
  other arithmetic  3.35 us (2%)
  local copies, waits for them, and re-layouts  1.93 us (1%)
    all_to_all x2, waiting for transfers between devices, reduced(): lax.all_to_all(part.reshape(nz, nx * n, cols), 'rows', split_axis=0, conc...  52.1 us
    all_to_all x2, blocking collectives, spread(): lax.all_to_all(jnp.broadcast_to(x[None], (size,) + x.shape), axis, split_...  50.6 us
    all_to_all x2, starting transfers between devices, reduced(): lax.all_to_all(part.reshape(nz, nx * n, cols), 'rows', split_axis=0, conc...  13.6 us
    dot_general x2, matrix products, reduced(): part = jnp.dot(rows, head_weight, preferred_element_type=F32).astype(F16)  9.5 us
    all_to_all x1, waiting for transfers between devices, spread(): lax.all_to_all(jnp.broadcast_to(x[None], (size,) + x.shape), axis, split_...  6.9 us
    ppermute x1, starting transfers between devices, local(): other = lax.ppermute(mine, 'core', [(0, 1), (1, 0)])  6.12 us
    all_to_all x1, waiting for transfers between devices, local(): logits = lax.all_to_all(both, 'x', split_axis=0, concat_axis=0, tiled=True)  5.94 us
    all_to_all x1, starting transfers between devices, spread(): lax.all_to_all(jnp.broadcast_to(x[None], (size,) + x.shape), axis, split_...  4.88 us
  transfers between devices with their start and end apart: 5, of which 4 were waited for; matrix products, arithmetic and copies ran while one was open for 6% of the time, Pallas kernels for 0%

profile of v1, /device:TPU:1, one launch (start us, length us, event | category | flops | bytes accessed | tf_op | source)
XLA Modules:
  0.0 159.0 jit_solution(1702482797395206880)
XLA Ops:
  0.6 0.9 broadcast_in_dim.9
  1.5 22.2 %all_to_all.34 = bf16[8,16,2048]{2,1,0:T(8,128)(2,1)S(1)} all-to-all(bf16[8,16,2048]{2,1,0:T(8,128)(2,1)S(1)} %broadcast_in_dim.9), channel_id=1, replica_groups=mesh['y'=8,'core'=2,'rows'=8,'x'=4] {'y'}, dimensions={0} | all-to-all | bytes 1048576 | tf_op jit(solution)/shard_map/all_to_all | solution.py:11
  23.7 0.2 broadcast_in_dim.10
  24.0 28.4 %all_to_all.35 = bf16[4,8,16,2048]{3,2,1,0:T(8,128)(2,1)S(1)} all-to-all(bf16[4,8,16,2048]{3,2,1,0:T(8,128)(2,1)S(1)} %broadcast_in_dim.10), channel_id=1, replica_groups=mesh['y'=8,'core'=2,'rows'=8,'x'=4] {'x'}, dimensions={0} | all-to-all | bytes 4194304 | tf_op jit(solution)/shard_map/all_to_all | solution.py:11
  52.4 0.1 copy.10
  52.5 6.1 %collective-permute-start = (bf16[512,2048]{1,0:T(8,128)(2,1)S(1)}, bf16[512,2048]{1,0:T(8,128)(2,1)}, u32[]{:S(2)}, u32[]{:S(2)}) collective-permute-start(bf16[512,2048]{1,0:T(8,128)(2,1)S(1)} %bitcast.29), channel_id=1, source_target_pairs={{0,32},{32,0},{1,33},{33,1},{2,34},{34,2},{3,35},{35,3},{4,36},{36... | collective-permute-start | bytes 6291464 | tf_op jit(solution)/shard_map/ppermute | solution.py:20
  58.6 3.4 %convolution_convert_fusion.1 = f16[512,1024]{1,0:T(8,128)(2,1)} fusion(bf16[512,2048]{1,0:T(8,128)(2,1)S(1)} %bitcast.30, bf16[2048,1024]{1,0:T(8,128)(2,1)S(1)} %copy-done.1), kind=kOutput, calls=%fused_computation.3 | convolution fusion | flops 2148007936 | bytes 7340032 | tf_op jit(solution)/shard_map/dot_general | solution.py:23
  62.0 10.0 %all-to-all-start.2 = ((f16[8,64,1024]{2,1,0:T(8,128)(2,1)}), f16[8,64,1024]{2,1,0:T(8,128)(2,1)S(1)}, u32[]{:S(2)}, u32[]{:S(2)}) async-start(f16[8,64,1024]{2,1,0:T(8,128)(2,1)} %bitcast.31), calls=%async_computation.2 | async-start | bytes 2097152 | tf_op jit(solution)/shard_map/all_to_all | solution.py:24
  72.0 6.1 %convolution_convert_fusion = f16[512,1024]{1,0:T(8,128)(2,1)} fusion(bf16[512,2048]{1,0:T(8,128)(2,1)} %collective-permute-done, bf16[2048,1024]{1,0:T(8,128)(2,1)} %param.4), kind=kOutput, calls=%fused_computation.2 | convolution fusion | flops 2148007936 | bytes 7340032 | tf_op jit(solution)/shard_map/dot_general | solution.py:23
  78.2 23.2 %all-to-all-done.2 = f16[8,64,1024]{2,1,0:T(8,128)(2,1)S(1)} async-done(((f16[8,64,1024]{2,1,0:T(8,128)(2,1)}), f16[8,64,1024]{2,1,0:T(8,128)(2,1)S(1)}, u32[]{:S(2)}, u32[]{:S(2)}) %all-to-all-start.2) | async-done | bytes 1048608 | tf_op jit(solution)/shard_map/all_to_all | solution.py:24
  101.3 3.6 %all-to-all-start.3 = ((f16[8,64,1024]{2,1,0:T(8,128)(2,1)}), f16[8,64,1024]{2,1,0:T(8,128)(2,1)S(1)}, u32[]{:S(2)}, u32[]{:S(2)}) async-start(f16[8,64,1024]{2,1,0:T(8,128)(2,1)} %bitcast.5), calls=%async_computation.3 | async-start | bytes 2097152 | tf_op jit(solution)/shard_map/all_to_all | solution.py:24
  104.9 0.2 convert_reduce_fusion.1
  105.2 28.9 %all-to-all-done.3 = f16[8,64,1024]{2,1,0:T(8,128)(2,1)S(1)} async-done(((f16[8,64,1024]{2,1,0:T(8,128)(2,1)}), f16[8,64,1024]{2,1,0:T(8,128)(2,1)S(1)}, u32[]{:S(2)}, u32[]{:S(2)}) %all-to-all-start.3) | async-done | bytes 1048608 | tf_op jit(solution)/shard_map/all_to_all | solution.py:24
  134.1 0.2 convert_reduce_fusion
  134.3 0.8 fusion.5
  135.1 3.4 %all-to-all-start.4 = ((f16[4,32,1024]{2,1,0:T(8,128)(2,1)}), f16[4,32,1024]{2,1,0:T(8,128)(2,1)S(1)}, u32[]{:S(2)}, u32[]{:S(2)}) async-start(f16[4,32,1024]{2,1,0:T(8,128)(2,1)} %bitcast.7), calls=%async_computation.4 | async-start | bytes 524288 | tf_op jit(solution)/shard_map/all_to_all | solution.py:30
  138.5 5.9 %all-to-all-done.4 = f16[4,32,1024]{2,1,0:T(8,128)(2,1)S(1)} async-done(((f16[4,32,1024]{2,1,0:T(8,128)(2,1)}), f16[4,32,1024]{2,1,0:T(8,128)(2,1)S(1)}, u32[]{:S(2)}, u32[]{:S(2)}) %all-to-all-start.4) | async-done | bytes 262176 | tf_op jit(solution)/shard_map/all_to_all | solution.py:30
  144.4 0.1 convert_reduce_fusion.2
  144.6 0.3 fusion.4
  145.0 0.6 broadcast_in_dim.13
  145.6 4.9 %all-to-all-start.5 = ((f32[16,1,96]{2,1,0:T(1,128)}), f32[16,1,96]{2,1,0:T(1,128)S(1)}, u32[]{:S(2)}, u32[]{:S(2)}) async-start(f32[16,1,96]{2,1,0:T(1,128)} %broadcast_in_dim.13), calls=%async_computation.5 | async-start | bytes 16384 | tf_op jit(solution)/shard_map/all_to_all | solution.py:11
  150.6 6.9 %all-to-all-done.5 = f32[16,1,96]{2,1,0:T(1,128)S(1)} async-done(((f32[16,1,96]{2,1,0:T(1,128)}), f32[16,1,96]{2,1,0:T(1,128)S(1)}, u32[]{:S(2)}, u32[]{:S(2)}) %all-to-all-start.5) | async-done | bytes 6176 | tf_op jit(solution)/shard_map/all_to_all | solution.py:11
  157.6 0.5 subtract_subtract_fusion.1
  158.1 0.9 subtract_subtract_fusion
  (11 shorter events, 0.3 us)
Async XLA Ops:
  52.4 6.3 %copy-start.1 = (bf16[2048,1024]{1,0:T(8,128)(2,1)S(1)}, bf16[2048,1024]{1,0:T(8,128)(2,1)}, u32[]{:S(2)}) copy-start(bf16[2048,1024]{1,0:T(8,128)(2,1)} %param.4) | copy-start | bytes 12582916
  52.5 19.5 %collective-permute-start = (bf16[512,2048]{1,0:T(8,128)(2,1)S(1)}, bf16[512,2048]{1,0:T(8,128)(2,1)}, u32[]{:S(2)}, u32[]{:S(2)}) collective-permute-start(bf16[512,2048]{1,0:T(8,128)(2,1)S(1)} %bitcast.29), channel_id=1, source_target_pairs={{0,32},{32,0},{1,33},{33,1},{2,34},{34,2},{3,35},{35,3},{4,36},{36... | collective-permute-start | bytes 6291464 | tf_op jit(solution)/shard_map/ppermute | solution.py:20
  62.0 39.3 %all-to-all-start.2 = ((f16[8,64,1024]{2,1,0:T(8,128)(2,1)}), f16[8,64,1024]{2,1,0:T(8,128)(2,1)S(1)}, u32[]{:S(2)}, u32[]{:S(2)}) async-start(f16[8,64,1024]{2,1,0:T(8,128)(2,1)} %bitcast.31), calls=%async_computation.2 | async-start | bytes 2097152 | tf_op jit(solution)/shard_map/all_to_all | solution.py:24
  101.3 32.7 %all-to-all-start.3 = ((f16[8,64,1024]{2,1,0:T(8,128)(2,1)}), f16[8,64,1024]{2,1,0:T(8,128)(2,1)S(1)}, u32[]{:S(2)}, u32[]{:S(2)}) async-start(f16[8,64,1024]{2,1,0:T(8,128)(2,1)} %bitcast.5), calls=%async_computation.3 | async-start | bytes 2097152 | tf_op jit(solution)/shard_map/all_to_all | solution.py:24
  104.9 39.7 %copy-start = (s32[32]{0:T(128)S(1)}, s32[32]{0:T(128)}, u32[]{:S(2)}) copy-start(s32[32]{0:T(128)} %param.5) | copy-start | bytes 388
  135.1 9.4 %all-to-all-start.4 = ((f16[4,32,1024]{2,1,0:T(8,128)(2,1)}), f16[4,32,1024]{2,1,0:T(8,128)(2,1)S(1)}, u32[]{:S(2)}, u32[]{:S(2)}) async-start(f16[4,32,1024]{2,1,0:T(8,128)(2,1)} %bitcast.7), calls=%async_computation.4 | async-start | bytes 524288 | tf_op jit(solution)/shard_map/all_to_all | solution.py:30
  145.6 11.9 %all-to-all-start.5 = ((f32[16,1,96]{2,1,0:T(1,128)}), f32[16,1,96]{2,1,0:T(1,128)S(1)}, u32[]{:S(2)}, u32[]{:S(2)}) async-start(f32[16,1,96]{2,1,0:T(1,128)} %broadcast_in_dim.13), calls=%async_computation.5 | async-start | bytes 16384 | tf_op jit(solution)/shard_map/all_to_all | solution.py:11

commit v2 on v1

v2 whole, which is shorter than its diff:
```python
import jax
import jax.numpy as jnp
from jax import lax
from jax.sharding import Mesh, PartitionSpec as P

F16 = jnp.float16
F32 = jnp.float32


def spread(x, axis, size):
    return lax.all_to_all(jnp.broadcast_to(x[None], (size,) + x.shape), axis, split_axis=0, concat_axis=0, tiled=True)


def local(ny, nz, nx, hidden, head_weight, tokens):
    n, k = hidden.shape
    m = n // 2
    cols = head_weight.shape[1]

    def reduced(rows):
        part = jnp.dot(rows, head_weight, preferred_element_type=F32).astype(F16)
        part = lax.all_to_all(part.reshape(nz * nx, 2 * m, cols), ("rows", "x"), split_axis=0, concat_axis=0, tiled=True)
        part = jnp.sum(part.reshape(nz, nx, 2 * m, cols).astype(F32), axis=0)
        return jnp.swapaxes(part, 0, 1).reshape(2, m, nx * cols)

    late = lax.all_gather(hidden[m:], ("y", "core", "x"), axis=0, tiled=True)
    early = spread(spread(spread(hidden[:m], "y", ny), "x", nx), "core", 2)
    early = jnp.transpose(early, (2, 0, 1, 3, 4)).reshape(ny * 2 * nx * m, k)
    logits = jnp.stack([reduced(early), reduced(late)], axis=1)

    width = nx * cols
    column = lax.axis_index(("y", "core")) * width + lax.broadcasted_iota(jnp.int32, logits.shape, 3)
    token = tokens.reshape(2, 2, m)
    peak = jnp.max(logits, axis=3)
    total = jnp.sum(jnp.exp(logits - peak[..., None]), axis=3)
    picked = jnp.sum(jnp.where(column == token[..., None], logits, 0.0), axis=3)
    stats = jnp.concatenate([peak.reshape(-1), total.reshape(-1), picked.reshape(-1)])
    peaks, totals, picks = jnp.split(spread(stats, ("y", "core"), 2 * ny), 3, axis=1)
    row_peak = jnp.max(peaks, axis=0)
    row_total = jnp.sum(totals * jnp.exp(peaks - row_peak), axis=0)
    shift = jnp.log(row_total)
    logprobs = logits.reshape(2 * n, width) - row_peak[:, None] - shift[:, None]
    target_logp = jnp.sum(picks, axis=0) - row_peak - shift
    return (logprobs, target_logp)


def solution(mesh):
    nv, nz, nx = mesh.devices.shape
    ny = nv // 2
    split = Mesh(mesh.devices.reshape(ny, 2, nz, nx), ("y", "core", "rows", "x"))
    in_specs = (P(("y", "core", "x"), "rows"), P("rows", ("y", "core", "x")), P(("rows", "x")))
    out_specs = (P(("rows", "x"), ("y", "core")), P(("rows", "x")))

    def body(*args):
        return local(ny, nz, nx, *args)

    return jax.shard_map(body, mesh=split, in_specs=in_specs, out_specs=out_specs, check_vma=False)
```

time: 159 us -> 167 us (1.050)
  between operations: 0.75 us -> 14.2 us
  blocking collectives: 50.6 us -> 43.2 us
  local copies, waits for them, and re-layouts: 1.93 us -> 5.78 us
  starting transfers between devices: 28 us -> 24.8 us
    all_gather x0 -> x1, waiting for transfers between devices: none -> 33.4 us  [local(): late = lax.all_gather(hidden[m:], ('y', 'core', 'x'), axis=0, tiled=True)]
    all_to_all x3 -> x2, waiting for transfers between devices: 58 us -> 26.2 us  [reduced(): lax.all_to_all(part.reshape(nz * nx, 2 * m, cols), ('rows', 'x'), split_a...]
    all_to_all x2 -> x3, blocking collectives: 50.6 us -> 43.2 us  [spread(): lax.all_to_all(jnp.broadcast_to(x[None], (size,) + x.shape), axis, split_...]
    ppermute x1 -> x0, starting transfers between devices: 6.12 us -> none  [local(): other = lax.ppermute(mine, 'core', [(0, 1), (1, 0)])]
    unnamed x4 -> x5, local copies, waits for them, and re-layouts: 0.01 us -> 1.97 us
    all_to_all x1, starting transfers between devices: 4.88 us -> 6.61 us  [spread(): lax.all_to_all(jnp.broadcast_to(x[None], (size,) + x.shape), axis, split_...]
    all_to_all x3 -> x2, starting transfers between devices: 17 us -> 18.1 us  [reduced(): lax.all_to_all(part.reshape(nz * nx, 2 * m, cols), ('rows', 'x'), split_a...]
  transfers between devices with their start and end apart: 5 -> 4, of which waited for: 4 -> 3; matrix products, arithmetic and copies ran while one was open for 6% -> 7% of each run, Pallas kernels for 0% -> 0%
where the time goes in v2:
time: 167 us; the launch traced here: 166 us
  waiting for transfers between devices  66.5 us (40%)
  blocking collectives  43.2 us (26%)
  starting transfers between devices  24.8 us (15%)
  between operations  14.2 us (9%)
  matrix products  9.47 us (6%)
  local copies, waits for them, and re-layouts  5.78 us (3%)
  other arithmetic  2.49 us (1%)
    all_to_all x3, blocking collectives, spread(): lax.all_to_all(jnp.broadcast_to(x[None], (size,) + x.shape), axis, split_...  43.2 us
    all_gather x1, waiting for transfers between devices, local(): late = lax.all_gather(hidden[m:], ('y', 'core', 'x'), axis=0, tiled=True)  33.4 us
    all_to_all x2, waiting for transfers between devices, reduced(): lax.all_to_all(part.reshape(nz * nx, 2 * m, cols), ('rows', 'x'), split_a...  26.2 us
    all_to_all x2, starting transfers between devices, reduced(): lax.all_to_all(part.reshape(nz * nx, 2 * m, cols), ('rows', 'x'), split_a...  18.1 us
    dot_general x2, matrix products, reduced(): part = jnp.dot(rows, head_weight, preferred_element_type=F32).astype(F16)  9.47 us
    all_to_all x1, waiting for transfers between devices, spread(): lax.all_to_all(jnp.broadcast_to(x[None], (size,) + x.shape), axis, split_...  6.9 us
    all_to_all x1, starting transfers between devices, spread(): lax.all_to_all(jnp.broadcast_to(x[None], (size,) + x.shape), axis, split_...  6.61 us
  transfers between devices with their start and end apart: 4, of which 3 were waited for; matrix products, arithmetic and copies ran while one was open for 7% of the time, Pallas kernels for 0%

profile of v2, /device:TPU:1, one launch (start us, length us, event | category | flops | bytes accessed | tf_op | source)
XLA Modules:
  0.0 166.4 jit_solution(17566436303740077389)
XLA Ops:
  7.2 1.4 fusion.2
  8.7 16.7 %all_to_all.34 = bf16[8,8,2048]{2,1,0:T(8,128)(2,1)S(1)} all-to-all(bf16[8,8,2048]{2,1,0:T(8,128)(2,1)S(1)} %broadcast_in_dim.11), channel_id=1, replica_groups=mesh['y'=8,'core'=2,'rows'=8,'x'=4] {'y'}, dimensions={0} | all-to-all | bytes 524288 | tf_op jit(solution)/shard_map/all_to_all | solution.py:11
  25.5 17.8 %all_to_all.35 = bf16[4,8,8,2048]{3,2,1,0:T(8,128)(2,1)S(1)} all-to-all(bf16[4,8,8,2048]{3,2,1,0:T(8,128)(2,1)S(1)} %broadcast_in_dim.12), channel_id=1, replica_groups=mesh['y'=8,'core'=2,'rows'=8,'x'=4] {'x'}, dimensions={0} | all-to-all | bytes 2097152 | tf_op jit(solution)/shard_map/all_to_all | solution.py:11
  43.4 0.3 broadcast_in_dim.13
  43.7 8.6 %all_to_all.36 = bf16[2,4,8,8,2048]{4,3,1,2,0:T(8,128)(2,1)S(1)} all-to-all(bf16[2,4,8,8,2048]{4,3,1,2,0:T(8,128)(2,1)S(1)} %broadcast_in_dim.13), channel_id=1, replica_groups=mesh['y'=8,'core'=2,'rows'=8,'x'=4] {'core'}, dimensions={0} | all-to-all | bytes 4194304 | tf_op jit(solution)/shard_map/all_to_all | solution.py:11
  52.3 0.2 copy.39
  52.5 1.9 %copy-done.1 = bf16[2048,1024]{1,0:T(8,128)(2,1)S(1)} copy-done((bf16[2048,1024]{1,0:T(8,128)(2,1)S(1)}, bf16[2048,1024]{1,0:T(8,128)(2,1)}, u32[]{:S(2)}) %copy-start.1) | copy-done | bytes 4194328
  54.5 3.3 %convolution_convert_fusion.1 = f16[512,1024]{1,0:T(8,128)(2,1)} fusion(bf16[512,2048]{1,0:T(8,128)(2,1)S(1)} %bitcast.22, bf16[2048,1024]{1,0:T(8,128)(2,1)S(1)} %copy-done.1), kind=kOutput, calls=%fused_computation.3 | convolution fusion | flops 2148007936 | bytes 7340032 | tf_op jit(solution)/shard_map/dot_general | solution.py:20
  57.8 10.9 %all-to-all-start.3 = ((f16[32,16,1024]{2,1,0:T(8,128)(2,1)}), f16[32,16,1024]{2,1,0:T(8,128)(2,1)S(1)}, u32[]{:S(2)}, u32[]{:S(2)}) async-start(f16[32,16,1024]{2,1,0:T(8,128)(2,1)} %bitcast.2), calls=%async_computation.3 | async-start | bytes 2097152 | tf_op jit(solution)/shard_map/all_to_all | solution.py:21
  68.7 33.4 %all-gather.2.cloned.1.call-done = bf16[512,2048]{1,0:T(8,128)(2,1)} async-done(((bf16[8,2048]{1,0:T(8,128)(2,1)}), bf16[512,2048]{1,0:T(8,128)(2,1)}) %all-gather.2.cloned.1.call-update) | async-done | bytes 2097168 | tf_op jit(solution)/shard_map/all_gather | solution.py:25
  102.2 6.1 %convolution_convert_fusion = f16[512,1024]{1,0:T(8,128)(2,1)} fusion(bf16[512,2048]{1,0:T(8,128)(2,1)} %all-gather.2.cloned.1.call-done, bf16[2048,1024]{1,0:T(8,128)(2,1)} %param.4), kind=kOutput, calls=%fused_computation.2 | convolution fusion | flops 2148007936 | bytes 7340032 | tf_op jit(solution)/shard_map/dot_general | solution.py:20
  108.3 7.2 %all-to-all-start.4 = ((f16[32,16,1024]{2,1,0:T(8,128)(2,1)}), f16[32,16,1024]{2,1,0:T(8,128)(2,1)S(1)}, u32[]{:S(2)}, u32[]{:S(2)}) async-start(f16[32,16,1024]{2,1,0:T(8,128)(2,1)} %bitcast.5), calls=%async_computation.4 | async-start | bytes 2097152 | tf_op jit(solution)/shard_map/all_to_all | solution.py:21
  115.6 0.2 convert_reduce_fusion.1
  115.9 0.2 copy.40
  116.0 0.2 stack_reshape.6
  116.3 26.2 %all-to-all-done.4 = f16[32,16,1024]{2,1,0:T(8,128)(2,1)S(1)} async-done(((f16[32,16,1024]{2,1,0:T(8,128)(2,1)}), f16[32,16,1024]{2,1,0:T(8,128)(2,1)S(1)}, u32[]{:S(2)}, u32[]{:S(2)}) %all-to-all-start.4) | async-done | bytes 1048608 | tf_op jit(solution)/shard_map/all_to_all | solution.py:21
  142.4 0.2 convert_reduce_fusion
  142.8 0.2 stack_reshape.7
  143.2 0.3 exponential_reduce_fusion
  143.8 0.6 broadcast_in_dim.16
  144.4 6.6 %all-to-all-start.5 = ((f32[16,1,96]{2,1,0:T(1,128)}), f32[16,1,96]{2,1,0:T(1,128)S(1)}, u32[]{:S(2)}, u32[]{:S(2)}) async-start(f32[16,1,96]{2,1,0:T(1,128)} %broadcast_in_dim.16), calls=%async_computation.5 | async-start | bytes 16384 | tf_op jit(solution)/shard_map/all_to_all | solution.py:11
  151.1 6.9 %all-to-all-done.5 = f32[16,1,96]{2,1,0:T(1,128)S(1)} async-done(((f32[16,1,96]{2,1,0:T(1,128)}), f32[16,1,96]{2,1,0:T(1,128)S(1)}, u32[]{:S(2)}, u32[]{:S(2)}) %all-to-all-start.5) | async-done | bytes 6176 | tf_op jit(solution)/shard_map/all_to_all | solution.py:11
  158.1 0.5 subtract_subtract_fusion
  158.6 0.9 fusion
  (26 shorter events, 1.2 us)
Async XLA Ops:
  7.2 95.0 %all-gather.2.cloned.1.call-start = ((), (), s32[]{:S(2)}) async-start(), calls=%async_computation.6 | async-start | bytes 2129920 | tf_op jit(solution)/shard_map/all_gather | solution.py:25
  52.3 2.2 %copy-start.1 = (bf16[2048,1024]{1,0:T(8,128)(2,1)S(1)}, bf16[2048,1024]{1,0:T(8,128)(2,1)}, u32[]{:S(2)}) copy-start(bf16[2048,1024]{1,0:T(8,128)(2,1)} %param.4) | copy-start | bytes 12582916
  57.8 50.5 %all-to-all-start.3 = ((f16[32,16,1024]{2,1,0:T(8,128)(2,1)}), f16[32,16,1024]{2,1,0:T(8,128)(2,1)S(1)}, u32[]{:S(2)}, u32[]{:S(2)}) async-start(f16[32,16,1024]{2,1,0:T(8,128)(2,1)} %bitcast.2), calls=%async_computation.3 | async-start | bytes 2097152 | tf_op jit(solution)/shard_map/all_to_all | solution.py:21
  108.3 7.2 %copy-start = (s32[32]{0:T(128)S(1)}, s32[32]{0:T(128)}, u32[]{:S(2)}) copy-start(s32[32]{0:T(128)} %param.5) | copy-start | bytes 388
  108.3 34.1 %all-to-all-start.4 = ((f16[32,16,1024]{2,1,0:T(8,128)(2,1)}), f16[32,16,1024]{2,1,0:T(8,128)(2,1)S(1)}, u32[]{:S(2)}, u32[]{:S(2)}) async-start(f16[32,16,1024]{2,1,0:T(8,128)(2,1)} %bitcast.5), calls=%async_computation.4 | async-start | bytes 2097152 | tf_op jit(solution)/shard_map/all_to_all | solution.py:21
  144.4 13.5 %all-to-all-start.5 = ((f32[16,1,96]{2,1,0:T(1,128)}), f32[16,1,96]{2,1,0:T(1,128)S(1)}, u32[]{:S(2)}, u32[]{:S(2)}) async-start(f32[16,1,96]{2,1,0:T(1,128)} %broadcast_in_dim.16), calls=%async_computation.5 | async-start | bytes 16384 | tf_op jit(solution)/shard_map/all_to_all | solution.py:11
Sparse Core Ops, SparseCore 0:
  11.9 90.2 all-gather.1

commit v3 on v1

--- a/solution.py
+++ b/solution.py
@@ -14,20 +14,39 @@
 def local(ny, nz, nx, hidden, head_weight, tokens):
     n, k = hidden.shape
     cols = head_weight.shape[1]
-    core = lax.axis_index("core")
-    mine = spread(spread(hidden, "y", ny), "x", nx)
-    mine = jnp.swapaxes(mine, 0, 1).reshape(ny * nx * n, k)
-    other = lax.ppermute(mine, "core", [(0, 1), (1, 0)])
+    core, at = lax.axis_index("core"), lax.axis_index("x")
 
-    def reduced(rows):
-        part = jnp.dot(rows, head_weight, preferred_element_type=F32).astype(F16)
-        part = lax.all_to_all(part.reshape(nz, nx * n, cols), "rows", split_axis=0, concat_axis=0, tiled=True)
-        return jnp.sum(part.astype(F32), axis=0)
+    base = spread(hidden, "y", ny)
 
-    first, second = reduced(mine), reduced(other)
-    both = jnp.where(core == 0, jnp.stack([first, second]), jnp.stack([second, first]))
-    both = both.astype(F16).reshape(nx, 2 * n, cols)
-    logits = lax.all_to_all(both, "x", split_axis=0, concat_axis=0, tiled=True)
+    def product(mine):
+        other = lax.ppermute(mine, "core", [(0, 1), (1, 0)])
+        both = jnp.concatenate([mine, other], axis=1).reshape(ny * 2 * n, k)
+        part = jnp.dot(both, head_weight, preferred_element_type=F32).astype(F16)
+        return part.reshape(nz, 2 * n, cols)
+
+    def summed(part):
+        part = lax.all_to_all(part, "rows", split_axis=0, concat_axis=0, tiled=True)
+        return jnp.sum(part.astype(F32), axis=0).reshape(2, 1, n, cols)
+
+    sums = {}
+    part = product(base)
+    order = [0, 1, 3, 2]
+    blocks = {s: lax.ppermute(base, "x", [(i, (i + s) % nx) for i in range(nx)]) for s in order[1:]}
+    for s, after in zip(order, order[1:] + [None]):
+        sums[s] = summed(part)
+        if after is not None:
+            mine, part = lax.optimization_barrier((blocks[after], part))
+            part = product(mine)
+    shape = (2, nx, n, cols)
+    to_core = lax.broadcasted_iota(jnp.int32, shape, 0)
+    to_x = lax.broadcasted_iota(jnp.int32, shape, 1)
+    turned = jnp.zeros(shape, F32)
+    for s in order:
+        for o in range(2):
+            here = (to_core == core ^ o) & (to_x == lax.rem(at + nx - s, nx))
+            turned = jnp.where(here, sums[s][o], turned)
+    turned = turned.astype(F16)
+    logits = lax.all_to_all(turned.reshape(nx, 2 * n, cols), "x", split_axis=0, concat_axis=0, tiled=True)
     logits = jnp.swapaxes(logits, 0, 1).reshape(2 * n, nx * cols).astype(F32)
 
     width = logits.shape[1]

time: 159 us -> 176 us (1.11)
  blocking collectives: 50.6 us -> 22.2 us
  starting transfers between devices: 28 us -> 54.6 us
  waiting for transfers between devices: 64.9 us -> 73.2 us
  matrix products: 9.5 us -> 17.1 us
    all_to_all x2 -> x1, blocking collectives: 50.6 us -> 22.2 us  [spread(): lax.all_to_all(jnp.broadcast_to(x[None], (size,) + x.shape), axis, split_...]
    ppermute x1 -> x7, waiting for transfers between devices: 0.01 us -> 18.8 us  [the longest x3 18.8 us: local(): lax.ppermute(base, 'x', [(i, (i + s) % nx) for i in range(nx)])]
    ppermute x1 -> x7, starting transfers between devices: 6.12 us -> 22.7 us  [the longest x4 14 us: product(): other = lax.ppermute(mine, 'core', [(0, 1), (1, 0)])]
    all_to_all x3 -> x5, waiting for transfers between devices: 58 us -> 47.5 us  [the longest x4 41.5 us: summed(): part = lax.all_to_all(part, 'rows', split_axis=0, concat_axis=0, tiled=True)]
    all_to_all x3 -> x5, starting transfers between devices: 17 us -> 27 us  [the longest x4 23.6 us: summed(): part = lax.all_to_all(part, 'rows', split_axis=0, concat_axis=0, tiled=True)]
    dot_general x2 -> x4, matrix products: 9.5 us -> 17.1 us  [product(): part = jnp.dot(both, head_weight, preferred_element_type=F32).astype(F16)]
  transfers between devices with their start and end apart: 5 -> 13, of which waited for: 4 -> 7; matrix products, arithmetic and copies ran while one was open for 6% -> 11% of each run, Pallas kernels for 0% -> 0%
where the time goes in v3:
time: 176 us; the launch traced here: 175 us
  waiting for transfers between devices  73.2 us (42%)
  starting transfers between devices  54.6 us (31%)
  blocking collectives  22.2 us (13%)
  matrix products  17.1 us (10%)
  other arithmetic  3.93 us (2%)
  local copies, waits for them, and re-layouts  2.61 us (1%)
    all_to_all x4, waiting for transfers between devices, summed(): part = lax.all_to_all(part, 'rows', split_axis=0, concat_axis=0, tiled=True)  41.5 us
    all_to_all x4, starting transfers between devices, summed(): part = lax.all_to_all(part, 'rows', split_axis=0, concat_axis=0, tiled=True)  23.6 us
    all_to_all x1, blocking collectives, spread(): lax.all_to_all(jnp.broadcast_to(x[None], (size,) + x.shape), axis, split_...  22.2 us
    ppermute x3, waiting for transfers between devices, local(): lax.ppermute(base, 'x', [(i, (i + s) % nx) for i in range(nx)])  18.8 us
    dot_general x4, matrix products, product(): part = jnp.dot(both, head_weight, preferred_element_type=F32).astype(F16)  17.1 us
    ppermute x4, starting transfers between devices, product(): other = lax.ppermute(mine, 'core', [(0, 1), (1, 0)])  14 us
    ppermute x3, starting transfers between devices, local(): lax.ppermute(base, 'x', [(i, (i + s) % nx) for i in range(nx)])  8.72 us
    all_to_all x1, waiting for transfers between devices, spread(): lax.all_to_all(jnp.broadcast_to(x[None], (size,) + x.shape), axis, split_...  6.9 us
  transfers between devices with their start and end apart: 13, of which 7 were waited for; matrix products, arithmetic and copies ran while one was open for 11% of the time, Pallas kernels for 0%

profile of v3, /device:TPU:1, one launch (start us, length us, event | category | flops | bytes accessed | tf_op | source)
XLA Modules:
  0.0 174.5 jit_solution(10073526499492606301)
XLA Ops:
  1.5 22.2 %all_to_all.39 = bf16[8,16,2048]{2,1,0:T(8,128)(2,1)S(1)} all-to-all(bf16[8,16,2048]{2,1,0:T(8,128)(2,1)S(1)} %broadcast_in_dim.83), channel_id=1, replica_groups=mesh['y'=8,'core'=2,'rows'=8,'x'=4] {'y'}, dimensions={0} | all-to-all | bytes 1048576 | tf_op jit(solution)/shard_map/all_to_all | solution.py:11
  23.7 5.6 %collective-permute-start.3 = (bf16[8,16,2048]{2,1,0:T(8,128)(2,1)S(1)}, bf16[8,16,2048]{2,1,0:T(8,128)(2,1)S(1)}, u32[]{:S(2)}, u32[]{:S(2)}) collective-permute-start(bf16[8,16,2048]{2,1,0:T(8,128)(2,1)S(1)} %all_to_all.39), channel_id=1, source_target_pairs={{0,32},{32,0},{1,33},{33,1},{2,34},{34,2},{3,35},{35,3},{4,36},{36... | collective-permute-start | bytes 1572872 | tf_op jit(solution)/shard_map/ppermute | solution.py:22
  29.3 3.1 %collective-permute-start.2 = (bf16[8,16,2048]{2,1,0:T(8,128)(2,1)S(1)}, bf16[8,16,2048]{2,1,0:T(8,128)(2,1)S(1)}, u32[]{:S(2)}, u32[]{:S(2)}) collective-permute-start(bf16[8,16,2048]{2,1,0:T(8,128)(2,1)S(1)} %all_to_all.39), channel_id=1, source_target_pairs={{0,1},{1,2},{2,3},{3,0},{4,5},{5,6},{6,7},{7,4},{8,9},{9,10},{10,1... | collective-permute-start | bytes 1572872 | tf_op jit(solution)/shard_map/ppermute | solution.py:34
  32.6 4.3 %convolution_convert_fusion.3 = f16[256,1024]{1,0:T(8,128)(2,1)} fusion(bf16[256,2048]{1,0:T(8,128)(2,1)S(1)} %bitcast.52, bf16[2048,1024]{1,0:T(8,128)(2,1)} %param.4), kind=kOutput, calls=%fused_computation.3 | convolution fusion | flops 1074003968 | bytes 5767168 | tf_op jit(solution)/shard_map/dot_general | solution.py:24
  36.8 9.2 %collective-permute-done.2 = bf16[8,16,2048]{2,1,0:T(8,128)(2,1)S(1)} collective-permute-done((bf16[8,16,2048]{2,1,0:T(8,128)(2,1)S(1)}, bf16[8,16,2048]{2,1,0:T(8,128)(2,1)S(1)}, u32[]{:S(2)}, u32[]{:S(2)}) %collective-permute-start.2) | collective-permute-done | bytes 524320 | tf_op jit(solution)/shard_map/ppermute | solution.py:34
  46.0 2.7 %collective-permute-start.4 = (bf16[8,16,2048]{2,1,0:T(8,128)(2,1)S(1)}, bf16[8,16,2048]{2,1,0:T(8,128)(2,1)S(1)}, u32[]{:S(2)}, u32[]{:S(2)}) collective-permute-start(bf16[8,16,2048]{2,1,0:T(8,128)(2,1)S(1)} %collective-permute-done.2), channel_id=1, source_target_pairs={{0,32},{32,0},{1,33},{33,1},{2,34},{34,2},{3,35},{35,3},{4,36},{36... | collective-permute-start | bytes 1572872 | tf_op jit(solution)/shard_map/ppermute | solution.py:22
  48.7 3.2 %collective-permute-start.1 = (bf16[8,16,2048]{2,1,0:T(8,128)(2,1)S(1)}, bf16[8,16,2048]{2,1,0:T(8,128)(2,1)S(1)}, u32[]{:S(2)}, u32[]{:S(2)}) collective-permute-start(bf16[8,16,2048]{2,1,0:T(8,128)(2,1)S(1)} %all_to_all.39), channel_id=1, source_target_pairs={{0,3},{1,0},{2,1},{3,2},{4,7},{5,4},{6,5},{7,6},{8,11},{9,8},{10,9... | collective-permute-start | bytes 1572872 | tf_op jit(solution)/shard_map/ppermute | solution.py:34
  51.9 10.0 %all-to-all-start.4 = ((f16[8,32,1024]{2,1,0:T(8,128)(2,1)}), f16[8,32,1024]{2,1,0:T(8,128)(2,1)S(1)}, u32[]{:S(2)}, u32[]{:S(2)}) async-start(f16[8,32,1024]{2,1,0:T(8,128)(2,1)} %bitcast.1), calls=%async_computation.4 | async-start | bytes 1048576 | tf_op jit(solution)/shard_map/all_to_all | solution.py:28
  62.0 4.3 %convolution_convert_fusion.2 = f16[256,1024]{1,0:T(8,128)(2,1)} fusion(bf16[256,2048]{1,0:T(8,128)(2,1)S(1)} %bitcast.49, bf16[2048,1024]{1,0:T(8,128)(2,1)} %param.4), kind=kOutput, calls=%fused_computation.2 | convolution fusion | flops 1074003968 | bytes 5767168 | tf_op jit(solution)/shard_map/dot_general | solution.py:24
  66.3 2.5 %collective-permute-start.5 = (bf16[8,16,2048]{2,1,0:T(8,128)(2,1)S(1)}, bf16[8,16,2048]{2,1,0:T(8,128)(2,1)S(1)}, u32[]{:S(2)}, u32[]{:S(2)}) collective-permute-start(bf16[8,16,2048]{2,1,0:T(8,128)(2,1)S(1)} %collective-permute-done.1), channel_id=1, source_target_pairs={{0,32},{32,0},{1,33},{33,1},{2,34},{34,2},{3,35},{35,3},{4,36},{36... | collective-permute-start | bytes 1572872 | tf_op jit(solution)/shard_map/ppermute | solution.py:22
  68.8 11.1 %all-to-all-done.4 = f16[8,32,1024]{2,1,0:T(8,128)(2,1)S(1)} async-done(((f16[8,32,1024]{2,1,0:T(8,128)(2,1)}), f16[8,32,1024]{2,1,0:T(8,128)(2,1)S(1)}, u32[]{:S(2)}, u32[]{:S(2)}) %all-to-all-start.4) | async-done | bytes 524320 | tf_op jit(solution)/shard_map/all_to_all | solution.py:28
  79.9 3.5 %all-to-all-start.3 = ((f16[8,32,1024]{2,1,0:T(8,128)(2,1)}), f16[8,32,1024]{2,1,0:T(8,128)(2,1)S(1)}, u32[]{:S(2)}, u32[]{:S(2)}) async-start(f16[8,32,1024]{2,1,0:T(8,128)(2,1)} %bitcast.3), calls=%async_computation.3 | async-start | bytes 1048576 | tf_op jit(solution)/shard_map/all_to_all | solution.py:28
  85.9 4.3 %convolution_convert_fusion.1 = f16[256,1024]{1,0:T(8,128)(2,1)} fusion(bf16[256,2048]{1,0:T(8,128)(2,1)S(1)} %bitcast.50, bf16[2048,1024]{1,0:T(8,128)(2,1)} %param.4), kind=kOutput, calls=%fused_computation.1 | convolution fusion | flops 1074003968 | bytes 5767168 | tf_op jit(solution)/shard_map/dot_general | solution.py:24
  90.2 9.6 %collective-permute-done = bf16[8,16,2048]{2,1,0:T(8,128)(2,1)S(1)} collective-permute-done((bf16[8,16,2048]{2,1,0:T(8,128)(2,1)S(1)}, bf16[8,16,2048]{2,1,0:T(8,128)(2,1)S(1)}, u32[]{:S(2)}, u32[]{:S(2)}) %collective-permute-start) | collective-permute-done | bytes 524320 | tf_op jit(solution)/shard_map/ppermute | solution.py:34
  99.8 3.2 %collective-permute-start.6 = (bf16[8,16,2048]{2,1,0:T(8,128)(2,1)S(1)}, bf16[8,16,2048]{2,1,0:T(8,128)(2,1)S(1)}, u32[]{:S(2)}, u32[]{:S(2)}) collective-permute-start(bf16[8,16,2048]{2,1,0:T(8,128)(2,1)S(1)} %collective-permute-done), channel_id=1, source_target_pairs={{0,32},{32,0},{1,33},{33,1},{2,34},{34,2},{3,35},{35,3},{4,36},{36... | collective-permute-start | bytes 1572872 | tf_op jit(solution)/shard_map/ppermute | solution.py:22
  103.1 6.6 %all-to-all-start.2 = ((f16[8,32,1024]{2,1,0:T(8,128)(2,1)}), f16[8,32,1024]{2,1,0:T(8,128)(2,1)S(1)}, u32[]{:S(2)}, u32[]{:S(2)}) async-start(f16[8,32,1024]{2,1,0:T(8,128)(2,1)} %bitcast.5), calls=%async_computation.2 | async-start | bytes 1048576 | tf_op jit(solution)/shard_map/all_to_all | solution.py:28
  110.6 4.3 %convolution_convert_fusion = f16[256,1024]{1,0:T(8,128)(2,1)} fusion(bf16[256,2048]{1,0:T(8,128)(2,1)S(1)} %bitcast.51, bf16[2048,1024]{1,0:T(8,128)(2,1)} %param.4), kind=kOutput, calls=%fused_computation | convolution fusion | flops 1074003968 | bytes 5767168 | tf_op jit(solution)/shard_map/dot_general | solution.py:24
  114.8 12.8 %all-to-all-done.2 = f16[8,32,1024]{2,1,0:T(8,128)(2,1)S(1)} async-done(((f16[8,32,1024]{2,1,0:T(8,128)(2,1)}), f16[8,32,1024]{2,1,0:T(8,128)(2,1)S(1)}, u32[]{:S(2)}, u32[]{:S(2)}) %all-to-all-start.2) | async-done | bytes 524320 | tf_op jit(solution)/shard_map/all_to_all | solution.py:28
  127.7 3.5 %all-to-all-start.1 = ((f16[8,32,1024]{2,1,0:T(8,128)(2,1)}), f16[8,32,1024]{2,1,0:T(8,128)(2,1)S(1)}, u32[]{:S(2)}, u32[]{:S(2)}) async-start(f16[8,32,1024]{2,1,0:T(8,128)(2,1)} %bitcast.7), calls=%async_computation.1 | async-start | bytes 1048576 | tf_op jit(solution)/shard_map/all_to_all | solution.py:28
  131.4 17.6 %all-to-all-done.1 = f16[8,32,1024]{2,1,0:T(8,128)(2,1)S(1)} async-done(((f16[8,32,1024]{2,1,0:T(8,128)(2,1)}), f16[8,32,1024]{2,1,0:T(8,128)(2,1)S(1)}, u32[]{:S(2)}, u32[]{:S(2)}) %all-to-all-start.1) | async-done | bytes 524320 | tf_op jit(solution)/shard_map/all_to_all | solution.py:28
  150.6 3.4 %all-to-all-start.5 = ((f16[4,32,1024]{2,1,0:T(8,128)(2,1)}), f16[4,32,1024]{2,1,0:T(8,128)(2,1)S(1)}, u32[]{:S(2)}, u32[]{:S(2)}) async-start(f16[4,32,1024]{2,1,0:T(8,128)(2,1)} %select_convert_fusion), calls=%async_computation.5 | async-start | bytes 524288 | tf_op jit(solution)/shard_map/all_to_all | solution.py:49
  154.0 5.9 %all-to-all-done.5 = f16[4,32,1024]{2,1,0:T(8,128)(2,1)S(1)} async-done(((f16[4,32,1024]{2,1,0:T(8,128)(2,1)}), f16[4,32,1024]{2,1,0:T(8,128)(2,1)S(1)}, u32[]{:S(2)}, u32[]{:S(2)}) %all-to-all-start.5) | async-done | bytes 262176 | tf_op jit(solution)/shard_map/all_to_all | solution.py:49
  161.1 4.9 %all-to-all-start.6 = ((f32[16,1,96]{2,1,0:T(1,128)}), f32[16,1,96]{2,1,0:T(1,128)S(1)}, u32[]{:S(2)}, u32[]{:S(2)}) async-start(f32[16,1,96]{2,1,0:T(1,128)} %broadcast_in_dim.102), calls=%async_computation.6 | async-start | bytes 16384 | tf_op jit(solution)/shard_map/all_to_all | solution.py:11
  166.1 6.9 %all-to-all-done.6 = f32[16,1,96]{2,1,0:T(1,128)S(1)} async-done(((f32[16,1,96]{2,1,0:T(1,128)}), f32[16,1,96]{2,1,0:T(1,128)S(1)}, u32[]{:S(2)}, u32[]{:S(2)}) %all-to-all-start.6) | async-done | bytes 6176 | tf_op jit(solution)/shard_map/all_to_all | solution.py:11
  (54 shorter events, 9.0 us)
Async XLA Ops:
  23.7 8.7 %collective-permute-start.3 = (bf16[8,16,2048]{2,1,0:T(8,128)(2,1)S(1)}, bf16[8,16,2048]{2,1,0:T(8,128)(2,1)S(1)}, u32[]{:S(2)}, u32[]{:S(2)}) collective-permute-start(bf16[8,16,2048]{2,1,0:T(8,128)(2,1)S(1)} %all_to_all.39), channel_id=1, source_target_pairs={{0,32},{32,0},{1,33},{33,1},{2,34},{34,2},{3,35},{35,3},{4,36},{36... | collective-permute-start | bytes 1572872 | tf_op jit(solution)/shard_map/ppermute | solution.py:22
  29.3 16.6 %collective-permute-start.2 = (bf16[8,16,2048]{2,1,0:T(8,128)(2,1)S(1)}, bf16[8,16,2048]{2,1,0:T(8,128)(2,1)S(1)}, u32[]{:S(2)}, u32[]{:S(2)}) collective-permute-start(bf16[8,16,2048]{2,1,0:T(8,128)(2,1)S(1)} %all_to_all.39), channel_id=1, source_target_pairs={{0,1},{1,2},{2,3},{3,0},{4,5},{5,6},{6,7},{7,4},{8,9},{9,10},{10,1... | collective-permute-start | bytes 1572872 | tf_op jit(solution)/shard_map/ppermute | solution.py:34
  46.0 15.9 %collective-permute-start.4 = (bf16[8,16,2048]{2,1,0:T(8,128)(2,1)S(1)}, bf16[8,16,2048]{2,1,0:T(8,128)(2,1)S(1)}, u32[]{:S(2)}, u32[]{:S(2)}) collective-permute-start(bf16[8,16,2048]{2,1,0:T(8,128)(2,1)S(1)} %collective-permute-done.2), channel_id=1, source_target_pairs={{0,32},{32,0},{1,33},{33,1},{2,34},{34,2},{3,35},{35,3},{4,36},{36... | collective-permute-start | bytes 1572872 | tf_op jit(solution)/shard_map/ppermute | solution.py:22
  48.7 17.6 %collective-permute-start.1 = (bf16[8,16,2048]{2,1,0:T(8,128)(2,1)S(1)}, bf16[8,16,2048]{2,1,0:T(8,128)(2,1)S(1)}, u32[]{:S(2)}, u32[]{:S(2)}) collective-permute-start(bf16[8,16,2048]{2,1,0:T(8,128)(2,1)S(1)} %all_to_all.39), channel_id=1, source_target_pairs={{0,3},{1,0},{2,1},{3,2},{4,7},{5,4},{6,5},{7,6},{8,11},{9,8},{10,9... | collective-permute-start | bytes 1572872 | tf_op jit(solution)/shard_map/ppermute | solution.py:34
  51.9 28.0 %all-to-all-start.4 = ((f16[8,32,1024]{2,1,0:T(8,128)(2,1)}), f16[8,32,1024]{2,1,0:T(8,128)(2,1)S(1)}, u32[]{:S(2)}, u32[]{:S(2)}) async-start(f16[8,32,1024]{2,1,0:T(8,128)(2,1)} %bitcast.1), calls=%async_computation.4 | async-start | bytes 1048576 | tf_op jit(solution)/shard_map/all_to_all | solution.py:28
  66.3 19.5 %collective-permute-start.5 = (bf16[8,16,2048]{2,1,0:T(8,128)(2,1)S(1)}, bf16[8,16,2048]{2,1,0:T(8,128)(2,1)S(1)}, u32[]{:S(2)}, u32[]{:S(2)}) collective-permute-start(bf16[8,16,2048]{2,1,0:T(8,128)(2,1)S(1)} %collective-permute-done.1), channel_id=1, source_target_pairs={{0,32},{32,0},{1,33},{33,1},{2,34},{34,2},{3,35},{35,3},{4,36},{36... | collective-permute-start | bytes 1572872 | tf_op jit(solution)/shard_map/ppermute | solution.py:22
  79.9 23.2 %all-to-all-start.3 = ((f16[8,32,1024]{2,1,0:T(8,128)(2,1)}), f16[8,32,1024]{2,1,0:T(8,128)(2,1)S(1)}, u32[]{:S(2)}, u32[]{:S(2)}) async-start(f16[8,32,1024]{2,1,0:T(8,128)(2,1)} %bitcast.3), calls=%async_computation.3 | async-start | bytes 1048576 | tf_op jit(solution)/shard_map/all_to_all | solution.py:28
  83.4 16.4 %collective-permute-start = (bf16[8,16,2048]{2,1,0:T(8,128)(2,1)S(1)}, bf16[8,16,2048]{2,1,0:T(8,128)(2,1)S(1)}, u32[]{:S(2)}, u32[]{:S(2)}) collective-permute-start(bf16[8,16,2048]{2,1,0:T(8,128)(2,1)S(1)} %all_to_all.39), channel_id=1, source_target_pairs={{0,2},{1,3},{2,0},{3,1},{4,6},{5,7},{6,4},{7,5},{8,10},{9,11},{10,... | collective-permute-start | bytes 1572872 | tf_op jit(solution)/shard_map/ppermute | solution.py:34
  99.8 10.7 %collective-permute-start.6 = (bf16[8,16,2048]{2,1,0:T(8,128)(2,1)S(1)}, bf16[8,16,2048]{2,1,0:T(8,128)(2,1)S(1)}, u32[]{:S(2)}, u32[]{:S(2)}) collective-permute-start(bf16[8,16,2048]{2,1,0:T(8,128)(2,1)S(1)} %collective-permute-done), channel_id=1, source_target_pairs={{0,32},{32,0},{1,33},{33,1},{2,34},{34,2},{3,35},{35,3},{4,36},{36... | collective-permute-start | bytes 1572872 | tf_op jit(solution)/shard_map/ppermute | solution.py:22
  103.1 24.6 %all-to-all-start.2 = ((f16[8,32,1024]{2,1,0:T(8,128)(2,1)}), f16[8,32,1024]{2,1,0:T(8,128)(2,1)S(1)}, u32[]{:S(2)}, u32[]{:S(2)}) async-start(f16[8,32,1024]{2,1,0:T(8,128)(2,1)} %bitcast.5), calls=%async_computation.2 | async-start | bytes 1048576 | tf_op jit(solution)/shard_map/all_to_all | solution.py:28
  127.7 21.4 %all-to-all-start.1 = ((f16[8,32,1024]{2,1,0:T(8,128)(2,1)}), f16[8,32,1024]{2,1,0:T(8,128)(2,1)S(1)}, u32[]{:S(2)}, u32[]{:S(2)}) async-start(f16[8,32,1024]{2,1,0:T(8,128)(2,1)} %bitcast.7), calls=%async_computation.1 | async-start | bytes 1048576 | tf_op jit(solution)/shard_map/all_to_all | solution.py:28
  149.3 10.8 %copy-start = (s32[32]{0:T(128)S(1)}, s32[32]{0:T(128)}, u32[]{:S(2)}) copy-start(s32[32]{0:T(128)} %param.5) | copy-start | bytes 388
  150.6 9.4 %all-to-all-start.5 = ((f16[4,32,1024]{2,1,0:T(8,128)(2,1)}), f16[4,32,1024]{2,1,0:T(8,128)(2,1)S(1)}, u32[]{:S(2)}, u32[]{:S(2)}) async-start(f16[4,32,1024]{2,1,0:T(8,128)(2,1)} %select_convert_fusion), calls=%async_computation.5 | async-start | bytes 524288 | tf_op jit(solution)/shard_map/all_to_all | solution.py:49
  161.1 11.9 %all-to-all-start.6 = ((f32[16,1,96]{2,1,0:T(1,128)}), f32[16,1,96]{2,1,0:T(1,128)S(1)}, u32[]{:S(2)}, u32[]{:S(2)}) async-start(f32[16,1,96]{2,1,0:T(1,128)} %broadcast_in_dim.102), calls=%async_computation.6 | async-start | bytes 16384 | tf_op jit(solution)/shard_map/all_to_all | solution.py:11

commit v4 on v1

v4 whole, which is shorter than its diff:
```python
import jax
import jax.numpy as jnp
from jax import lax
from jax.sharding import Mesh, PartitionSpec as P

F16 = jnp.float16
F32 = jnp.float32
Y = ("yh", "yl")
Z = ("zh", "zl")


def spread(x, axis, size):
    return lax.all_to_all(jnp.broadcast_to(x[None], (size,) + x.shape), axis, split_axis=0, concat_axis=0, tiled=True)


def local(ny, nz, nx, hidden, head_weight, tokens):
    n, k = hidden.shape
    cols = head_weight.shape[1]
    half = cols // 2
    yh, zh = ny // 2, nz // 2
    core, odd = lax.axis_index("core"), lax.axis_index("zl")
    west = [(i, i ^ 1) for i in range(nz)]
    east = [(i, (i + 1) % nz if i % 2 else (i - 1) % nz) for i in range(nz)]

    mine = spread(spread(hidden, "yh", yh), ("yl", "x"), 2 * nx).reshape(2, nx, yh, n, k)
    give = lax.dynamic_index_in_dim(mine, 1 - odd, 0, keepdims=False)
    keep = lax.dynamic_index_in_dim(mine, odd, 0, keepdims=False)
    give_other = lax.ppermute(give, "core", [(0, 1), (1, 0)])
    keep_other = lax.ppermute(keep, "core", [(0, 1), (1, 0)])

    def product(own, other):
        place = lax.broadcasted_iota(jnp.int32, (2,) + own.shape, 0)
        rows = jnp.where(place == core, own[None], other[None])
        rows = jnp.transpose(rows, (2, 0, 1, 3, 4)).reshape(yh * 2 * nx * n, k)
        return jnp.dot(rows, head_weight, preferred_element_type=F32)

    given = product(give, give_other).astype(F16)
    left = lax.ppermute(given[:, :half], Z, west)
    right = lax.ppermute(given[:, half:], Z, east)
    kept = lax.optimization_barrier(product(keep, keep_other))
    pair = (kept + jnp.concatenate([left, right], axis=1).astype(F32)).astype(F16)
    part = lax.all_to_all(pair.reshape(zh * nx, 2 * n, cols), ("zh", "x"), split_axis=0, concat_axis=0, tiled=True)
    logits = jnp.sum(part.reshape(zh, nx, 2 * n, cols).astype(F32), axis=0)
    logits = jnp.swapaxes(logits, 0, 1).reshape(2 * n, nx * cols)

    width = logits.shape[1]
    column = lax.axis_index(Y + ("core",)) * width + lax.broadcasted_iota(jnp.int32, logits.shape, 1)
    peak = jnp.max(logits, axis=1)
    total = jnp.sum(jnp.exp(logits - peak[:, None]), axis=1)
    picked = jnp.sum(jnp.where(column == tokens[:, None], logits, 0.0), axis=1)
    stats, logits = lax.optimization_barrier((jnp.concatenate([peak, total, picked]), logits))
    peaks, totals, picks = jnp.split(spread(stats, Y + ("core",), 2 * ny), 3, axis=1)
    row_peak = jnp.max(peaks, axis=0)
    row_total = jnp.sum(totals * jnp.exp(peaks - row_peak), axis=0)
    shift = jnp.log(row_total)
    logprobs = logits - row_peak[:, None] - shift[:, None]
    target_logp = jnp.sum(picks, axis=0) - row_peak - shift
    return (logprobs, target_logp)


def solution(mesh):
    nv, nz, nx = mesh.devices.shape
    ny = nv // 2
    split = Mesh(mesh.devices.reshape(ny // 2, 2, 2, nz // 2, 2, nx), Y + ("core",) + Z + ("x",))
    in_specs = (P(Y + ("core", "x"), Z), P(Z, Y + ("core", "x")), P(Z + ("x",)))
    out_specs = (P(Z + ("x",), Y + ("core",)), P(Z + ("x",)))

    def body(*args):
        return local(ny, nz, nx, *args)

    return jax.shard_map(body, mesh=split, in_specs=in_specs, out_specs=out_specs, check_vma=False)
```

time: 159 us -> 143 us (0.90)
  blocking collectives: 50.6 us -> 31.4 us
  matrix products: 9.5 us -> 4.72 us
  other arithmetic: 3.35 us -> 7.4 us
  local copies, waits for them, and re-layouts: 1.93 us -> 4.84 us
    all_to_all x3 -> x1, waiting for transfers between devices: 58 us -> 27.3 us  [local(): lax.all_to_all(pair.reshape(zh * nx, 2 * n, cols), ('zh', 'x'), split_axi...]
    all_to_all x2, blocking collectives: 50.6 us -> 31.4 us  [spread(): lax.all_to_all(jnp.broadcast_to(x[None], (size,) + x.shape), axis, split_...]
    all_to_all x1, waiting for transfers between devices: 6.9 us -> 26 us  [spread(): lax.all_to_all(jnp.broadcast_to(x[None], (size,) + x.shape), axis, split_...]
    ppermute x1 -> x4, waiting for transfers between devices: 0.01 us -> 12.2 us  [the longest x1 8.61 us: local(): right = lax.ppermute(given[:, half:], Z, east)]
    ppermute x1 -> x4, starting transfers between devices: 6.12 us -> 17.7 us  [the longest x1 8.85 us: local(): right = lax.ppermute(given[:, half:], Z, east)]
    all_to_all x3 -> x1, starting transfers between devices: 17 us -> 5.85 us  [local(): lax.all_to_all(pair.reshape(zh * nx, 2 * n, cols), ('zh', 'x'), split_axi...]
    dot_general x2, matrix products: 9.5 us -> 4.72 us  [product(): return jnp.dot(rows, head_weight, preferred_element_type=F32)]
    select_n x0 -> x1, other arithmetic: none -> 3.71 us  [product(): rows = jnp.where(place == core, own[None], other[None])]
  transfers between devices with their start and end apart: 5 -> 6, of which waited for: 4 -> 6; matrix products, arithmetic and copies ran while one was open for 6% -> 2% of each run, Pallas kernels for 0% -> 0%
where the time goes in v4:
time: 143 us; the launch traced here: 142 us
  waiting for transfers between devices  65.5 us (46%)
  blocking collectives  31.4 us (22%)
  starting transfers between devices  27.9 us (20%)
  other arithmetic  7.4 us (5%)
  local copies, waits for them, and re-layouts  4.84 us (3%)
  matrix products  4.72 us (3%)
    all_to_all x2, blocking collectives, spread(): lax.all_to_all(jnp.broadcast_to(x[None], (size,) + x.shape), axis, split_...  31.4 us
    all_to_all x1, waiting for transfers between devices, local(): lax.all_to_all(pair.reshape(zh * nx, 2 * n, cols), ('zh', 'x'), split_axi...  27.3 us
    all_to_all x1, waiting for transfers between devices, spread(): lax.all_to_all(jnp.broadcast_to(x[None], (size,) + x.shape), axis, split_...  26 us
    ppermute x1, starting transfers between devices, local(): right = lax.ppermute(given[:, half:], Z, east)  8.85 us
    ppermute x1, waiting for transfers between devices, local(): right = lax.ppermute(given[:, half:], Z, east)  8.61 us
    all_to_all x1, starting transfers between devices, local(): lax.all_to_all(pair.reshape(zh * nx, 2 * n, cols), ('zh', 'x'), split_axi...  5.85 us
    dot_general x2, matrix products, product(): return jnp.dot(rows, head_weight, preferred_element_type=F32)  4.72 us
    all_to_all x1, starting transfers between devices, spread(): lax.all_to_all(jnp.broadcast_to(x[None], (size,) + x.shape), axis, split_...  4.29 us
  transfers between devices with their start and end apart: 6, of which 6 were waited for; matrix products, arithmetic and copies ran while one was open for 2% of the time, Pallas kernels for 0%

profile of v4, /device:TPU:1, one launch (start us, length us, event | category | flops | bytes accessed | tf_op | source)
XLA Modules:
  0.0 142.4 jit_solution(103780744826508147)
XLA Ops:
  0.6 0.9 broadcast_in_dim.77
  1.5 16.4 %all_to_all.24 = bf16[4,16,2048]{2,1,0:T(8,128)(2,1)S(1)} all-to-all(bf16[4,16,2048]{2,1,0:T(8,128)(2,1)S(1)} %broadcast_in_dim.77), channel_id=1, replica_groups=mesh['yh'=4,'yl'=2,'core'=2,'zh'=4,'zl'=2,'x'=4] {'yh'}, dimensions={0} | all-to-all | bytes 524288 | tf_op jit(solution)/shard_map/all_to_all | solution.py:13
  17.9 1.6 %broadcast_in_dim.78 = bf16[8,4,16,2048]{3,2,1,0:T(8,128)(2,1)} broadcast(bf16[4,16,2048]{2,1,0:T(8,128)(2,1)S(1)} %all_to_all.24), dimensions={1,2,3} | broadcast | bytes 2359296 | tf_op jit(solution)/shard_map/broadcast_in_dim | solution.py:13
  19.5 4.3 %all-to-all-start.1 = ((bf16[8,4,16,2048]{3,2,1,0:T(8,128)(2,1)}), bf16[8,4,16,2048]{3,2,1,0:T(8,128)(2,1)S(1)}, u32[]{:S(2)}, u32[]{:S(2)}) async-start(bf16[8,4,16,2048]{3,2,1,0:T(8,128)(2,1)} %broadcast_in_dim.78), calls=%async_computation.1 | async-start | bytes 4194304 | tf_op jit(solution)/shard_map/all_to_all | solution.py:13
  23.8 26.0 %all-to-all-done.1 = bf16[8,4,16,2048]{3,2,1,0:T(8,128)(2,1)S(1)} async-done(((bf16[8,4,16,2048]{3,2,1,0:T(8,128)(2,1)}), bf16[8,4,16,2048]{3,2,1,0:T(8,128)(2,1)S(1)}, u32[]{:S(2)}, u32[]{:S(2)}) %all-to-all-start.1) | async-done | bytes 2097184 | tf_op jit(solution)/shard_map/all_to_all | solution.py:13
  49.8 1.9 %dynamic-slice_bitcast_fusion = (bf16[4,4,16,2048]{3,2,0,1:T(8,128)(2,1)S(1)}, bf16[4,4,16,2048]{3,2,0,1:T(8,128)(2,1)}, bf16[4,4,16,2048]{3,2,1,0:T(8,128)(2,1)}, bf16[4,4,16,2048]{3,2,1,0:T(8,128)(2,1)}) fusion(bf16[2,4,4,16,2048]{4,3,2,1,0:T(8,128)(2,1)S(1)} %bitcast.47, s32[]{:T(128)S(6)} %select_n.25, s32[]{:T(128)S(6)} %select_n.23), kind=kLoop, calls=%fused_computation.5 | loop fusion | bytes 6291464 | tf_op jit(solution)/shard_map/jit(_where)/broadcast_in_dim | solution.py:33
  51.7 2.9 %collective-permute-start = (bf16[4,4,16,2048]{3,2,1,0:T(8,128)(2,1)}, bf16[4,4,16,2048]{3,2,1,0:T(8,128)(2,1)S(1)}, u32[]{:S(2)}, u32[]{:S(2)}) collective-permute-start(bf16[4,4,16,2048]{3,2,1,0:T(8,128)(2,1)} %get-tuple-element.13), channel_id=1, source_target_pairs={{0,32},{32,0},{1,33},{33,1},{2,34},{34,2},{3,35},{35,3},{4,36},{36... | collective-permute-start | bytes 3145736 | tf_op jit(solution)/shard_map/ppermute | solution.py:29
  54.7 1.9 %collective-permute-start.1 = (bf16[4,4,16,2048]{3,2,1,0:T(8,128)(2,1)}, bf16[4,4,16,2048]{3,2,1,0:T(8,128)(2,1)S(1)}, u32[]{:S(2)}, u32[]{:S(2)}) collective-permute-start(bf16[4,4,16,2048]{3,2,1,0:T(8,128)(2,1)} %get-tuple-element.12), channel_id=1, source_target_pairs={{0,32},{32,0},{1,33},{33,1},{2,34},{34,2},{3,35},{35,3},{4,36},{36... | collective-permute-start | bytes 3145736 | tf_op jit(solution)/shard_map/ppermute | solution.py:28
  56.8 0.4 collective-permute-done
  57.1 2.3 %collective-permute-done.1 = bf16[4,4,16,2048]{3,2,1,0:T(8,128)(2,1)S(1)} collective-permute-done((bf16[4,4,16,2048]{3,2,1,0:T(8,128)(2,1)}, bf16[4,4,16,2048]{3,2,1,0:T(8,128)(2,1)S(1)}, u32[]{:S(2)}, u32[]{:S(2)}) %collective-permute-start.1) | collective-permute-done | bytes 1048608 | tf_op jit(solution)/shard_map/ppermute | solution.py:28
  59.4 3.7 %bitcast_select_fusion = (bf16[512,2048]{1,0:T(8,128)(2,1)S(1)}, bf16[512,2048]{1,0:T(8,128)(2,1)S(1)}) fusion(pred[512]{0:T(512)(128)(4,1)S(1)} %iota.31, bf16[4,4,16,2048]{3,2,0,1:T(8,128)(2,1)} %get-tuple-element.11, bf16[4,4,16,2048]{3,2,1,0:T(8,128)(2,1)S(1)} %collective-permute-done, bf16[4,4,16,2048]{3,2,0,1:T(8,128)(2,1)S(1)} %get-tuple-element.10, ...), kind=kLoop, calls=%fused_computation.1 | loop fusion | flops 2097152 | bytes 8389120 | tf_op jit(solution)/shard_map/jit(_where)/select_n | solution.py:33
  63.1 2.4 %convolution_convert_fusion = f16[512,1024]{1,0:T(8,128)(2,1)S(1)} fusion(bf16[512,2048]{1,0:T(8,128)(2,1)S(1)} %get-tuple-element.18, bf16[2048,1024]{1,0:T(8,128)(2,1)S(1)} %copy-done.1), kind=kOutput, calls=%fused_computation.4 | convolution fusion | flops 2148007936 | bytes 7340032 | tf_op jit(solution)/shard_map/dot_general | solution.py:35
  65.7 4.0 %collective-permute-start.2 = (f16[512,512]{1,0:T(8,128)(2,1)S(1)}, f16[512,512]{1,0:T(8,128)(2,1)S(1)}, u32[]{:S(2)}, u32[]{:S(2)}) collective-permute-start(f16[512,512]{1,0:T(8,128)(2,1)S(1)} %get-tuple-element.14), channel_id=1, source_target_pairs={{0,4},{4,0},{8,12},{12,8},{16,20},{20,16},{24,28},{28,24},{1,5},{5... | collective-permute-start | bytes 1572872 | tf_op jit(solution)/shard_map/ppermute | solution.py:38
  69.7 8.8 %collective-permute-start.3 = (f16[512,512]{1,0:T(8,128)(2,1)S(1)}, f16[512,512]{1,0:T(8,128)(2,1)S(1)}, u32[]{:S(2)}, u32[]{:S(2)}) collective-permute-start(f16[512,512]{1,0:T(8,128)(2,1)S(1)} %get-tuple-element.15), channel_id=1, source_target_pairs={{0,28},{4,8},{8,4},{12,16},{16,12},{20,24},{24,20},{28,0},{1,29},{... | collective-permute-start | bytes 1572872 | tf_op jit(solution)/shard_map/ppermute | solution.py:39
  78.6 2.4 %fusion.5 = f32[512,1024]{1,0:T(8,128)S(1)} fusion(bf16[512,2048]{1,0:T(8,128)(2,1)S(1)} %get-tuple-element.19, bf16[2048,1024]{1,0:T(8,128)(2,1)S(1)} %copy-done.1), kind=kOutput, calls=%fused_computation.24 | convolution fusion | flops 2147483648 | bytes 8388608 | tf_op jit(solution)/shard_map/dot_general | solution.py:35
  81.0 0.9 collective-permute-done.2
  81.9 8.6 %collective-permute-done.3 = f16[512,512]{1,0:T(8,128)(2,1)S(1)} collective-permute-done((f16[512,512]{1,0:T(8,128)(2,1)S(1)}, f16[512,512]{1,0:T(8,128)(2,1)S(1)}, u32[]{:S(2)}, u32[]{:S(2)}) %collective-permute-start.3) | collective-permute-done | bytes 524320 | tf_op jit(solution)/shard_map/ppermute | solution.py:39
  90.5 1.4 add_convert_fusion
  91.9 5.9 %all-to-all-start.2 = ((f16[16,32,1024]{2,1,0:T(8,128)(2,1)}), f16[16,32,1024]{2,1,0:T(8,128)(2,1)S(1)}, u32[]{:S(2)}, u32[]{:S(2)}) async-start(f16[16,32,1024]{2,1,0:T(8,128)(2,1)} %bitcast.11), calls=%async_computation.2 | async-start | bytes 2097152 | tf_op jit(solution)/shard_map/all_to_all | solution.py:42
  97.8 27.3 %all-to-all-done.2 = f16[16,32,1024]{2,1,0:T(8,128)(2,1)S(1)} async-done(((f16[16,32,1024]{2,1,0:T(8,128)(2,1)}), f16[16,32,1024]{2,1,0:T(8,128)(2,1)S(1)}, u32[]{:S(2)}, u32[]{:S(2)}) %all-to-all-start.2) | async-done | bytes 1048608 | tf_op jit(solution)/shard_map/all_to_all | solution.py:42
  125.5 0.3 fusion.1
  125.9 15.0 %all_to_all.25 = f32[16,1,96]{2,1,0:T(1,128)S(1)} all-to-all(f32[16,1,96]{2,1,0:T(1,128)S(1)} %broadcast_in_dim.94), channel_id=1, replica_groups=mesh['yh'=4,'yl'=2,'core'=2,'zh'=4,'zl'=2,'x'=4] {'yh','yl','core'}, dimensions={0} | all-to-all | bytes 12288 | tf_op jit(solution)/shard_map/all_to_all | solution.py:13
  141.0 0.5 subtract_subtract_fusion.1
  141.5 0.9 subtract_subtract_fusion
  (16 shorter events, 1.1 us)
Async XLA Ops:
  19.5 30.2 %all-to-all-start.1 = ((bf16[8,4,16,2048]{3,2,1,0:T(8,128)(2,1)}), bf16[8,4,16,2048]{3,2,1,0:T(8,128)(2,1)S(1)}, u32[]{:S(2)}, u32[]{:S(2)}) async-start(bf16[8,4,16,2048]{3,2,1,0:T(8,128)(2,1)} %broadcast_in_dim.78), calls=%async_computation.1 | async-start | bytes 4194304 | tf_op jit(solution)/shard_map/all_to_all | solution.py:13
  51.7 5.4 %collective-permute-start = (bf16[4,4,16,2048]{3,2,1,0:T(8,128)(2,1)}, bf16[4,4,16,2048]{3,2,1,0:T(8,128)(2,1)S(1)}, u32[]{:S(2)}, u32[]{:S(2)}) collective-permute-start(bf16[4,4,16,2048]{3,2,1,0:T(8,128)(2,1)} %get-tuple-element.13), channel_id=1, source_target_pairs={{0,32},{32,0},{1,33},{33,1},{2,34},{34,2},{3,35},{35,3},{4,36},{36... | collective-permute-start | bytes 3145736 | tf_op jit(solution)/shard_map/ppermute | solution.py:29
  54.7 4.8 %collective-permute-start.1 = (bf16[4,4,16,2048]{3,2,1,0:T(8,128)(2,1)}, bf16[4,4,16,2048]{3,2,1,0:T(8,128)(2,1)S(1)}, u32[]{:S(2)}, u32[]{:S(2)}) collective-permute-start(bf16[4,4,16,2048]{3,2,1,0:T(8,128)(2,1)} %get-tuple-element.12), channel_id=1, source_target_pairs={{0,32},{32,0},{1,33},{33,1},{2,34},{34,2},{3,35},{35,3},{4,36},{36... | collective-permute-start | bytes 3145736 | tf_op jit(solution)/shard_map/ppermute | solution.py:28
  59.4 3.7 %copy-start.1 = (bf16[2048,1024]{1,0:T(8,128)(2,1)S(1)}, bf16[2048,1024]{1,0:T(8,128)(2,1)}, u32[]{:S(2)}) copy-start(bf16[2048,1024]{1,0:T(8,128)(2,1)} %param.4) | copy-start | bytes 12582916
  65.7 16.2 %collective-permute-start.2 = (f16[512,512]{1,0:T(8,128)(2,1)S(1)}, f16[512,512]{1,0:T(8,128)(2,1)S(1)}, u32[]{:S(2)}, u32[]{:S(2)}) collective-permute-start(f16[512,512]{1,0:T(8,128)(2,1)S(1)} %get-tuple-element.14), channel_id=1, source_target_pairs={{0,4},{4,0},{8,12},{12,8},{16,20},{20,16},{24,28},{28,24},{1,5},{5... | collective-permute-start | bytes 1572872 | tf_op jit(solution)/shard_map/ppermute | solution.py:38
  69.7 20.8 %collective-permute-start.3 = (f16[512,512]{1,0:T(8,128)(2,1)S(1)}, f16[512,512]{1,0:T(8,128)(2,1)S(1)}, u32[]{:S(2)}, u32[]{:S(2)}) collective-permute-start(f16[512,512]{1,0:T(8,128)(2,1)S(1)} %get-tuple-element.15), channel_id=1, source_target_pairs={{0,28},{4,8},{8,4},{12,16},{16,12},{20,24},{24,20},{28,0},{1,29},{... | collective-permute-start | bytes 1572872 | tf_op jit(solution)/shard_map/ppermute | solution.py:39
  91.9 33.2 %all-to-all-start.2 = ((f16[16,32,1024]{2,1,0:T(8,128)(2,1)}), f16[16,32,1024]{2,1,0:T(8,128)(2,1)S(1)}, u32[]{:S(2)}, u32[]{:S(2)}) async-start(f16[16,32,1024]{2,1,0:T(8,128)(2,1)} %bitcast.11), calls=%async_computation.2 | async-start | bytes 2097152 | tf_op jit(solution)/shard_map/all_to_all | solution.py:42
  97.7 27.8 %copy-start = (s32[32]{0:T(128)S(1)}, s32[32]{0:T(128)}, u32[]{:S(2)}) copy-start(s32[32]{0:T(128)} %param.5) | copy-start | bytes 388

commit v5 on v4

v5 whole, which is shorter than its diff:
```python
import jax
import jax.numpy as jnp
from jax import lax
from jax.sharding import Mesh, PartitionSpec as P

F16 = jnp.float16
F32 = jnp.float32
Y = ("yh", "yl")
Z = ("zh", "zl")


def spread(x, axis, size):
    return lax.all_to_all(jnp.broadcast_to(x[None], (size,) + x.shape), axis, split_axis=0, concat_axis=0, tiled=True)


def local(ny, nz, nx, hidden, head_weight, tokens):
    n, k = hidden.shape
    cols = head_weight.shape[1]
    yh, zh = ny // 2, nz // 2
    core, odd, first = lax.axis_index("core"), lax.axis_index("zl"), lax.axis_index(Y + ("core",))
    hidden, tokens, core, odd, first = lax.optimization_barrier((hidden, tokens, core, odd, first * (nx * cols)))
    pairs = [(i, i ^ 1) for i in range(nz)]
    pairs += [(nz + i, nz + ((i + 1) % nz if i % 2 else (i - 1) % nz)) for i in range(nz)]

    mine = spread(spread(hidden, "yh", yh), ("yl", "x"), 2 * nx)
    other = lax.ppermute(mine, "core", [(0, 1), (1, 0)])

    def product(rows):
        part = jnp.dot(rows.reshape(2 * nx * yh * n, k), head_weight, preferred_element_type=F32)
        return part.astype(F16).reshape(2, nx, yh, n, cols)

    both = (product(mine), product(other))

    def parity(which):
        return jnp.stack([lax.dynamic_index_in_dim(p, which, 0, keepdims=False) for p in both])

    taken = lax.ppermute(parity(1 - odd), ("core",) + Z, pairs)
    pair = parity(odd).astype(F32) + taken.astype(F32)
    place = lax.broadcasted_iota(jnp.int32, pair.shape, 0)
    pair = jnp.where(place == core, pair[:1], pair[1:]).astype(F16)
    pair = jnp.transpose(pair, (2, 0, 1, 3, 4)).reshape(zh * nx, 2 * n, cols)
    part = lax.all_to_all(pair, ("zh", "x"), split_axis=0, concat_axis=0, tiled=True)
    logits = jnp.sum(part.reshape(zh, nx, 2 * n, cols).astype(F32), axis=0)
    logits = jnp.swapaxes(logits, 0, 1).reshape(2 * n, nx * cols)

    width = logits.shape[1]
    column = first + lax.broadcasted_iota(jnp.int32, logits.shape, 1)
    peak = jnp.max(logits, axis=1)
    total = jnp.sum(jnp.exp(logits - peak[:, None]), axis=1)
    picked = jnp.sum(jnp.where(column == tokens[:, None], logits, 0.0), axis=1)
    stats, logits = lax.optimization_barrier((jnp.concatenate([peak, total, picked]), logits))
    peaks, totals, picks = jnp.split(spread(stats, Y + ("core",), 2 * ny), 3, axis=1)
    row_peak = jnp.max(peaks, axis=0)
    row_total = jnp.sum(totals * jnp.exp(peaks - row_peak), axis=0)
    shift = jnp.log(row_total)
    logprobs = logits - row_peak[:, None] - shift[:, None]
    target_logp = jnp.sum(picks, axis=0) - row_peak - shift
    return (logprobs, target_logp)


def solution(mesh):
    nv, nz, nx = mesh.devices.shape
    ny = nv // 2
    split = Mesh(mesh.devices.reshape(ny // 2, 2, 2, nz // 2, 2, nx), Y + ("core",) + Z + ("x",))
    in_specs = (P(Y + ("core", "x"), Z), P(Z, Y + ("core", "x")), P(Z + ("x",)))
    out_specs = (P(Z + ("x",), Y + ("core",)), P(Z + ("x",)))

    def body(*args):
        return local(ny, nz, nx, *args)

    return jax.shard_map(body, mesh=split, in_specs=in_specs, out_specs=out_specs, check_vma=False)
```

time: 143 us -> 136 us (0.951)
  the two profiles are of different devices: /device:TPU:1 before, /device:TPU:65 now
where the time goes in v5:
time: 136 us
  blocking collectives  55.8 us (41%)
  waiting for transfers between devices  43 us (32%)
  starting transfers between devices  20.4 us (15%)
  matrix products  8.63 us (6%)
  other arithmetic  4.41 us (3%)
  local copies, waits for them, and re-layouts  2.91 us (2%)
    all_to_all x3, blocking collectives, spread(): lax.all_to_all(jnp.broadcast_to(x[None], (size,) + x.shape), axis, split_...  55.8 us
    all_to_all x1, waiting for transfers between devices, local(): lax.all_to_all(pair, ('zh', 'x'), split_axis=0, concat_axis=0, tiled=True)  30.9 us
    ppermute x1, waiting for transfers between devices, local(): taken = lax.ppermute(parity(1 - odd), ('core',) + Z, pairs)  12.1 us
    all_to_all x1, starting transfers between devices, local(): lax.all_to_all(pair, ('zh', 'x'), split_axis=0, concat_axis=0, tiled=True)  10 us
    dot_general x2, matrix products, product(): jnp.dot(rows.reshape(2 * nx * yh * n, k), head_weight, preferred_element_...  8.63 us
    ppermute x1, starting transfers between devices, local(): other = lax.ppermute(mine, 'core', [(0, 1), (1, 0)])  6.39 us
    ppermute x1, starting transfers between devices, local(): taken = lax.ppermute(parity(1 - odd), ('core',) + Z, pairs)  4 us
  transfers between devices with their start and end apart: 3, of which 2 were waited for; matrix products, arithmetic and copies ran while one was open for 4% of the time, Pallas kernels for 0%

profile of v5, /device:TPU:65, one launch (start us, length us, event | category | flops | bytes accessed | tf_op | source)
XLA Modules:
  0.0 136.0 jit_solution(558493180290237721)
XLA Ops:
  0.6 0.9 broadcast_in_dim.55
  1.5 15.3 %all_to_all.24 = bf16[4,16,2048]{2,1,0:T(8,128)(2,1)S(1)} all-to-all(bf16[4,16,2048]{2,1,0:T(8,128)(2,1)S(1)} %broadcast_in_dim.55), channel_id=1, replica_groups=mesh['yh'=4,'yl'=2,'core'=2,'zh'=4,'zl'=2,'x'=4] {'yh'}, dimensions={0} | all-to-all | bytes 524288 | tf_op jit(solution)/shard_map/all_to_all | solution.py:13
  16.8 0.2 broadcast_in_dim.56
  17.0 27.8 %all_to_all.25 = bf16[8,4,16,2048]{3,2,1,0:T(8,128)(2,1)S(1)} all-to-all(bf16[8,4,16,2048]{3,2,1,0:T(8,128)(2,1)S(1)} %broadcast_in_dim.56), channel_id=1, replica_groups=mesh['yh'=4,'yl'=2,'core'=2,'zh'=4,'zl'=2,'x'=4] {'yl','x'}, dimensions={0} | all-to-all | bytes 4194304 | tf_op jit(solution)/shard_map/all_to_all | solution.py:13
  44.8 6.4 %collective-permute-start = (bf16[8,4,16,2048]{3,2,1,0:T(8,128)(2,1)S(1)}, bf16[8,4,16,2048]{3,2,1,0:T(8,128)(2,1)}, u32[]{:S(2)}, u32[]{:S(2)}) collective-permute-start(bf16[8,4,16,2048]{3,2,1,0:T(8,128)(2,1)S(1)} %all_to_all.25), channel_id=1, source_target_pairs={{0,32},{32,0},{1,33},{33,1},{2,34},{34,2},{3,35},{35,3},{4,36},{36... | collective-permute-start | bytes 6291464 | tf_op jit(solution)/shard_map/ppermute | solution.py:26
  51.2 4.7 %convolution_convert_fusion.1 = f16[512,1024]{1,0:T(8,128)(2,1)S(1)} fusion(bf16[512,2048]{1,0:T(8,128)(2,1)S(1)} %bitcast.37, bf16[2048,1024]{1,0:T(8,128)(2,1)} %param.4), kind=kOutput, calls=%fused_computation.4 | convolution fusion | flops 2148007936 | bytes 7340032 | tf_op jit(solution)/shard_map/dot_general | solution.py:29
  55.9 4.0 %convolution_convert_fusion = f16[512,1024]{1,0:T(8,128)(2,1)S(1)} fusion(bf16[512,2048]{1,0:T(8,128)(2,1)} %bitcast.2, bf16[2048,1024]{1,0:T(8,128)(2,1)S(1)} %copy-done.1), kind=kOutput, calls=%fused_computation.3 | convolution fusion | flops 2148007936 | bytes 7340032 | tf_op jit(solution)/shard_map/dot_general | solution.py:29
  59.9 0.6 constant_dynamic-slice_fusion.2
  60.5 0.3 pad_maximum_fusion
  60.8 4.0 %collective-permute-start.1 = (f16[2,4,4,16,1024]{4,3,2,1,0:T(8,128)(2,1)S(1)}, f16[2,4,4,16,1024]{4,3,2,1,0:T(8,128)(2,1)S(1)}, u32[]{:S(2)}, u32[]{:S(2)}) collective-permute-start(f16[2,4,4,16,1024]{4,3,2,1,0:T(8,128)(2,1)S(1)} %pad_maximum_fusion), channel_id=1, source_target_pairs={{0,4},{4,0},{8,12},{12,8},{16,20},{20,16},{24,28},{28,24},{32,60},... | collective-permute-start | bytes 3145736 | tf_op jit(solution)/shard_map/ppermute | solution.py:37
  65.0 12.1 %collective-permute-done.1 = f16[2,4,4,16,1024]{4,3,2,1,0:T(8,128)(2,1)S(1)} collective-permute-done((f16[2,4,4,16,1024]{4,3,2,1,0:T(8,128)(2,1)S(1)}, f16[2,4,4,16,1024]{4,3,2,1,0:T(8,128)(2,1)S(1)}, u32[]{:S(2)}, u32[]{:S(2)}) %collective-permute-start.1) | collective-permute-done | bytes 1048608 | tf_op jit(solution)/shard_map/ppermute | solution.py:37
  77.1 0.5 convert_add_fusion
  77.6 0.2 slice_bitcast_fusion
  78.1 0.2 broadcast_in_dim.59
  78.3 0.3 broadcast_in_dim.63
  78.6 1.2 select_convert_fusion
  79.9 10.0 %all-to-all-start.2 = ((f16[16,32,1024]{2,1,0:T(8,128)(2,1)}), f16[16,32,1024]{2,1,0:T(8,128)(2,1)S(1)}, u32[]{:S(2)}, u32[]{:S(2)}) async-start(f16[16,32,1024]{2,1,0:T(8,128)(2,1)} %select_convert_fusion), calls=%async_computation.2 | async-start | bytes 2097152 | tf_op jit(solution)/shard_map/all_to_all | solution.py:42
  89.9 30.9 %all-to-all-done.2 = f16[16,32,1024]{2,1,0:T(8,128)(2,1)S(1)} async-done(((f16[16,32,1024]{2,1,0:T(8,128)(2,1)}), f16[16,32,1024]{2,1,0:T(8,128)(2,1)S(1)}, u32[]{:S(2)}, u32[]{:S(2)}) %all-to-all-start.2) | async-done | bytes 1048608 | tf_op jit(solution)/shard_map/all_to_all | solution.py:42
  120.8 0.3 convert_reduce_fusion
  121.1 0.1 reduce_max.18
  121.3 0.3 fusion.1
  121.7 12.7 %all_to_all.26 = f32[16,1,96]{2,1,0:T(1,128)S(1)} all-to-all(f32[16,1,96]{2,1,0:T(1,128)S(1)} %broadcast_in_dim.66), channel_id=1, replica_groups=mesh['yh'=4,'yl'=2,'core'=2,'zh'=4,'zl'=2,'x'=4] {'yh','yl','core'}, dimensions={0} | all-to-all | bytes 12288 | tf_op jit(solution)/shard_map/all_to_all | solution.py:13
  134.5 0.5 subtract_subtract_fusion.1
  135.1 0.9 subtract_subtract_fusion
  (16 shorter events, 0.6 us)
Async XLA Ops:
  44.8 11.1 %collective-permute-start = (bf16[8,4,16,2048]{3,2,1,0:T(8,128)(2,1)S(1)}, bf16[8,4,16,2048]{3,2,1,0:T(8,128)(2,1)}, u32[]{:S(2)}, u32[]{:S(2)}) collective-permute-start(bf16[8,4,16,2048]{3,2,1,0:T(8,128)(2,1)S(1)} %all_to_all.25), channel_id=1, source_target_pairs={{0,32},{32,0},{1,33},{33,1},{2,34},{34,2},{3,35},{35,3},{4,36},{36... | collective-permute-start | bytes 6291464 | tf_op jit(solution)/shard_map/ppermute | solution.py:26
  51.2 4.7 %copy-start.1 = (bf16[2048,1024]{1,0:T(8,128)(2,1)S(1)}, bf16[2048,1024]{1,0:T(8,128)(2,1)}, u32[]{:S(2)}) copy-start(bf16[2048,1024]{1,0:T(8,128)(2,1)} %param.4) | copy-start | bytes 12582916
  60.8 16.3 %collective-permute-start.1 = (f16[2,4,4,16,1024]{4,3,2,1,0:T(8,128)(2,1)S(1)}, f16[2,4,4,16,1024]{4,3,2,1,0:T(8,128)(2,1)S(1)}, u32[]{:S(2)}, u32[]{:S(2)}) collective-permute-start(f16[2,4,4,16,1024]{4,3,2,1,0:T(8,128)(2,1)S(1)} %pad_maximum_fusion), channel_id=1, source_target_pairs={{0,4},{4,0},{8,12},{12,8},{16,20},{20,16},{24,28},{28,24},{32,60},... | collective-permute-start | bytes 3145736 | tf_op jit(solution)/shard_map/ppermute | solution.py:37
  79.9 40.9 %all-to-all-start.2 = ((f16[16,32,1024]{2,1,0:T(8,128)(2,1)}), f16[16,32,1024]{2,1,0:T(8,128)(2,1)S(1)}, u32[]{:S(2)}, u32[]{:S(2)}) async-start(f16[16,32,1024]{2,1,0:T(8,128)(2,1)} %select_convert_fusion), calls=%async_computation.2 | async-start | bytes 2097152 | tf_op jit(solution)/shard_map/all_to_all | solution.py:42
  89.9 31.4 %copy-start = (s32[32]{0:T(128)S(1)}, s32[32]{0:T(128)}, u32[]{:S(2)}) copy-start(s32[32]{0:T(128)} %param.5) | copy-start | bytes 388

commit v6 on v5

v6 whole, which is shorter than its diff:
```python
import jax
import jax.numpy as jnp
from jax import lax
from jax.sharding import Mesh, PartitionSpec as P

F16 = jnp.float16
F32 = jnp.float32
Y = ("yh", "yl")
Z = ("zh", "zl")


def spread(x, axis, size):
    return lax.all_to_all(jnp.broadcast_to(x[None], (size,) + x.shape), axis, split_axis=0, concat_axis=0, tiled=True)


def local(ny, nz, nx, hidden, head_weight, tokens):
    n, k = hidden.shape
    cols = head_weight.shape[1]
    yh, zh = ny // 2, nz // 2
    core, odd, block = lax.axis_index("core"), lax.axis_index("zl"), lax.axis_index(Y + ("core",))
    pairs = [(i, i ^ 1) for i in range(nz)]
    pairs += [(nz + i, nz + ((i + 1) % nz if i % 2 else (i - 1) % nz)) for i in range(nz)]
    token = tokens - block * (nx * cols)
    hidden, token, core, odd = lax.optimization_barrier((hidden, token, core, odd))

    mine = spread(spread(hidden, "yh", yh), ("yl", "x"), 2 * nx).reshape(2, nx, yh, n, k)
    mine = jnp.swapaxes(mine, 1, 2)
    other = lax.ppermute(mine, "core", [(0, 1), (1, 0)])

    def product(rows):
        part = jnp.dot(rows.reshape(2 * nx * yh * n, k), head_weight, preferred_element_type=F32)
        return part.astype(F16).reshape(2, yh, nx, n, cols)

    own, far = product(mine), product(other)

    def parity(which):
        a, b = (lax.dynamic_index_in_dim(p, which, 0, keepdims=True) for p in (own, far))
        place = lax.broadcasted_iota(jnp.int32, (2,) + a.shape[1:], 0)
        return jnp.where(place == core, a, b)

    taken = lax.ppermute(parity(1 - odd), ("core",) + Z, pairs)
    pair = (parity(odd).astype(F32) + taken.astype(F32)).astype(F16)
    pair = jnp.swapaxes(pair, 0, 1).reshape(zh * nx, 2 * n, cols)
    part = lax.all_to_all(pair, ("zh", "x"), split_axis=0, concat_axis=0, tiled=True)
    logits = jnp.sum(part.reshape(zh, nx, 2 * n, cols).astype(F32), axis=0)

    column = lax.broadcasted_iota(jnp.int32, logits.shape, 0) * cols + lax.broadcasted_iota(jnp.int32, logits.shape, 2)
    peak = jnp.max(logits, axis=(0, 2))
    total = jnp.sum(jnp.exp(logits - peak[:, None]), axis=(0, 2))
    picked = jnp.sum(jnp.where(column == token[:, None], logits, 0.0), axis=(0, 2))
    logits = jnp.swapaxes(logits, 0, 1).reshape(2 * n, nx * cols)
    stats, logits = lax.optimization_barrier((jnp.concatenate([peak, total, picked]), logits))
    peaks, totals, picks = jnp.split(spread(stats, Y + ("core",), 2 * ny), 3, axis=1)
    row_peak = jnp.max(peaks, axis=0)
    row_total = jnp.sum(totals * jnp.exp(peaks - row_peak), axis=0)
    shift = jnp.log(row_total)
    logprobs = logits - row_peak[:, None] - shift[:, None]
    target_logp = jnp.sum(picks, axis=0) - row_peak - shift
    return (logprobs, target_logp)


def solution(mesh):
    nv, nz, nx = mesh.devices.shape
    ny = nv // 2
    split = Mesh(mesh.devices.reshape(ny // 2, 2, 2, nz // 2, 2, nx), Y + ("core",) + Z + ("x",))
    in_specs = (P(Y + ("core", "x"), Z), P(Z, Y + ("core", "x")), P(Z + ("x",)))
    out_specs = (P(Z + ("x",), Y + ("core",)), P(Z + ("x",)))

    def body(*args):
        return local(ny, nz, nx, *args)

    return jax.shard_map(body, mesh=split, in_specs=in_specs, out_specs=out_specs, check_vma=False)
```

time: 136 us -> 136 us (level)
  matrix products: 8.63 us -> 4.75 us
  local copies, waits for them, and re-layouts: 2.91 us -> 5.65 us
    dot_general x2, matrix products: 8.63 us -> 4.75 us  [product(): jnp.dot(rows.reshape(2 * nx * yh * n, k), head_weight, preferred_element_...]
    unnamed x4 -> x2, local copies, waits for them, and re-layouts: 0.01 us -> 2.04 us
    ppermute x0 -> x1, local copies, waits for them, and re-layouts: none -> 1.73 us  [local(): other = lax.ppermute(mine, 'core', [(0, 1), (1, 0)])]
  transfers between devices with their start and end apart: 3 -> 3, of which waited for: 2 -> 2; matrix products, arithmetic and copies ran while one was open for 4% -> 2% of each run, Pallas kernels for 0% -> 0%
where the time goes in v6:
time: 136 us
  blocking collectives  55.8 us (41%)
  waiting for transfers between devices  43.2 us (32%)
  starting transfers between devices  20.4 us (15%)
  local copies, waits for them, and re-layouts  5.65 us (4%)
  other arithmetic  5.07 us (4%)
  matrix products  4.75 us (3%)
    all_to_all x3, blocking collectives, spread(): lax.all_to_all(jnp.broadcast_to(x[None], (size,) + x.shape), axis, split_...  55.8 us
    all_to_all x1, waiting for transfers between devices, local(): lax.all_to_all(pair, ('zh', 'x'), split_axis=0, concat_axis=0, tiled=True)  30.9 us
    ppermute x1, waiting for transfers between devices, local(): taken = lax.ppermute(parity(1 - odd), ('core',) + Z, pairs)  12.3 us
    all_to_all x1, starting transfers between devices, local(): lax.all_to_all(pair, ('zh', 'x'), split_axis=0, concat_axis=0, tiled=True)  10 us
    ppermute x1, starting transfers between devices, local(): other = lax.ppermute(mine, 'core', [(0, 1), (1, 0)])  6.39 us
    dot_general x2, matrix products, product(): jnp.dot(rows.reshape(2 * nx * yh * n, k), head_weight, preferred_element_...  4.75 us
    ppermute x1, starting transfers between devices, local(): taken = lax.ppermute(parity(1 - odd), ('core',) + Z, pairs)  4 us
  transfers between devices with their start and end apart: 3, of which 2 were waited for; matrix products, arithmetic and copies ran while one was open for 2% of the time, Pallas kernels for 0%

profile of v6, /device:TPU:65, one launch (start us, length us, event | category | flops | bytes accessed | tf_op | source)
XLA Modules:
  0.0 135.6 jit_solution(15265272759314256525)
XLA Ops:
  0.6 0.7 broadcast_subtract_fusion
  1.3 0.9 broadcast_in_dim.59
  2.2 15.3 %all_to_all.24 = bf16[4,16,2048]{2,1,0:T(8,128)(2,1)S(1)} all-to-all(bf16[4,16,2048]{2,1,0:T(8,128)(2,1)S(1)} %broadcast_in_dim.59), channel_id=1, replica_groups=mesh['yh'=4,'yl'=2,'core'=2,'zh'=4,'zl'=2,'x'=4] {'yh'}, dimensions={0} | all-to-all | bytes 524288 | tf_op jit(solution)/shard_map/all_to_all | solution.py:13
  17.4 0.2 broadcast_in_dim.60
  17.7 27.8 %all_to_all.25 = bf16[8,4,16,2048]{3,2,1,0:T(8,128)(2,1)S(1)} all-to-all(bf16[8,4,16,2048]{3,2,1,0:T(8,128)(2,1)S(1)} %broadcast_in_dim.60), channel_id=1, replica_groups=mesh['yh'=4,'yl'=2,'core'=2,'zh'=4,'zl'=2,'x'=4] {'yl','x'}, dimensions={0} | all-to-all | bytes 4194304 | tf_op jit(solution)/shard_map/all_to_all | solution.py:13
  45.5 6.4 %collective-permute-start = (bf16[2,4,4,16,2048]{4,3,1,2,0:T(8,128)(2,1)S(1)}, bf16[2,4,4,16,2048]{4,3,1,2,0:T(8,128)(2,1)}, u32[]{:S(2)}, u32[]{:S(2)}) collective-permute-start(bf16[2,4,4,16,2048]{4,3,1,2,0:T(8,128)(2,1)S(1)} %bitcast.29), channel_id=1, source_target_pairs={{0,32},{32,0},{1,33},{33,1},{2,34},{34,2},{3,35},{35,3},{4,36},{36... | collective-permute-start | bytes 6291464 | tf_op jit(solution)/shard_map/ppermute | solution.py:28
  51.9 0.1 copy.15
  52.0 2.0 %copy-done = bf16[2048,1024]{1,0:T(8,128)(2,1)S(1)} copy-done((bf16[2048,1024]{1,0:T(8,128)(2,1)S(1)}, bf16[2048,1024]{1,0:T(8,128)(2,1)}, u32[]{:S(2)}) %copy-start) | copy-done | bytes 4194328
  54.1 2.4 %convolution_convert_fusion.1 = f16[512,1024]{1,0:T(8,128)(2,1)S(1)} fusion(bf16[512,2048]{1,0:T(8,128)(2,1)S(1)} %bitcast.34, bf16[2048,1024]{1,0:T(8,128)(2,1)S(1)} %copy-done), kind=kOutput, calls=%fused_computation.3 | convolution fusion | flops 2148007936 | bytes 7340032 | tf_op jit(solution)/shard_map/dot_general | solution.py:31
  56.5 1.7 %copy.16 = bf16[2,4,4,16,2048]{4,3,2,1,0:T(8,128)(2,1)S(1)} copy(bf16[2,4,4,16,2048]{4,3,1,2,0:T(8,128)(2,1)} %collective-permute-done) | data formatting | bytes 4194304 | tf_op jit(solution)/shard_map/ppermute | solution.py:28
  58.2 2.4 %convolution_convert_fusion = f16[512,1024]{1,0:T(8,128)(2,1)S(1)} fusion(bf16[512,2048]{1,0:T(8,128)(2,1)S(1)} %bitcast.33, bf16[2048,1024]{1,0:T(8,128)(2,1)S(1)} %copy-done), kind=kOutput, calls=%fused_computation.2 | convolution fusion | flops 2148007936 | bytes 7340032 | tf_op jit(solution)/shard_map/dot_general | solution.py:31
  60.6 0.6 dynamic-slice_bitcast_fusion.2
  61.2 0.4 broadcast_select_fusion
  61.6 4.0 %collective-permute-start.1 = (f16[2,4,4,16,1024]{4,3,2,0,1:T(8,128)(2,1)S(1)}, f16[2,4,4,16,1024]{4,3,2,0,1:T(8,128)(2,1)S(1)}, u32[]{:S(2)}, u32[]{:S(2)}) collective-permute-start(f16[2,4,4,16,1024]{4,3,2,0,1:T(8,128)(2,1)S(1)} %broadcast_select_fusion), channel_id=1, source_target_pairs={{0,4},{4,0},{8,12},{12,8},{16,20},{20,16},{24,28},{28,24},{32,60},... | collective-permute-start | bytes 3145736 | tf_op jit(solution)/shard_map/ppermute | solution.py:41
  65.6 12.3 %collective-permute-done.1 = f16[2,4,4,16,1024]{4,3,2,0,1:T(8,128)(2,1)S(1)} collective-permute-done((f16[2,4,4,16,1024]{4,3,2,0,1:T(8,128)(2,1)S(1)}, f16[2,4,4,16,1024]{4,3,2,0,1:T(8,128)(2,1)S(1)}, u32[]{:S(2)}, u32[]{:S(2)}) %collective-permute-start.1) | collective-permute-done | bytes 1048608 | tf_op jit(solution)/shard_map/ppermute | solution.py:41
  77.9 1.7 %add_convert_fusion = f16[2,4,4,16,1024]{4,3,2,0,1:T(8,128)(2,1)} fusion(f16[2,4,4,16,1024]{4,3,2,0,1:T(8,128)(2,1)S(1)} %collective-permute-done.1, pred[2]{0:T(512)(128)(4,1)S(1)} %iota_compare_fusion, f16[4,4,16,1024]{3,2,1,0:T(8,128)(2,1)S(1)} %get-tuple-element.20, f16[4,4,16,1024]{3,2,1,0:T(8,128)(2,1)S(1)} %get-tuple-element.25), kind=kLoop, calls=%fused_computation.1 | loop fusion | flops 2621440 | bytes 3145730 | tf_op jit(solution)/shard_map/convert_element_type | solution.py:42
  79.6 10.0 %all-to-all-start.2 = ((f16[16,32,1024]{2,1,0:T(8,128)(2,1)}), f16[16,32,1024]{2,1,0:T(8,128)(2,1)S(1)}, u32[]{:S(2)}, u32[]{:S(2)}) async-start(f16[16,32,1024]{2,1,0:T(8,128)(2,1)} %bitcast.12), calls=%async_computation.2 | async-start | bytes 2097152 | tf_op jit(solution)/shard_map/all_to_all | solution.py:44
  89.6 30.9 %all-to-all-done.2 = f16[16,32,1024]{2,1,0:T(8,128)(2,1)S(1)} async-done(((f16[16,32,1024]{2,1,0:T(8,128)(2,1)}), f16[16,32,1024]{2,1,0:T(8,128)(2,1)S(1)}, u32[]{:S(2)}, u32[]{:S(2)}) %all-to-all-start.2) | async-done | bytes 1048608 | tf_op jit(solution)/shard_map/all_to_all | solution.py:44
  120.5 0.2 convert_reduce_fusion
  120.8 0.1 reduce_max.18
  121.0 0.3 exponential_reduce_fusion
  121.4 12.7 %all_to_all.26 = f32[16,1,96]{2,1,0:T(1,128)S(1)} all-to-all(f32[16,1,96]{2,1,0:T(1,128)S(1)} %broadcast_in_dim.70), channel_id=1, replica_groups=mesh['yh'=4,'yl'=2,'core'=2,'zh'=4,'zl'=2,'x'=4] {'yh','yl','core'}, dimensions={0} | all-to-all | bytes 12288 | tf_op jit(solution)/shard_map/all_to_all | solution.py:13
  134.2 0.5 subtract_subtract_fusion.1
  134.7 0.9 subtract_subtract_fusion
  (9 shorter events, 0.3 us)
Async XLA Ops:
  45.5 11.0 %collective-permute-start = (bf16[2,4,4,16,2048]{4,3,1,2,0:T(8,128)(2,1)S(1)}, bf16[2,4,4,16,2048]{4,3,1,2,0:T(8,128)(2,1)}, u32[]{:S(2)}, u32[]{:S(2)}) collective-permute-start(bf16[2,4,4,16,2048]{4,3,1,2,0:T(8,128)(2,1)S(1)} %bitcast.29), channel_id=1, source_target_pairs={{0,32},{32,0},{1,33},{33,1},{2,34},{34,2},{3,35},{35,3},{4,36},{36... | collective-permute-start | bytes 6291464 | tf_op jit(solution)/shard_map/ppermute | solution.py:28
  51.9 2.2 %copy-start = (bf16[2048,1024]{1,0:T(8,128)(2,1)S(1)}, bf16[2048,1024]{1,0:T(8,128)(2,1)}, u32[]{:S(2)}) copy-start(bf16[2048,1024]{1,0:T(8,128)(2,1)} %param.4) | copy-start | bytes 12582916
  61.6 16.3 %collective-permute-start.1 = (f16[2,4,4,16,1024]{4,3,2,0,1:T(8,128)(2,1)S(1)}, f16[2,4,4,16,1024]{4,3,2,0,1:T(8,128)(2,1)S(1)}, u32[]{:S(2)}, u32[]{:S(2)}) collective-permute-start(f16[2,4,4,16,1024]{4,3,2,0,1:T(8,128)(2,1)S(1)} %broadcast_select_fusion), channel_id=1, source_target_pairs={{0,4},{4,0},{8,12},{12,8},{16,20},{20,16},{24,28},{28,24},{32,60},... | collective-permute-start | bytes 3145736 | tf_op jit(solution)/shard_map/ppermute | solution.py:41
  79.6 40.9 %all-to-all-start.2 = ((f16[16,32,1024]{2,1,0:T(8,128)(2,1)}), f16[16,32,1024]{2,1,0:T(8,128)(2,1)S(1)}, u32[]{:S(2)}, u32[]{:S(2)}) async-start(f16[16,32,1024]{2,1,0:T(8,128)(2,1)} %bitcast.12), calls=%async_computation.2 | async-start | bytes 2097152 | tf_op jit(solution)/shard_map/all_to_all | solution.py:44

commit v7 on v6

v7 whole, which is shorter than its diff:
```python
import jax
import jax.numpy as jnp
from jax import lax
from jax.sharding import Mesh, PartitionSpec as P

F16 = jnp.float16
F32 = jnp.float32
Y = ("yh", "yl")
Z = ("zh", "zl")


def spread(x, axis, size):
    return lax.all_to_all(jnp.broadcast_to(x[None], (size,) + x.shape), axis, split_axis=0, concat_axis=0, tiled=True)


def local(ny, nz, nx, hidden, head_weight, tokens):
    n, k = hidden.shape
    cols = head_weight.shape[1]
    yh, zh = ny // 2, nz // 2
    core, odd, block = lax.axis_index("core"), lax.axis_index("zl"), lax.axis_index(Y + ("core",))
    pairs = [(i, i ^ 1) for i in range(nz)]
    pairs += [(nz + i, nz + ((i + 1) % nz if i % 2 else (i - 1) % nz)) for i in range(nz)]
    token = tokens - block * (nx * cols)
    hidden, token, core, odd = lax.optimization_barrier((hidden, token, core, odd))
    m, xh = n // 2, nx // 2

    def parity(own, far, which):
        a, b = (lax.dynamic_index_in_dim(p, which, 0, keepdims=True) for p in (own, far))
        place = lax.broadcasted_iota(jnp.int32, (2,) + a.shape[1:], 0)
        return jnp.where(place == core, a, b)

    def product(rows):
        part = jnp.dot(rows, head_weight, preferred_element_type=F32)
        return part.astype(F16).reshape(2, xh * yh, 2 * m, cols)

    def given(mine):
        mine = mine.reshape(xh, 2, 2, yh, m, k)
        mine = jnp.transpose(mine, (2, 0, 3, 1, 4, 5)).reshape(2 * nx * yh * m, k)
        mine = lax.optimization_barrier(mine)
        other = lax.ppermute(mine, "core", [(0, 1), (1, 0)])
        own, far = product(mine), product(other)
        return own, far, parity(own, far, 1 - odd)

    def paired(own, far, taken):
        return (parity(own, far, odd).astype(F32) + taken.astype(F32)).astype(F16)

    def summed(pair):
        part = lax.all_to_all(pair.reshape(nx * zh, 2 * m, cols), ("x", "zh"), split_axis=0, concat_axis=0, tiled=True)
        return jnp.sum(part.reshape(nx, zh, 2 * m, cols).astype(F32), axis=1)

    def local_stats(logits, token):
        column = lax.broadcasted_iota(jnp.int32, logits.shape, 0) * cols + lax.broadcasted_iota(jnp.int32, logits.shape, 2)
        peak = jnp.max(logits, axis=(0, 2))
        total = jnp.sum(jnp.exp(logits - peak[:, None]), axis=(0, 2))
        picked = jnp.sum(jnp.where(column == token[:, None], logits, 0.0), axis=(0, 2))
        return peak, total, picked

    near = spread(hidden, "yh", yh)
    gathered = [spread(near[:, h * m:(h + 1) * m], ("x", "yl"), 2 * nx) for h in range(2)]
    own, far, give = given(gathered[0])
    taken = lax.ppermute(give, ("core",) + Z, pairs)
    _, rows = lax.optimization_barrier((taken, gathered[1]))
    early = paired(own, far, taken)
    own, far, give = given(rows)
    give, _ = lax.optimization_barrier((give, early))
    taken = lax.ppermute(give, ("core",) + Z, pairs)
    logits = [summed(early), summed(paired(own, far, taken))]
    halves = [local_stats(v, token.reshape(2, 2, m)[:, h].reshape(2 * m)) for h, v in enumerate(logits)]
    stats = jnp.concatenate([jnp.concatenate(s) for s in zip(*halves)])
    stats, logits = lax.optimization_barrier((stats, logits))
    peaks, totals, picks = jnp.split(spread(stats, Y + ("core",), 2 * ny), 3, axis=1)
    row_peak = jnp.max(peaks, axis=0)
    row_total = jnp.sum(totals * jnp.exp(peaks - row_peak), axis=0)
    shift = jnp.log(row_total)
    target_logp = jnp.sum(picks, axis=0) - row_peak - shift
    target_logp = jnp.swapaxes(target_logp.reshape(2, 2, m), 0, 1).reshape(2 * n)
    outs = []
    for h, v in enumerate(logits):
        rows = slice(h * 2 * m, (h + 1) * 2 * m)
        v = v - row_peak[rows][:, None] - shift[rows][:, None]
        outs.append(jnp.swapaxes(v, 0, 1).reshape(2, m, nx * cols))
    logprobs = jnp.stack(outs, axis=1).reshape(2 * n, nx * cols)
    return (logprobs, target_logp)


def solution(mesh):
    nv, nz, nx = mesh.devices.shape
    ny = nv // 2
    split = Mesh(mesh.devices.reshape(ny // 2, 2, 2, nz // 2, 2, nx), Y + ("core",) + Z + ("x",))
    in_specs = (P(Y + ("core", "x"), Z), P(Z, Y + ("core", "x")), P(Z + ("x",)))
    out_specs = (P(Z + ("x",), Y + ("core",)), P(Z + ("x",)))

    def body(*args):
        return local(ny, nz, nx, *args)

    return jax.shard_map(body, mesh=split, in_specs=in_specs, out_specs=out_specs, check_vma=False)
```

time: 136 us -> 144 us (1.059)
  the two profiles are of different devices: /device:TPU:65 before, /device:TPU:1 now
where the time goes in v7:
time: 144 us; the launch traced here: 143 us
  blocking collectives  48.3 us (34%)
  starting transfers between devices  40 us (28%)
  waiting for transfers between devices  33.9 us (24%)
  matrix products  9.8 us (7%)
  local copies, waits for them, and re-layouts  5.48 us (4%)
  other arithmetic  4.57 us (3%)
    all_to_all x3, blocking collectives, spread(): lax.all_to_all(jnp.broadcast_to(x[None], (size,) + x.shape), axis, split_...  48.3 us
    ppermute x2, waiting for transfers between devices, local(): taken = lax.ppermute(give, ('core',) + Z, pairs)  17.2 us
    all_to_all x2, waiting for transfers between devices, summed(): lax.all_to_all(pair.reshape(nx * zh, 2 * m, cols), ('x', 'zh'), split_axi...  16.8 us
    ppermute x2, starting transfers between devices, local(): taken = lax.ppermute(give, ('core',) + Z, pairs)  16.1 us
    all_to_all x2, starting transfers between devices, summed(): lax.all_to_all(pair.reshape(nx * zh, 2 * m, cols), ('x', 'zh'), split_axi...  12.7 us
    dot_general x4, matrix products, product(): part = jnp.dot(rows, head_weight, preferred_element_type=F32)  9.8 us
    ppermute x2, starting transfers between devices, given(): other = lax.ppermute(mine, 'core', [(0, 1), (1, 0)])  7.67 us
    all_to_all x1, starting transfers between devices, spread(): lax.all_to_all(jnp.broadcast_to(x[None], (size,) + x.shape), axis, split_...  3.56 us
  transfers between devices with their start and end apart: 7, of which 3 were waited for; matrix products, arithmetic and copies ran while one was open for 10% of the time, Pallas kernels for 0%

profile of v7, /device:TPU:1, one launch (start us, length us, event | category | flops | bytes accessed | tf_op | source)
XLA Modules:
  0.0 143.0 jit_solution(13960640928335530536)
XLA Ops:
  0.6 0.7 broadcast_subtract_fusion
  1.3 0.9 broadcast_in_dim.92
  2.2 16.4 %all_to_all.34 = bf16[4,16,2048]{2,1,0:T(8,128)(2,1)S(1)} all-to-all(bf16[4,16,2048]{2,1,0:T(8,128)(2,1)S(1)} %broadcast_in_dim.92), channel_id=1, replica_groups=mesh['yh'=4,'yl'=2,'core'=2,'zh'=4,'zl'=2,'x'=4] {'yh'}, dimensions={0} | all-to-all | bytes 524288 | tf_op jit(solution)/shard_map/all_to_all | solution.py:13
  18.7 16.9 %all_to_all.35 = bf16[8,4,8,2048]{3,2,1,0:T(8,128)(2,1)S(1)} all-to-all(bf16[8,4,8,2048]{3,2,1,0:T(8,128)(2,1)S(1)} %broadcast_in_dim.93), channel_id=1, replica_groups=mesh['yh'=4,'yl'=2,'core'=2,'zh'=4,'zl'=2,'x'=4] {'x','yl'}, dimensions={0} | all-to-all | bytes 2097152 | tf_op jit(solution)/shard_map/all_to_all | solution.py:13
  35.7 5.8 %collective-permute-start = (bf16[256,2048]{1,0:T(8,128)(2,1)S(1)}, bf16[256,2048]{1,0:T(8,128)(2,1)S(1)}, u32[]{:S(2)}, u32[]{:S(2)}) collective-permute-start(bf16[256,2048]{1,0:T(8,128)(2,1)S(1)} %bitcast.53), channel_id=1, source_target_pairs={{0,32},{32,0},{1,33},{33,1},{2,34},{34,2},{3,35},{35,3},{4,36},{36... | collective-permute-start | bytes 3145736 | tf_op jit(solution)/shard_map/ppermute | solution.py:40
  41.5 1.1 broadcast_in_dim.102
  42.6 3.6 %all-to-all-start.3 = ((bf16[8,4,8,2048]{3,2,1,0:T(8,128)(2,1)}), bf16[8,4,8,2048]{3,2,1,0:T(8,128)(2,1)S(1)}, u32[]{:S(2)}, u32[]{:S(2)}) async-start(bf16[8,4,8,2048]{3,2,1,0:T(8,128)(2,1)} %broadcast_in_dim.102), calls=%async_computation.3 | async-start | bytes 2097152 | tf_op jit(solution)/shard_map/all_to_all | solution.py:13
  46.2 3.6 %convolution_convert_fusion.3 = f16[256,1024]{1,0:T(8,128)(2,1)S(1)} fusion(bf16[256,2048]{1,0:T(8,128)(2,1)S(1)} %bitcast.54, bf16[2048,1024]{1,0:T(8,128)(2,1)} %param.4), kind=kOutput, calls=%fused_computation.3 | convolution fusion | flops 1074003968 | bytes 5767168 | tf_op jit(solution)/shard_map/dot_general | solution.py:33
  49.9 1.3 convolution_convert_fusion.2
  51.6 10.7 %collective-permute-start.1 = (f16[2,8,16,1024]{3,2,1,0:T(8,128)(2,1)S(1)}, f16[2,8,16,1024]{3,2,1,0:T(8,128)(2,1)S(1)}, u32[]{:S(2)}, u32[]{:S(2)}) collective-permute-start(f16[2,8,16,1024]{3,2,1,0:T(8,128)(2,1)S(1)} %broadcast_select_fusion.1), channel_id=1, source_target_pairs={{0,4},{4,0},{8,12},{12,8},{16,20},{20,16},{24,28},{28,24},{32,60},... | collective-permute-start | bytes 1572872 | tf_op jit(solution)/shard_map/ppermute | solution.py:61
  62.2 6.5 %collective-permute-done.1 = f16[2,8,16,1024]{3,2,1,0:T(8,128)(2,1)S(1)} collective-permute-done((f16[2,8,16,1024]{3,2,1,0:T(8,128)(2,1)S(1)}, f16[2,8,16,1024]{3,2,1,0:T(8,128)(2,1)S(1)}, u32[]{:S(2)}, u32[]{:S(2)}) %collective-permute-start.1) | collective-permute-done | bytes 524320 | tf_op jit(solution)/shard_map/ppermute | solution.py:61
  68.9 1.9 %collective-permute-start.2 = (bf16[256,2048]{1,0:T(8,128)(2,1)S(1)}, bf16[256,2048]{1,0:T(8,128)(2,1)S(1)}, u32[]{:S(2)}, u32[]{:S(2)}) collective-permute-start(bf16[256,2048]{1,0:T(8,128)(2,1)S(1)} %bitcast.55), channel_id=1, source_target_pairs={{0,32},{32,0},{1,33},{33,1},{2,34},{34,2},{3,35},{35,3},{4,36},{36... | collective-permute-start | bytes 3145736 | tf_op jit(solution)/shard_map/ppermute | solution.py:40
  70.8 1.1 add_convert_fusion.1
  72.0 6.8 %all-to-all-start.2 = ((f16[16,16,1024]{2,1,0:T(8,128)(2,1)}), f16[16,16,1024]{2,1,0:T(8,128)(2,1)S(1)}, u32[]{:S(2)}, u32[]{:S(2)}) async-start(f16[16,16,1024]{2,1,0:T(8,128)(2,1)} %bitcast.9), calls=%async_computation.2 | async-start | bytes 1048576 | tf_op jit(solution)/shard_map/all_to_all | solution.py:48
  78.8 3.6 %convolution_convert_fusion.1 = f16[256,1024]{1,0:T(8,128)(2,1)S(1)} fusion(bf16[256,2048]{1,0:T(8,128)(2,1)S(1)} %bitcast.56, bf16[2048,1024]{1,0:T(8,128)(2,1)} %param.4), kind=kOutput, calls=%fused_computation.1 | convolution fusion | flops 1074003968 | bytes 5767168 | tf_op jit(solution)/shard_map/dot_general | solution.py:33
  82.5 1.3 convolution_convert_fusion
  84.3 5.4 %collective-permute-start.3 = (f16[2,8,16,1024]{3,2,1,0:T(8,128)(2,1)S(1)}, f16[2,8,16,1024]{3,2,1,0:T(8,128)(2,1)S(1)}, u32[]{:S(2)}, u32[]{:S(2)}) collective-permute-start(f16[2,8,16,1024]{3,2,1,0:T(8,128)(2,1)S(1)} %broadcast_select_fusion), channel_id=1, source_target_pairs={{0,4},{4,0},{8,12},{12,8},{16,20},{20,16},{24,28},{28,24},{32,60},... | collective-permute-start | bytes 1572872 | tf_op jit(solution)/shard_map/ppermute | solution.py:66
  89.7 10.6 %collective-permute-done.3 = f16[2,8,16,1024]{3,2,1,0:T(8,128)(2,1)S(1)} collective-permute-done((f16[2,8,16,1024]{3,2,1,0:T(8,128)(2,1)S(1)}, f16[2,8,16,1024]{3,2,1,0:T(8,128)(2,1)S(1)}, u32[]{:S(2)}, u32[]{:S(2)}) %collective-permute-start.3) | collective-permute-done | bytes 524320 | tf_op jit(solution)/shard_map/ppermute | solution.py:66
  100.3 1.1 add_convert_fusion
  101.4 5.9 %all-to-all-start.4 = ((f16[16,16,1024]{2,1,0:T(8,128)(2,1)}), f16[16,16,1024]{2,1,0:T(8,128)(2,1)S(1)}, u32[]{:S(2)}, u32[]{:S(2)}) async-start(f16[16,16,1024]{2,1,0:T(8,128)(2,1)} %bitcast.20), calls=%async_computation.4 | async-start | bytes 1048576 | tf_op jit(solution)/shard_map/all_to_all | solution.py:48
  107.9 16.8 %all-to-all-done.4 = f16[16,16,1024]{2,1,0:T(8,128)(2,1)S(1)} async-done(((f16[16,16,1024]{2,1,0:T(8,128)(2,1)}), f16[16,16,1024]{2,1,0:T(8,128)(2,1)S(1)}, u32[]{:S(2)}, u32[]{:S(2)}) %all-to-all-start.4) | async-done | bytes 524320 | tf_op jit(solution)/shard_map/all_to_all | solution.py:48
  125.3 15.0 %all_to_all.36 = f32[16,1,96]{2,1,0:T(1,128)S(1)} all-to-all(f32[16,1,96]{2,1,0:T(1,128)S(1)} %broadcast_in_dim.112), channel_id=1, replica_groups=mesh['yh'=4,'yl'=2,'core'=2,'zh'=4,'zl'=2,'x'=4] {'yh','yl','core'}, dimensions={0} | all-to-all | bytes 12288 | tf_op jit(solution)/shard_map/all_to_all | solution.py:13
  141.5 0.8 copy.28
  142.4 0.6 reshape.87
  (44 shorter events, 3.7 us)
Async XLA Ops:
  35.7 14.2 %collective-permute-start = (bf16[256,2048]{1,0:T(8,128)(2,1)S(1)}, bf16[256,2048]{1,0:T(8,128)(2,1)S(1)}, u32[]{:S(2)}, u32[]{:S(2)}) collective-permute-start(bf16[256,2048]{1,0:T(8,128)(2,1)S(1)} %bitcast.53), channel_id=1, source_target_pairs={{0,32},{32,0},{1,33},{33,1},{2,34},{34,2},{3,35},{35,3},{4,36},{36... | collective-permute-start | bytes 3145736 | tf_op jit(solution)/shard_map/ppermute | solution.py:40
  42.6 19.6 %all-to-all-start.3 = ((bf16[8,4,8,2048]{3,2,1,0:T(8,128)(2,1)}), bf16[8,4,8,2048]{3,2,1,0:T(8,128)(2,1)S(1)}, u32[]{:S(2)}, u32[]{:S(2)}) async-start(bf16[8,4,8,2048]{3,2,1,0:T(8,128)(2,1)} %broadcast_in_dim.102), calls=%async_computation.3 | async-start | bytes 2097152 | tf_op jit(solution)/shard_map/all_to_all | solution.py:13
  46.2 3.7 %copy-start = (bf16[2048,1024]{1,0:T(8,128)(2,1)S(1)}, bf16[2048,1024]{1,0:T(8,128)(2,1)}, u32[]{:S(2)}) copy-start(bf16[2048,1024]{1,0:T(8,128)(2,1)} %param.4) | copy-start | bytes 12582916
  51.6 17.2 %collective-permute-start.1 = (f16[2,8,16,1024]{3,2,1,0:T(8,128)(2,1)S(1)}, f16[2,8,16,1024]{3,2,1,0:T(8,128)(2,1)S(1)}, u32[]{:S(2)}, u32[]{:S(2)}) collective-permute-start(f16[2,8,16,1024]{3,2,1,0:T(8,128)(2,1)S(1)} %broadcast_select_fusion.1), channel_id=1, source_target_pairs={{0,4},{4,0},{8,12},{12,8},{16,20},{20,16},{24,28},{28,24},{32,60},... | collective-permute-start | bytes 1572872 | tf_op jit(solution)/shard_map/ppermute | solution.py:61
  68.9 13.5 %collective-permute-start.2 = (bf16[256,2048]{1,0:T(8,128)(2,1)S(1)}, bf16[256,2048]{1,0:T(8,128)(2,1)S(1)}, u32[]{:S(2)}, u32[]{:S(2)}) collective-permute-start(bf16[256,2048]{1,0:T(8,128)(2,1)S(1)} %bitcast.55), channel_id=1, source_target_pairs={{0,32},{32,0},{1,33},{33,1},{2,34},{34,2},{3,35},{35,3},{4,36},{36... | collective-permute-start | bytes 3145736 | tf_op jit(solution)/shard_map/ppermute | solution.py:40
  72.0 29.5 %all-to-all-start.2 = ((f16[16,16,1024]{2,1,0:T(8,128)(2,1)}), f16[16,16,1024]{2,1,0:T(8,128)(2,1)S(1)}, u32[]{:S(2)}, u32[]{:S(2)}) async-start(f16[16,16,1024]{2,1,0:T(8,128)(2,1)} %bitcast.9), calls=%async_computation.2 | async-start | bytes 1048576 | tf_op jit(solution)/shard_map/all_to_all | solution.py:48
  78.8 3.6 %copy-start.1 = (bf16[2048,1024]{1,0:T(8,128)(2,1)S(1)}, bf16[2048,1024]{1,0:T(8,128)(2,1)}, u32[]{:S(2)}) copy-start(bf16[2048,1024]{1,0:T(8,128)(2,1)} %param.4) | copy-start | bytes 12582916
  84.3 16.0 %collective-permute-start.3 = (f16[2,8,16,1024]{3,2,1,0:T(8,128)(2,1)S(1)}, f16[2,8,16,1024]{3,2,1,0:T(8,128)(2,1)S(1)}, u32[]{:S(2)}, u32[]{:S(2)}) collective-permute-start(f16[2,8,16,1024]{3,2,1,0:T(8,128)(2,1)S(1)} %broadcast_select_fusion), channel_id=1, source_target_pairs={{0,4},{4,0},{8,12},{12,8},{16,20},{20,16},{24,28},{28,24},{32,60},... | collective-permute-start | bytes 1572872 | tf_op jit(solution)/shard_map/ppermute | solution.py:66
  101.4 23.2 %all-to-all-start.4 = ((f16[16,16,1024]{2,1,0:T(8,128)(2,1)}), f16[16,16,1024]{2,1,0:T(8,128)(2,1)S(1)}, u32[]{:S(2)}, u32[]{:S(2)}) async-start(f16[16,16,1024]{2,1,0:T(8,128)(2,1)} %bitcast.20), calls=%async_computation.4 | async-start | bytes 1048576 | tf_op jit(solution)/shard_map/all_to_all | solution.py:48

commit v8 on v6

--- a/solution.py
+++ b/solution.py
@@ -16,20 +16,20 @@
 def local(ny, nz, nx, hidden, head_weight, tokens):
     n, k = hidden.shape
     cols = head_weight.shape[1]
-    yh, zh = ny // 2, nz // 2
+    yh, zh, xh = ny // 2, nz // 2, nx // 2
     core, odd, block = lax.axis_index("core"), lax.axis_index("zl"), lax.axis_index(Y + ("core",))
     pairs = [(i, i ^ 1) for i in range(nz)]
     pairs += [(nz + i, nz + ((i + 1) % nz if i % 2 else (i - 1) % nz)) for i in range(nz)]
     token = tokens - block * (nx * cols)
     hidden, token, core, odd = lax.optimization_barrier((hidden, token, core, odd))
 
-    mine = spread(spread(hidden, "yh", yh), ("yl", "x"), 2 * nx).reshape(2, nx, yh, n, k)
-    mine = jnp.swapaxes(mine, 1, 2)
+    mine = spread(spread(hidden, "yh", yh), ("x", "yl"), 2 * nx).reshape(xh, 2, 2, yh, n, k)
+    mine = jnp.transpose(mine, (2, 0, 3, 1, 4, 5)).reshape(2 * nx * yh * n, k)
     other = lax.ppermute(mine, "core", [(0, 1), (1, 0)])
 
     def product(rows):
-        part = jnp.dot(rows.reshape(2 * nx * yh * n, k), head_weight, preferred_element_type=F32)
-        return part.astype(F16).reshape(2, yh, nx, n, cols)
+        part = jnp.dot(rows, head_weight, preferred_element_type=F32)
+        return part.astype(F16).reshape(2, xh * zh, 2 * n, cols)
 
     own, far = product(mine), product(other)
 
@@ -40,9 +40,8 @@
 
     taken = lax.ppermute(parity(1 - odd), ("core",) + Z, pairs)
     pair = (parity(odd).astype(F32) + taken.astype(F32)).astype(F16)
-    pair = jnp.swapaxes(pair, 0, 1).reshape(zh * nx, 2 * n, cols)
-    part = lax.all_to_all(pair, ("zh", "x"), split_axis=0, concat_axis=0, tiled=True)
-    logits = jnp.sum(part.reshape(zh, nx, 2 * n, cols).astype(F32), axis=0)
+    part = lax.all_to_all(pair.reshape(nx * zh, 2 * n, cols), ("x", "zh"), split_axis=0, concat_axis=0, tiled=True)
+    logits = jnp.sum(part.reshape(nx, zh, 2 * n, cols).astype(F32), axis=1)
 
     column = lax.broadcasted_iota(jnp.int32, logits.shape, 0) * cols + lax.broadcasted_iota(jnp.int32, logits.shape, 2)
     peak = jnp.max(logits, axis=(0, 2))
@@ -50,7 +49,7 @@
     picked = jnp.sum(jnp.where(column == token[:, None], logits, 0.0), axis=(0, 2))
     logits = jnp.swapaxes(logits, 0, 1).reshape(2 * n, nx * cols)
     stats, logits = lax.optimization_barrier((jnp.concatenate([peak, total, picked]), logits))
-    peaks, totals, picks = jnp.split(spread(stats, Y + ("core",), 2 * ny), 3, axis=1)
+    peaks, totals, picks = jnp.split(spread(stats, ("core", "yl", "yh"), 2 * ny), 3, axis=1)
     row_peak = jnp.max(peaks, axis=0)
     row_total = jnp.sum(totals * jnp.exp(peaks - row_peak), axis=0)
     shift = jnp.log(row_total)

time: 136 us -> 135 us (level)
  the two profiles are of different devices: /device:TPU:65 before, /device:TPU:64 now
where the time goes in v8:
time: 135 us
  blocking collectives  59.3 us (44%)
  waiting for transfers between devices  44.8 us (33%)
  starting transfers between devices  13.9 us (10%)
  matrix products  8.68 us (6%)
  other arithmetic  5.13 us (4%)
  local copies, waits for them, and re-layouts  1.96 us (1%)
    all_to_all x3, blocking collectives, spread(): lax.all_to_all(jnp.broadcast_to(x[None], (size,) + x.shape), axis, split_...  59.3 us
    all_to_all x1, waiting for transfers between devices, local(): lax.all_to_all(pair.reshape(nx * zh, 2 * n, cols), ('x', 'zh'), split_axi...  30.1 us
    ppermute x1, waiting for transfers between devices, local(): taken = lax.ppermute(parity(1 - odd), ('core',) + Z, pairs)  14.8 us
    all_to_all x1, starting transfers between devices, local(): lax.all_to_all(pair.reshape(nx * zh, 2 * n, cols), ('x', 'zh'), split_axi...  10.1 us
    dot_general x2, matrix products, product(): part = jnp.dot(rows, head_weight, preferred_element_type=F32)  8.68 us
  transfers between devices with their start and end apart: 3, of which 2 were waited for; matrix products, arithmetic and copies ran while one was open for 4% of the time, Pallas kernels for 0%

profile of v8, /device:TPU:64, one launch (start us, length us, event | category | flops | bytes accessed | tf_op | source)
XLA Modules:
  0.0 134.6 jit_solution(9421390824783084551)
XLA Ops:
  0.6 0.7 broadcast_subtract_fusion
  1.3 0.9 broadcast_in_dim.59
  2.2 17.7 %all_to_all.24 = bf16[4,16,2048]{2,1,0:T(8,128)(2,1)S(1)} all-to-all(bf16[4,16,2048]{2,1,0:T(8,128)(2,1)S(1)} %broadcast_in_dim.59), channel_id=1, replica_groups=mesh['yh'=4,'yl'=2,'core'=2,'zh'=4,'zl'=2,'x'=4] {'yh'}, dimensions={0} | all-to-all | bytes 524288 | tf_op jit(solution)/shard_map/all_to_all | solution.py:13
  19.9 0.2 broadcast_in_dim.60
  20.1 29.2 %all_to_all.25 = bf16[8,4,16,2048]{3,2,1,0:T(8,128)(2,1)S(1)} all-to-all(bf16[8,4,16,2048]{3,2,1,0:T(8,128)(2,1)S(1)} %broadcast_in_dim.60), channel_id=1, replica_groups=mesh['yh'=4,'yl'=2,'core'=2,'zh'=4,'zl'=2,'x'=4] {'x','yl'}, dimensions={0} | all-to-all | bytes 4194304 | tf_op jit(solution)/shard_map/all_to_all | solution.py:13
  49.3 0.1 copy.9
  49.5 1.9 %collective-permute-start = (bf16[512,2048]{1,0:T(8,128)(2,1)S(1)}, bf16[512,2048]{1,0:T(8,128)(2,1)}, u32[]{:S(2)}, u32[]{:S(2)}) collective-permute-start(bf16[512,2048]{1,0:T(8,128)(2,1)S(1)} %bitcast.29), channel_id=1, source_target_pairs={{0,32},{32,0},{1,33},{33,1},{2,34},{34,2},{3,35},{35,3},{4,36},{36... | collective-permute-start | bytes 6291464 | tf_op jit(solution)/shard_map/ppermute | solution.py:28
  51.4 4.7 %convolution_convert_fusion.1 = f16[512,1024]{1,0:T(8,128)(2,1)S(1)} fusion(bf16[512,2048]{1,0:T(8,128)(2,1)S(1)} %bitcast.30, bf16[2048,1024]{1,0:T(8,128)(2,1)} %param.4), kind=kOutput, calls=%fused_computation.3 | convolution fusion | flops 2148007936 | bytes 7340032 | tf_op jit(solution)/shard_map/dot_general | solution.py:31
  56.2 4.0 %convolution_convert_fusion = f16[512,1024]{1,0:T(8,128)(2,1)S(1)} fusion(bf16[512,2048]{1,0:T(8,128)(2,1)} %collective-permute-done, bf16[2048,1024]{1,0:T(8,128)(2,1)S(1)} %copy-done), kind=kOutput, calls=%fused_computation.2 | convolution fusion | flops 2148007936 | bytes 7340032 | tf_op jit(solution)/shard_map/dot_general | solution.py:31
  60.2 0.7 dynamic-slice_bitcast_fusion.2
  60.8 0.4 broadcast_select_fusion
  61.3 1.9 %collective-permute-start.1 = (f16[2,8,32,1024]{3,2,1,0:T(8,128)(2,1)S(1)}, f16[2,8,32,1024]{3,2,1,0:T(8,128)(2,1)S(1)}, u32[]{:S(2)}, u32[]{:S(2)}) collective-permute-start(f16[2,8,32,1024]{3,2,1,0:T(8,128)(2,1)S(1)} %broadcast_select_fusion), channel_id=1, source_target_pairs={{0,4},{4,0},{8,12},{12,8},{16,20},{20,16},{24,28},{28,24},{32,60},... | collective-permute-start | bytes 3145736 | tf_op jit(solution)/shard_map/ppermute | solution.py:41
  63.2 14.8 %collective-permute-done.1 = f16[2,8,32,1024]{3,2,1,0:T(8,128)(2,1)S(1)} collective-permute-done((f16[2,8,32,1024]{3,2,1,0:T(8,128)(2,1)S(1)}, f16[2,8,32,1024]{3,2,1,0:T(8,128)(2,1)S(1)}, u32[]{:S(2)}, u32[]{:S(2)}) %collective-permute-start.1) | collective-permute-done | bytes 1048608 | tf_op jit(solution)/shard_map/ppermute | solution.py:41
  78.0 1.7 %add_convert_fusion = f16[2,8,32,1024]{3,2,1,0:T(8,128)(2,1)} fusion(f16[2,8,32,1024]{3,2,1,0:T(8,128)(2,1)S(1)} %collective-permute-done.1, pred[2]{0:T(512)(128)(4,1)S(1)} %iota_compare_fusion, f16[8,32,1024]{2,1,0:T(8,128)(2,1)S(1)} %get-tuple-element.20, f16[8,32,1024]{2,1,0:T(8,128)(2,1)S(1)} %get-tuple-element.25), kind=kLoop, calls=%fused_computation.1 | loop fusion | flops 2621440 | bytes 3145730 | tf_op jit(solution)/shard_map/convert_element_type | solution.py:42
  79.7 10.1 %all-to-all-start.2 = ((f16[16,32,1024]{2,1,0:T(8,128)(2,1)}), f16[16,32,1024]{2,1,0:T(8,128)(2,1)S(1)}, u32[]{:S(2)}, u32[]{:S(2)}) async-start(f16[16,32,1024]{2,1,0:T(8,128)(2,1)} %bitcast.9), calls=%async_computation.2 | async-start | bytes 2097152 | tf_op jit(solution)/shard_map/all_to_all | solution.py:43
  89.7 30.1 %all-to-all-done.2 = f16[16,32,1024]{2,1,0:T(8,128)(2,1)S(1)} async-done(((f16[16,32,1024]{2,1,0:T(8,128)(2,1)}), f16[16,32,1024]{2,1,0:T(8,128)(2,1)S(1)}, u32[]{:S(2)}, u32[]{:S(2)}) %all-to-all-start.2) | async-done | bytes 1048608 | tf_op jit(solution)/shard_map/all_to_all | solution.py:43
  119.8 0.3 convert_reduce_fusion
  120.0 0.1 reduce_max.18
  120.2 0.3 exponential_reduce_fusion
  120.6 0.1 pad_maximum_fusion
  120.7 12.4 %all_to_all.26 = f32[16,1,96]{2,1,0:T(1,128)S(1)} all-to-all(f32[16,1,96]{2,1,0:T(1,128)S(1)} %broadcast_in_dim.70), channel_id=1, replica_groups=mesh['yh'=4,'yl'=2,'core'=2,'zh'=4,'zl'=2,'x'=4] {'core','yl','yh'}, dimensions={0} | all-to-all | bytes 12288 | tf_op jit(solution)/shard_map/all_to_all | solution.py:13
  133.1 0.1 slice_reduce_fusion
  133.2 0.5 subtract_subtract_fusion.1
  133.7 0.9 subtract_subtract_fusion
  (8 shorter events, 0.1 us)
Async XLA Ops:
  49.5 6.7 %collective-permute-start = (bf16[512,2048]{1,0:T(8,128)(2,1)S(1)}, bf16[512,2048]{1,0:T(8,128)(2,1)}, u32[]{:S(2)}, u32[]{:S(2)}) collective-permute-start(bf16[512,2048]{1,0:T(8,128)(2,1)S(1)} %bitcast.29), channel_id=1, source_target_pairs={{0,32},{32,0},{1,33},{33,1},{2,34},{34,2},{3,35},{35,3},{4,36},{36... | collective-permute-start | bytes 6291464 | tf_op jit(solution)/shard_map/ppermute | solution.py:28
  51.4 4.7 %copy-start = (bf16[2048,1024]{1,0:T(8,128)(2,1)S(1)}, bf16[2048,1024]{1,0:T(8,128)(2,1)}, u32[]{:S(2)}) copy-start(bf16[2048,1024]{1,0:T(8,128)(2,1)} %param.4) | copy-start | bytes 12582916
  61.3 16.7 %collective-permute-start.1 = (f16[2,8,32,1024]{3,2,1,0:T(8,128)(2,1)S(1)}, f16[2,8,32,1024]{3,2,1,0:T(8,128)(2,1)S(1)}, u32[]{:S(2)}, u32[]{:S(2)}) collective-permute-start(f16[2,8,32,1024]{3,2,1,0:T(8,128)(2,1)S(1)} %broadcast_select_fusion), channel_id=1, source_target_pairs={{0,4},{4,0},{8,12},{12,8},{16,20},{20,16},{24,28},{28,24},{32,60},... | collective-permute-start | bytes 3145736 | tf_op jit(solution)/shard_map/ppermute | solution.py:41
  79.7 40.1 %all-to-all-start.2 = ((f16[16,32,1024]{2,1,0:T(8,128)(2,1)}), f16[16,32,1024]{2,1,0:T(8,128)(2,1)S(1)}, u32[]{:S(2)}, u32[]{:S(2)}) async-start(f16[16,32,1024]{2,1,0:T(8,128)(2,1)} %bitcast.9), calls=%async_computation.2 | async-start | bytes 2097152 | tf_op jit(solution)/shard_map/all_to_all | solution.py:43

commit v9 on v8

--- a/solution.py
+++ b/solution.py
@@ -20,12 +20,14 @@
     core, odd, block = lax.axis_index("core"), lax.axis_index("zl"), lax.axis_index(Y + ("core",))
     pairs = [(i, i ^ 1) for i in range(nz)]
     pairs += [(nz + i, nz + ((i + 1) % nz if i % 2 else (i - 1) % nz)) for i in range(nz)]
-    token = tokens - block * (nx * cols)
-    hidden, token, core, odd = lax.optimization_barrier((hidden, token, core, odd))
+    hidden, core, odd, block = lax.optimization_barrier((hidden, core, odd, block))
 
     mine = spread(spread(hidden, "yh", yh), ("x", "yl"), 2 * nx).reshape(xh, 2, 2, yh, n, k)
     mine = jnp.transpose(mine, (2, 0, 3, 1, 4, 5)).reshape(2 * nx * yh * n, k)
+    mine, tokens = lax.optimization_barrier((mine, tokens))
     other = lax.ppermute(mine, "core", [(0, 1), (1, 0)])
+    token_block = tokens // cols - block * nx
+    token_column = lax.rem(tokens, cols)
 
     def product(rows):
         part = jnp.dot(rows, head_weight, preferred_element_type=F32)
@@ -40,13 +42,15 @@
 
     taken = lax.ppermute(parity(1 - odd), ("core",) + Z, pairs)
     pair = (parity(odd).astype(F32) + taken.astype(F32)).astype(F16)
+    pair, token_block, token_column = lax.optimization_barrier((pair, token_block, token_column))
     part = lax.all_to_all(pair.reshape(nx * zh, 2 * n, cols), ("x", "zh"), split_axis=0, concat_axis=0, tiled=True)
     logits = jnp.sum(part.reshape(nx, zh, 2 * n, cols).astype(F32), axis=1)
 
-    column = lax.broadcasted_iota(jnp.int32, logits.shape, 0) * cols + lax.broadcasted_iota(jnp.int32, logits.shape, 2)
+    hit = lax.broadcasted_iota(jnp.int32, logits.shape, 0) == token_block[:, None]
+    hit &= lax.broadcasted_iota(jnp.int32, logits.shape, 2) == token_column[:, None]
     peak = jnp.max(logits, axis=(0, 2))
     total = jnp.sum(jnp.exp(logits - peak[:, None]), axis=(0, 2))
-    picked = jnp.sum(jnp.where(column == token[:, None], logits, 0.0), axis=(0, 2))
+    picked = jnp.sum(jnp.where(hit, logits, 0.0), axis=(0, 2))
     logits = jnp.swapaxes(logits, 0, 1).reshape(2 * n, nx * cols)
     stats, logits = lax.optimization_barrier((jnp.concatenate([peak, total, picked]), logits))
     peaks, totals, picks = jnp.split(spread(stats, ("core", "yl", "yh"), 2 * ny), 3, axis=1)

time: 135 us -> 133 us (0.985)
  the two profiles are of different devices: /device:TPU:64 before, /device:TPU:2 now
where the time goes in v9:
time: 133 us
  blocking collectives  99.1 us (75%)
  waiting for transfers between devices  12.7 us (10%)
  matrix products  8.66 us (7%)
  starting transfers between devices  6.2 us (5%)
  other arithmetic  3.42 us (3%)
  local copies, waits for them, and re-layouts  1.9 us (1%)
    all_to_all x3, blocking collectives, spread(): lax.all_to_all(jnp.broadcast_to(x[None], (size,) + x.shape), axis, split_...  58.1 us
    all_to_all x1, blocking collectives, local(): lax.all_to_all(pair.reshape(nx * zh, 2 * n, cols), ('x', 'zh'), split_axi...  41 us
    ppermute x1, waiting for transfers between devices, local(): taken = lax.ppermute(parity(1 - odd), ('core',) + Z, pairs)  12.7 us
    dot_general x2, matrix products, product(): part = jnp.dot(rows, head_weight, preferred_element_type=F32)  8.66 us
    ppermute x1, starting transfers between devices, local(): taken = lax.ppermute(parity(1 - odd), ('core',) + Z, pairs)  4.28 us
  transfers between devices with their start and end apart: 2, of which 1 were waited for; matrix products, arithmetic and copies ran while one was open for 4% of the time, Pallas kernels for 0%

profile of v9, /device:TPU:2, one launch (start us, length us, event | category | flops | bytes accessed | tf_op | source)
XLA Modules:
  0.0 132.8 jit_solution(8374196691831839817)
XLA Ops:
  0.6 0.9 broadcast_in_dim.59
  1.5 17.7 %all_to_all.24 = bf16[4,16,2048]{2,1,0:T(8,128)(2,1)S(1)} all-to-all(bf16[4,16,2048]{2,1,0:T(8,128)(2,1)S(1)} %broadcast_in_dim.59), channel_id=1, replica_groups=mesh['yh'=4,'yl'=2,'core'=2,'zh'=4,'zl'=2,'x'=4] {'yh'}, dimensions={0} | all-to-all | bytes 524288 | tf_op jit(solution)/shard_map/all_to_all | solution.py:13
  19.2 0.2 broadcast_in_dim.60
  19.5 28.0 %all_to_all.25 = bf16[8,4,16,2048]{3,2,1,0:T(8,128)(2,1)S(1)} all-to-all(bf16[8,4,16,2048]{3,2,1,0:T(8,128)(2,1)S(1)} %broadcast_in_dim.60), channel_id=1, replica_groups=mesh['yh'=4,'yl'=2,'core'=2,'zh'=4,'zl'=2,'x'=4] {'x','yl'}, dimensions={0} | all-to-all | bytes 4194304 | tf_op jit(solution)/shard_map/all_to_all | solution.py:13
  47.4 0.1 copy.9
  47.6 1.9 %collective-permute-start = (bf16[512,2048]{1,0:T(8,128)(2,1)S(1)}, bf16[512,2048]{1,0:T(8,128)(2,1)}, u32[]{:S(2)}, u32[]{:S(2)}) collective-permute-start(bf16[512,2048]{1,0:T(8,128)(2,1)S(1)} %bitcast.30), channel_id=1, source_target_pairs={{0,32},{32,0},{1,33},{33,1},{2,34},{34,2},{3,35},{35,3},{4,36},{36... | collective-permute-start | bytes 6291464 | tf_op jit(solution)/shard_map/ppermute | solution.py:28
  49.5 0.0 copy-start.1
  49.5 4.7 %convolution_convert_fusion.1 = f16[512,1024]{1,0:T(8,128)(2,1)S(1)} fusion(bf16[512,2048]{1,0:T(8,128)(2,1)S(1)} %bitcast.31, bf16[2048,1024]{1,0:T(8,128)(2,1)} %param.4), kind=kOutput, calls=%fused_computation.3 | convolution fusion | flops 2148007936 | bytes 7340032 | tf_op jit(solution)/shard_map/dot_general | solution.py:33
  54.3 4.0 %convolution_convert_fusion = f16[512,1024]{1,0:T(8,128)(2,1)S(1)} fusion(bf16[512,2048]{1,0:T(8,128)(2,1)} %collective-permute-done, bf16[2048,1024]{1,0:T(8,128)(2,1)S(1)} %copy-done.1), kind=kOutput, calls=%fused_computation.2 | convolution fusion | flops 2148007936 | bytes 7340032 | tf_op jit(solution)/shard_map/dot_general | solution.py:33
  58.2 0.6 dynamic-slice_bitcast_fusion.2
  58.8 0.0 copy-start
  58.9 0.4 broadcast_select_fusion
  59.3 4.3 %collective-permute-start.1 = (f16[2,8,32,1024]{3,2,1,0:T(8,128)(2,1)S(1)}, f16[2,8,32,1024]{3,2,1,0:T(8,128)(2,1)S(1)}, u32[]{:S(2)}, u32[]{:S(2)}) collective-permute-start(f16[2,8,32,1024]{3,2,1,0:T(8,128)(2,1)S(1)} %broadcast_select_fusion), channel_id=1, source_target_pairs={{0,4},{4,0},{8,12},{12,8},{16,20},{20,16},{24,28},{28,24},{32,60},... | collective-permute-start | bytes 3145736 | tf_op jit(solution)/shard_map/ppermute | solution.py:43
  63.6 12.7 %collective-permute-done.1 = f16[2,8,32,1024]{3,2,1,0:T(8,128)(2,1)S(1)} collective-permute-done((f16[2,8,32,1024]{3,2,1,0:T(8,128)(2,1)S(1)}, f16[2,8,32,1024]{3,2,1,0:T(8,128)(2,1)S(1)}, u32[]{:S(2)}, u32[]{:S(2)}) %collective-permute-start.1) | collective-permute-done | bytes 1048608 | tf_op jit(solution)/shard_map/ppermute | solution.py:43
  76.3 0.7 add_convert_fusion
  77.0 41.0 %all_to_all.26 = f16[16,32,1024]{2,1,0:T(8,128)(2,1)S(1)} all-to-all(f16[16,32,1024]{2,1,0:T(8,128)(2,1)S(1)} %bitcast.28), channel_id=1, replica_groups=mesh['yh'=4,'yl'=2,'core'=2,'zh'=4,'zl'=2,'x'=4] {'x','zh'}, dimensions={0} | all-to-all | bytes 2097152 | tf_op jit(solution)/shard_map/all_to_all | solution.py:46
  118.0 0.2 convert_reduce_fusion
  118.2 0.1 reduce_max.18
  118.4 0.3 exponential_reduce_fusion
  118.7 0.1 pad_maximum_fusion
  118.8 12.4 %all_to_all.27 = f32[16,1,96]{2,1,0:T(1,128)S(1)} all-to-all(f32[16,1,96]{2,1,0:T(1,128)S(1)} %broadcast_in_dim.70), channel_id=1, replica_groups=mesh['yh'=4,'yl'=2,'core'=2,'zh'=4,'zl'=2,'x'=4] {'core','yl','yh'}, dimensions={0} | all-to-all | bytes 12288 | tf_op jit(solution)/shard_map/all_to_all | solution.py:13
  131.2 0.1 slice_reduce_fusion
  131.3 0.5 subtract_subtract_fusion.1
  131.9 0.9 subtract_subtract_fusion
  (8 shorter events, 0.1 us)
Async XLA Ops:
  47.6 6.7 %collective-permute-start = (bf16[512,2048]{1,0:T(8,128)(2,1)S(1)}, bf16[512,2048]{1,0:T(8,128)(2,1)}, u32[]{:S(2)}, u32[]{:S(2)}) collective-permute-start(bf16[512,2048]{1,0:T(8,128)(2,1)S(1)} %bitcast.30), channel_id=1, source_target_pairs={{0,32},{32,0},{1,33},{33,1},{2,34},{34,2},{3,35},{35,3},{4,36},{36... | collective-permute-start | bytes 6291464 | tf_op jit(solution)/shard_map/ppermute | solution.py:28
  49.5 4.7 %copy-start.1 = (bf16[2048,1024]{1,0:T(8,128)(2,1)S(1)}, bf16[2048,1024]{1,0:T(8,128)(2,1)}, u32[]{:S(2)}) copy-start(bf16[2048,1024]{1,0:T(8,128)(2,1)} %param.4) | copy-start | bytes 12582916
  58.8 4.7 %copy-start = (s32[32]{0:T(128)S(1)}, s32[32]{0:T(128)}, u32[]{:S(2)}) copy-start(s32[32]{0:T(128)} %param.5) | copy-start | bytes 388
  59.3 17.1 %collective-permute-start.1 = (f16[2,8,32,1024]{3,2,1,0:T(8,128)(2,1)S(1)}, f16[2,8,32,1024]{3,2,1,0:T(8,128)(2,1)S(1)}, u32[]{:S(2)}, u32[]{:S(2)}) collective-permute-start(f16[2,8,32,1024]{3,2,1,0:T(8,128)(2,1)S(1)} %broadcast_select_fusion), channel_id=1, source_target_pairs={{0,4},{4,0},{8,12},{12,8},{16,20},{20,16},{24,28},{28,24},{32,60},... | collective-permute-start | bytes 3145736 | tf_op jit(solution)/shard_map/ppermute | solution.py:43

commit v10 on v9

--- a/solution.py
+++ b/solution.py
@@ -33,15 +33,20 @@
         part = jnp.dot(rows, head_weight, preferred_element_type=F32)
         return part.astype(F16).reshape(2, xh * zh, 2 * n, cols)
 
-    own, far = product(mine), product(other)
+    def parity(part, which):
+        return lax.dynamic_index_in_dim(part, which, 0, keepdims=False)
 
-    def parity(which):
-        a, b = (lax.dynamic_index_in_dim(p, which, 0, keepdims=True) for p in (own, far))
-        place = lax.broadcasted_iota(jnp.int32, (2,) + a.shape[1:], 0)
-        return jnp.where(place == core, a, b)
+    def partner(part):
+        return lax.ppermute(part, ("core",) + Z, pairs)
 
-    taken = lax.ppermute(parity(1 - odd), ("core",) + Z, pairs)
-    pair = (parity(odd).astype(F32) + taken.astype(F32)).astype(F16)
+    own = product(mine)
+    give = parity(own, 1 - odd)
+    other, _ = lax.optimization_barrier((other, give))
+    far = product(other)
+    own = parity(own, odd).astype(F32) + partner(give).astype(F32)
+    far = parity(far, odd).astype(F32) + partner(parity(far, 1 - odd)).astype(F32)
+    place = lax.broadcasted_iota(jnp.int32, (2,) + own.shape, 0)
+    pair = jnp.where(place == core, own[None], far[None]).astype(F16)
     pair, token_block, token_column = lax.optimization_barrier((pair, token_block, token_column))
     part = lax.all_to_all(pair.reshape(nx * zh, 2 * n, cols), ("x", "zh"), split_axis=0, concat_axis=0, tiled=True)
     logits = jnp.sum(part.reshape(nx, zh, 2 * n, cols).astype(F32), axis=1)

time: 133 us -> 133 us (level)
  the two profiles are of different devices: /device:TPU:2 before, /device:TPU:1 now
where the time goes in v10:
time: 133 us; the launch traced here: 132 us
  blocking collectives  89.9 us (68%)
  starting transfers between devices  18.5 us (14%)
  matrix products  8.63 us (6%)
  waiting for transfers between devices  7.95 us (6%)
  other arithmetic  4.04 us (3%)
  local copies, waits for them, and re-layouts  2.31 us (2%)
    all_to_all x3, blocking collectives, spread(): lax.all_to_all(jnp.broadcast_to(x[None], (size,) + x.shape), axis, split_...  58.7 us
    all_to_all x1, blocking collectives, local(): lax.all_to_all(pair.reshape(nx * zh, 2 * n, cols), ('x', 'zh'), split_axi...  31.1 us
    ppermute x2, starting transfers between devices, partner(): return lax.ppermute(part, ('core',) + Z, pairs)  12.7 us
    dot_general x2, matrix products, product(): part = jnp.dot(rows, head_weight, preferred_element_type=F32)  8.63 us
    ppermute x2, waiting for transfers between devices, partner(): return lax.ppermute(part, ('core',) + Z, pairs)  7.95 us
    ppermute x1, starting transfers between devices, local(): other = lax.ppermute(mine, 'core', [(0, 1), (1, 0)])  5.75 us
  transfers between devices with their start and end apart: 3, of which 2 were waited for; matrix products, arithmetic and copies ran while one was open for 8% of the time, Pallas kernels for 0%

profile of v10, /device:TPU:1, one launch (start us, length us, event | category | flops | bytes accessed | tf_op | source)
XLA Modules:
  0.0 132.1 jit_solution(5803453511205884757)
XLA Ops:
  0.6 0.9 broadcast_in_dim.26
  1.5 16.4 %all_to_all.24 = bf16[4,16,2048]{2,1,0:T(8,128)(2,1)S(1)} all-to-all(bf16[4,16,2048]{2,1,0:T(8,128)(2,1)S(1)} %broadcast_in_dim.26), channel_id=1, replica_groups=mesh['yh'=4,'yl'=2,'core'=2,'zh'=4,'zl'=2,'x'=4] {'yh'}, dimensions={0} | all-to-all | bytes 524288 | tf_op jit(solution)/shard_map/all_to_all | solution.py:13
  17.9 0.2 broadcast_in_dim.27
  18.2 28.1 %all_to_all.25 = bf16[8,4,16,2048]{3,2,1,0:T(8,128)(2,1)S(1)} all-to-all(bf16[8,4,16,2048]{3,2,1,0:T(8,128)(2,1)S(1)} %broadcast_in_dim.27), channel_id=1, replica_groups=mesh['yh'=4,'yl'=2,'core'=2,'zh'=4,'zl'=2,'x'=4] {'x','yl'}, dimensions={0} | all-to-all | bytes 4194304 | tf_op jit(solution)/shard_map/all_to_all | solution.py:13
  46.3 0.1 copy.9
  46.5 5.8 %collective-permute-start.1 = (bf16[512,2048]{1,0:T(8,128)(2,1)S(1)}, bf16[512,2048]{1,0:T(8,128)(2,1)}, u32[]{:S(2)}, u32[]{:S(2)}) collective-permute-start(bf16[512,2048]{1,0:T(8,128)(2,1)S(1)} %bitcast.32), channel_id=1, source_target_pairs={{0,32},{32,0},{1,33},{33,1},{2,34},{34,2},{3,35},{35,3},{4,36},{36... | collective-permute-start | bytes 6291464 | tf_op jit(solution)/shard_map/ppermute | solution.py:28
  52.2 4.7 %convolution_convert_fusion.1 = f16[512,1024]{1,0:T(8,128)(2,1)S(1)} fusion(bf16[512,2048]{1,0:T(8,128)(2,1)S(1)} %bitcast.33, bf16[2048,1024]{1,0:T(8,128)(2,1)} %param.4), kind=kOutput, calls=%fused_computation.3 | convolution fusion | flops 2148007936 | bytes 7340032 | tf_op jit(solution)/shard_map/dot_general | solution.py:33
  56.9 0.9 dynamic-slice_bitcast_fusion.1
  57.8 10.8 %collective-permute-start = (f16[8,32,1024]{2,1,0:T(8,128)(2,1)}, f16[8,32,1024]{2,1,0:T(8,128)(2,1)}, u32[]{:S(2)}, u32[]{:S(2)}) collective-permute-start(f16[8,32,1024]{2,1,0:T(8,128)(2,1)} %dynamic-slice_bitcast_fusion.1), channel_id=1, source_target_pairs={{0,4},{4,0},{8,12},{12,8},{16,20},{20,16},{24,28},{28,24},{32,60},... | collective-permute-start | bytes 1572872 | tf_op jit(solution)/shard_map/ppermute | solution.py:40
  68.6 4.0 %convolution_convert_fusion = f16[512,1024]{1,0:T(8,128)(2,1)S(1)} fusion(bf16[512,2048]{1,0:T(8,128)(2,1)} %collective-permute-done.1, bf16[2048,1024]{1,0:T(8,128)(2,1)S(1)} %copy-done.1), kind=kOutput, calls=%fused_computation.2 | convolution fusion | flops 2148007936 | bytes 7340032 | tf_op jit(solution)/shard_map/dot_general | solution.py:33
  72.6 0.1 dynamic-slice_bitcast_fusion
  72.7 1.9 %collective-permute-start.2 = (f16[8,32,1024]{2,1,0:T(8,128)(2,1)S(1)}, f16[8,32,1024]{2,1,0:T(8,128)(2,1)S(1)}, u32[]{:S(2)}, u32[]{:S(2)}) collective-permute-start(f16[8,32,1024]{2,1,0:T(8,128)(2,1)S(1)} %dynamic-slice_bitcast_fusion), channel_id=1, source_target_pairs={{0,4},{4,0},{8,12},{12,8},{16,20},{20,16},{24,28},{28,24},{32,60},... | collective-permute-start | bytes 1572872 | tf_op jit(solution)/shard_map/ppermute | solution.py:40
  74.7 0.8 collective-permute-done
  75.5 1.2 convert_add_fusion.1
  76.7 7.2 %collective-permute-done.2 = f16[8,32,1024]{2,1,0:T(8,128)(2,1)S(1)} collective-permute-done((f16[8,32,1024]{2,1,0:T(8,128)(2,1)S(1)}, f16[8,32,1024]{2,1,0:T(8,128)(2,1)S(1)}, u32[]{:S(2)}, u32[]{:S(2)}) %collective-permute-start.2) | collective-permute-done | bytes 524320 | tf_op jit(solution)/shard_map/ppermute | solution.py:40
  83.9 0.2 convert_add_fusion
  84.0 0.3 select_convert_fusion
  84.4 31.1 %all_to_all.26 = f16[16,32,1024]{2,1,0:T(8,128)(2,1)S(1)} all-to-all(f16[16,32,1024]{2,1,0:T(8,128)(2,1)S(1)} %bitcast.30), channel_id=1, replica_groups=mesh['yh'=4,'yl'=2,'core'=2,'zh'=4,'zl'=2,'x'=4] {'x','zh'}, dimensions={0} | all-to-all | bytes 2097152 | tf_op jit(solution)/shard_map/all_to_all | solution.py:51
  115.5 0.2 convert_reduce_fusion
  115.8 0.1 reduce_max.18
  116.0 0.3 exponential_reduce_fusion
  116.4 14.2 %all_to_all.27 = f32[16,1,96]{2,1,0:T(1,128)S(1)} all-to-all(f32[16,1,96]{2,1,0:T(1,128)S(1)} %broadcast_in_dim.48), channel_id=1, replica_groups=mesh['yh'=4,'yl'=2,'core'=2,'zh'=4,'zl'=2,'x'=4] {'core','yl','yh'}, dimensions={0} | all-to-all | bytes 12288 | tf_op jit(solution)/shard_map/all_to_all | solution.py:13
  130.6 0.5 subtract_subtract_fusion.1
  131.2 0.9 subtract_subtract_fusion
  (12 shorter events, 0.3 us)
Async XLA Ops:
  46.5 22.1 %collective-permute-start.1 = (bf16[512,2048]{1,0:T(8,128)(2,1)S(1)}, bf16[512,2048]{1,0:T(8,128)(2,1)}, u32[]{:S(2)}, u32[]{:S(2)}) collective-permute-start(bf16[512,2048]{1,0:T(8,128)(2,1)S(1)} %bitcast.32), channel_id=1, source_target_pairs={{0,32},{32,0},{1,33},{33,1},{2,34},{34,2},{3,35},{35,3},{4,36},{36... | collective-permute-start | bytes 6291464 | tf_op jit(solution)/shard_map/ppermute | solution.py:28
  52.2 16.4 %copy-start.1 = (bf16[2048,1024]{1,0:T(8,128)(2,1)S(1)}, bf16[2048,1024]{1,0:T(8,128)(2,1)}, u32[]{:S(2)}) copy-start(bf16[2048,1024]{1,0:T(8,128)(2,1)} %param.4) | copy-start | bytes 12582916
  57.8 16.9 %copy-start = (s32[32]{0:T(128)S(1)}, s32[32]{0:T(128)}, u32[]{:S(2)}) copy-start(s32[32]{0:T(128)} %param.5) | copy-start | bytes 388
  57.8 17.7 %collective-permute-start = (f16[8,32,1024]{2,1,0:T(8,128)(2,1)}, f16[8,32,1024]{2,1,0:T(8,128)(2,1)}, u32[]{:S(2)}, u32[]{:S(2)}) collective-permute-start(f16[8,32,1024]{2,1,0:T(8,128)(2,1)} %dynamic-slice_bitcast_fusion.1), channel_id=1, source_target_pairs={{0,4},{4,0},{8,12},{12,8},{16,20},{20,16},{24,28},{28,24},{32,60},... | collective-permute-start | bytes 1572872 | tf_op jit(solution)/shard_map/ppermute | solution.py:40
  72.7 11.1 %collective-permute-start.2 = (f16[8,32,1024]{2,1,0:T(8,128)(2,1)S(1)}, f16[8,32,1024]{2,1,0:T(8,128)(2,1)S(1)}, u32[]{:S(2)}, u32[]{:S(2)}) collective-permute-start(f16[8,32,1024]{2,1,0:T(8,128)(2,1)S(1)} %dynamic-slice_bitcast_fusion), channel_id=1, source_target_pairs={{0,4},{4,0},{8,12},{12,8},{16,20},{20,16},{24,28},{28,24},{32,60},... | collective-permute-start | bytes 1572872 | tf_op jit(solution)/shard_map/ppermute | solution.py:40

commit v11 on v10

--- a/solution.py
+++ b/solution.py
@@ -20,31 +20,36 @@
     core, odd, block = lax.axis_index("core"), lax.axis_index("zl"), lax.axis_index(Y + ("core",))
     pairs = [(i, i ^ 1) for i in range(nz)]
     pairs += [(nz + i, nz + ((i + 1) % nz if i % 2 else (i - 1) % nz)) for i in range(nz)]
-    hidden, core, odd, block = lax.optimization_barrier((hidden, core, odd, block))
+    hidden, core, odd, block = lax.optimization_barrier((hidden, core, odd, block * nx))
 
     mine = spread(spread(hidden, "yh", yh), ("x", "yl"), 2 * nx).reshape(xh, 2, 2, yh, n, k)
-    mine = jnp.transpose(mine, (2, 0, 3, 1, 4, 5)).reshape(2 * nx * yh * n, k)
-    mine, tokens = lax.optimization_barrier((mine, tokens))
-    other = lax.ppermute(mine, "core", [(0, 1), (1, 0)])
-    token_block = tokens // cols - block * nx
+    mine, tokens, core, odd, block = lax.optimization_barrier((mine, tokens, core, odd, block))
+    token_block = tokens // cols - block
     token_column = lax.rem(tokens, cols)
+
+    def parity(which):
+        rows = lax.dynamic_index_in_dim(mine, which, 2, keepdims=False)
+        return jnp.swapaxes(rows, 1, 2).reshape(nx * yh * n, k)
 
     def product(rows):
         part = jnp.dot(rows, head_weight, preferred_element_type=F32)
-        return part.astype(F16).reshape(2, xh * zh, 2 * n, cols)
+        return part.reshape(xh * zh, 2 * n, cols)
 
-    def parity(part, which):
-        return lax.dynamic_index_in_dim(part, which, 0, keepdims=False)
+    def swapped(rows):
+        return lax.ppermute(rows, "core", [(0, 1), (1, 0)])
 
     def partner(part):
-        return lax.ppermute(part, ("core",) + Z, pairs)
+        return lax.ppermute(part.astype(F16), ("core",) + Z, pairs).astype(F32)
 
-    own = product(mine)
-    give = parity(own, 1 - odd)
-    other, _ = lax.optimization_barrier((other, give))
-    far = product(other)
-    own = parity(own, odd).astype(F32) + partner(give).astype(F32)
-    far = parity(far, odd).astype(F32) + partner(parity(far, 1 - odd)).astype(F32)
+    give, keep = lax.optimization_barrier((parity(1 - odd), parity(odd)))
+    give_far = swapped(give)
+    given = product(give).astype(F16)
+    give_far, _ = lax.optimization_barrier((give_far, given))
+    given_far = product(give_far).astype(F16)
+    taken, taken_far = partner(given), partner(given_far)
+    keep, _ = lax.optimization_barrier((keep, taken))
+    kept, kept_far = lax.optimization_barrier((product(keep), product(swapped(keep))))
+    own, far = kept + taken, kept_far + taken_far
     place = lax.broadcasted_iota(jnp.int32, (2,) + own.shape, 0)
     pair = jnp.where(place == core, own[None], far[None]).astype(F16)
     pair, token_block, token_column = lax.optimization_barrier((pair, token_block, token_column))

time: 133 us -> 127 us (0.955)
  the two profiles are of different devices: /device:TPU:1 before, /device:TPU:2 now
where the time goes in v11:
time: 127 us; the launch traced here: 126 us
  blocking collectives  97.6 us (77%)
  starting transfers between devices  10.8 us (9%)
  waiting for transfers between devices  7.64 us (6%)
  matrix products  5.12 us (4%)
  other arithmetic  3 us (2%)
  local copies, waits for them, and re-layouts  1.47 us (1%)
    all_to_all x3, blocking collectives, spread(): lax.all_to_all(jnp.broadcast_to(x[None], (size,) + x.shape), axis, split_...  58.1 us
    all_to_all x1, blocking collectives, local(): lax.all_to_all(pair.reshape(nx * zh, 2 * n, cols), ('x', 'zh'), split_axi...  39.5 us
    ppermute x2, waiting for transfers between devices, partner(): return lax.ppermute(part.astype(F16), ('core',) + Z, pairs).astype(F32)  7.63 us
    ppermute x2, starting transfers between devices, partner(): return lax.ppermute(part.astype(F16), ('core',) + Z, pairs).astype(F32)  6.2 us
    dot_general x4, matrix products, product(): part = jnp.dot(rows, head_weight, preferred_element_type=F32)  5.12 us
    ppermute x2, starting transfers between devices, swapped(): return lax.ppermute(rows, 'core', [(0, 1), (1, 0)])  4.59 us
  transfers between devices with their start and end apart: 4, of which 2 were waited for; matrix products, arithmetic and copies ran while one was open for 4% of the time, Pallas kernels for 0%

profile of v11, /device:TPU:2, one launch (start us, length us, event | category | flops | bytes accessed | tf_op | source)
XLA Modules:
  0.0 126.5 jit_solution(8931807507470170375)
XLA Ops:
  0.6 0.9 broadcast_in_dim.26
  1.5 17.7 %all_to_all.24 = bf16[4,16,2048]{2,1,0:T(8,128)(2,1)S(1)} all-to-all(bf16[4,16,2048]{2,1,0:T(8,128)(2,1)S(1)} %broadcast_in_dim.26), channel_id=1, replica_groups=mesh['yh'=4,'yl'=2,'core'=2,'zh'=4,'zl'=2,'x'=4] {'yh'}, dimensions={0} | all-to-all | bytes 524288 | tf_op jit(solution)/shard_map/all_to_all | solution.py:13
  19.2 0.2 broadcast_in_dim.27
  19.5 28.0 %all_to_all.25 = bf16[8,4,16,2048]{3,2,1,0:T(8,128)(2,1)S(1)} all-to-all(bf16[8,4,16,2048]{3,2,1,0:T(8,128)(2,1)S(1)} %broadcast_in_dim.27), channel_id=1, replica_groups=mesh['yh'=4,'yl'=2,'core'=2,'zh'=4,'zl'=2,'x'=4] {'x','yl'}, dimensions={0} | all-to-all | bytes 4194304 | tf_op jit(solution)/shard_map/all_to_all | solution.py:13
  47.8 2.2 %collective-permute-start.1 = (bf16[256,2048]{1,0:T(8,128)(2,1)S(1)}, bf16[256,2048]{1,0:T(8,128)(2,1)S(1)}, u32[]{:S(2)}, u32[]{:S(2)}) collective-permute-start(bf16[256,2048]{1,0:T(8,128)(2,1)S(1)} %bitcast.35), channel_id=1, source_target_pairs={{0,32},{32,0},{1,33},{33,1},{2,34},{34,2},{3,35},{35,3},{4,36},{36... | collective-permute-start | bytes 3145736 | tf_op jit(solution)/shard_map/ppermute | solution.py:39
  50.0 2.4 %collective-permute-start.2 = (bf16[256,2048]{1,0:T(8,128)(2,1)S(1)}, bf16[256,2048]{1,0:T(8,128)(2,1)S(1)}, u32[]{:S(2)}, u32[]{:S(2)}) collective-permute-start(bf16[256,2048]{1,0:T(8,128)(2,1)S(1)} %bitcast.37), channel_id=1, source_target_pairs={{0,32},{32,0},{1,33},{33,1},{2,34},{34,2},{3,35},{35,3},{4,36},{36... | collective-permute-start | bytes 3145736 | tf_op jit(solution)/shard_map/ppermute | solution.py:39
  52.4 1.3 %convolution_convert_fusion.1 = f16[256,1024]{1,0:T(8,128)(2,1)S(1)} fusion(bf16[256,2048]{1,0:T(8,128)(2,1)S(1)} %bitcast.38, bf16[2048,1024]{1,0:T(8,128)(2,1)S(1)} %copy-done.1), kind=kOutput, calls=%fused_computation.3 | convolution fusion | flops 1074003968 | bytes 5767168 | tf_op jit(solution)/shard_map/dot_general | solution.py:35
  53.7 4.3 %collective-permute-start = (f16[8,32,1024]{2,1,0:T(8,128)(2,1)S(1)}, f16[8,32,1024]{2,1,0:T(8,128)(2,1)S(1)}, u32[]{:S(2)}, u32[]{:S(2)}) collective-permute-start(f16[8,32,1024]{2,1,0:T(8,128)(2,1)S(1)} %bitcast.43), channel_id=1, source_target_pairs={{0,4},{4,0},{8,12},{12,8},{16,20},{20,16},{24,28},{28,24},{32,60},... | collective-permute-start | bytes 1572872 | tf_op jit(solution)/shard_map/ppermute | solution.py:42
  58.0 1.3 %fusion.3 = f32[256,1024]{1,0:T(8,128)S(1)} fusion(bf16[256,2048]{1,0:T(8,128)(2,1)S(1)} %bitcast.36, bf16[2048,1024]{1,0:T(8,128)(2,1)S(1)} %copy-done.1), kind=kOutput, calls=%fused_computation.26 | convolution fusion | flops 1073741824 | bytes 6291456 | tf_op jit(solution)/shard_map/dot_general | solution.py:35
  59.3 1.3 %convolution_convert_fusion = f16[256,1024]{1,0:T(8,128)(2,1)S(1)} fusion(bf16[256,2048]{1,0:T(8,128)(2,1)S(1)} %collective-permute-done.2, bf16[2048,1024]{1,0:T(8,128)(2,1)S(1)} %copy-done.1), kind=kOutput, calls=%fused_computation.2 | convolution fusion | flops 1074003968 | bytes 5767168 | tf_op jit(solution)/shard_map/dot_general | solution.py:35
  60.6 1.9 %collective-permute-start.3 = (f16[8,32,1024]{2,1,0:T(8,128)(2,1)S(1)}, f16[8,32,1024]{2,1,0:T(8,128)(2,1)S(1)}, u32[]{:S(2)}, u32[]{:S(2)}) collective-permute-start(f16[8,32,1024]{2,1,0:T(8,128)(2,1)S(1)} %bitcast.44), channel_id=1, source_target_pairs={{0,4},{4,0},{8,12},{12,8},{16,20},{20,16},{24,28},{28,24},{32,60},... | collective-permute-start | bytes 1572872 | tf_op jit(solution)/shard_map/ppermute | solution.py:42
  62.5 1.3 %fusion.4 = f32[256,1024]{1,0:T(8,128)S(1)} fusion(bf16[256,2048]{1,0:T(8,128)(2,1)S(1)} %collective-permute-done.1, bf16[2048,1024]{1,0:T(8,128)(2,1)S(1)} %copy-done.1), kind=kOutput, calls=%fused_computation.27 | convolution fusion | flops 1073741824 | bytes 6291456 | tf_op jit(solution)/shard_map/dot_general | solution.py:35
  63.8 1.3 %collective-permute-done = f16[8,32,1024]{2,1,0:T(8,128)(2,1)S(1)} collective-permute-done((f16[8,32,1024]{2,1,0:T(8,128)(2,1)S(1)}, f16[8,32,1024]{2,1,0:T(8,128)(2,1)S(1)}, u32[]{:S(2)}, u32[]{:S(2)}) %collective-permute-start) | collective-permute-done | bytes 524320 | tf_op jit(solution)/shard_map/ppermute | solution.py:42
  65.1 0.2 convert_add_fusion.1
  65.3 6.3 %collective-permute-done.3 = f16[8,32,1024]{2,1,0:T(8,128)(2,1)S(1)} collective-permute-done((f16[8,32,1024]{2,1,0:T(8,128)(2,1)S(1)}, f16[8,32,1024]{2,1,0:T(8,128)(2,1)S(1)}, u32[]{:S(2)}, u32[]{:S(2)}) %collective-permute-start.3) | collective-permute-done | bytes 524320 | tf_op jit(solution)/shard_map/ppermute | solution.py:42
  71.7 0.1 convert_add_fusion
  71.8 0.3 select_convert_fusion
  72.1 39.5 %all_to_all.26 = f16[16,32,1024]{2,1,0:T(8,128)(2,1)S(1)} all-to-all(f16[16,32,1024]{2,1,0:T(8,128)(2,1)S(1)} %bitcast.33), channel_id=1, replica_groups=mesh['yh'=4,'yl'=2,'core'=2,'zh'=4,'zl'=2,'x'=4] {'x','zh'}, dimensions={0} | all-to-all | bytes 2097152 | tf_op jit(solution)/shard_map/all_to_all | solution.py:56
  111.7 0.2 convert_reduce_fusion
  111.9 0.1 reduce_max.18
  112.1 0.3 exponential_reduce_fusion
  112.5 12.4 %all_to_all.27 = f32[16,1,96]{2,1,0:T(1,128)S(1)} all-to-all(f32[16,1,96]{2,1,0:T(1,128)S(1)} %broadcast_in_dim.48), channel_id=1, replica_groups=mesh['yh'=4,'yl'=2,'core'=2,'zh'=4,'zl'=2,'x'=4] {'core','yl','yh'}, dimensions={0} | all-to-all | bytes 12288 | tf_op jit(solution)/shard_map/all_to_all | solution.py:13
  125.0 0.5 subtract_subtract_fusion.1
  125.6 0.9 subtract_subtract_fusion
  (16 shorter events, 0.6 us)
Async XLA Ops:
  47.4 4.9 %copy-start.1 = (bf16[2048,1024]{1,0:T(8,128)(2,1)S(1)}, bf16[2048,1024]{1,0:T(8,128)(2,1)}, u32[]{:S(2)}) copy-start(bf16[2048,1024]{1,0:T(8,128)(2,1)} %param.4) | copy-start | bytes 12582916
  47.8 10.2 %copy-start = (s32[32]{0:T(128)S(1)}, s32[32]{0:T(128)}, u32[]{:S(2)}) copy-start(s32[32]{0:T(128)} %param.5) | copy-start | bytes 388
  47.8 14.7 %collective-permute-start.1 = (bf16[256,2048]{1,0:T(8,128)(2,1)S(1)}, bf16[256,2048]{1,0:T(8,128)(2,1)S(1)}, u32[]{:S(2)}, u32[]{:S(2)}) collective-permute-start(bf16[256,2048]{1,0:T(8,128)(2,1)S(1)} %bitcast.35), channel_id=1, source_target_pairs={{0,32},{32,0},{1,33},{33,1},{2,34},{34,2},{3,35},{35,3},{4,36},{36... | collective-permute-start | bytes 3145736 | tf_op jit(solution)/shard_map/ppermute | solution.py:39
  50.0 9.3 %collective-permute-start.2 = (bf16[256,2048]{1,0:T(8,128)(2,1)S(1)}, bf16[256,2048]{1,0:T(8,128)(2,1)S(1)}, u32[]{:S(2)}, u32[]{:S(2)}) collective-permute-start(bf16[256,2048]{1,0:T(8,128)(2,1)S(1)} %bitcast.37), channel_id=1, source_target_pairs={{0,32},{32,0},{1,33},{33,1},{2,34},{34,2},{3,35},{35,3},{4,36},{36... | collective-permute-start | bytes 3145736 | tf_op jit(solution)/shard_map/ppermute | solution.py:39
  53.7 11.4 %collective-permute-start = (f16[8,32,1024]{2,1,0:T(8,128)(2,1)S(1)}, f16[8,32,1024]{2,1,0:T(8,128)(2,1)S(1)}, u32[]{:S(2)}, u32[]{:S(2)}) collective-permute-start(f16[8,32,1024]{2,1,0:T(8,128)(2,1)S(1)} %bitcast.43), channel_id=1, source_target_pairs={{0,4},{4,0},{8,12},{12,8},{16,20},{20,16},{24,28},{28,24},{32,60},... | collective-permute-start | bytes 1572872 | tf_op jit(solution)/shard_map/ppermute | solution.py:42
  60.6 11.1 %collective-permute-start.3 = (f16[8,32,1024]{2,1,0:T(8,128)(2,1)S(1)}, f16[8,32,1024]{2,1,0:T(8,128)(2,1)S(1)}, u32[]{:S(2)}, u32[]{:S(2)}) collective-permute-start(f16[8,32,1024]{2,1,0:T(8,128)(2,1)S(1)} %bitcast.44), channel_id=1, source_target_pairs={{0,4},{4,0},{8,12},{12,8},{16,20},{20,16},{24,28},{28,24},{32,60},... | collective-permute-start | bytes 1572872 | tf_op jit(solution)/shard_map/ppermute | solution.py:42

commit v12 on v11

--- a/solution.py
+++ b/solution.py
@@ -39,17 +39,16 @@
         return lax.ppermute(rows, "core", [(0, 1), (1, 0)])
 
     def partner(part):
-        return lax.ppermute(part.astype(F16), ("core",) + Z, pairs).astype(F32)
+        return lax.ppermute(part, ("core",) + Z, pairs)
 
     give, keep = lax.optimization_barrier((parity(1 - odd), parity(odd)))
     give_far = swapped(give)
     given = product(give).astype(F16)
-    give_far, _ = lax.optimization_barrier((give_far, given))
-    given_far = product(give_far).astype(F16)
-    taken, taken_far = partner(given), partner(given_far)
-    keep, _ = lax.optimization_barrier((keep, taken))
+    taken = partner(given)
+    keep, given = lax.optimization_barrier((keep, given))
+    taken_far = partner(product(give_far).astype(F16))
     kept, kept_far = lax.optimization_barrier((product(keep), product(swapped(keep))))
-    own, far = kept + taken, kept_far + taken_far
+    own, far = kept + taken.astype(F32), kept_far + taken_far.astype(F32)
     place = lax.broadcasted_iota(jnp.int32, (2,) + own.shape, 0)
     pair = jnp.where(place == core, own[None], far[None]).astype(F16)
     pair, token_block, token_column = lax.optimization_barrier((pair, token_block, token_column))

time: 127 us -> 129 us (1.016)
  the two profiles are of different devices: /device:TPU:2 before, /device:TPU:1 now
where the time goes in v12:
time: 129 us
  blocking collectives  90.4 us (70%)
  starting transfers between devices  21.1 us (16%)
  waiting for transfers between devices  7.15 us (6%)
  matrix products  5.11 us (4%)
  other arithmetic  3.01 us (2%)
  local copies, waits for them, and re-layouts  1.47 us (1%)
    all_to_all x3, blocking collectives, spread(): lax.all_to_all(jnp.broadcast_to(x[None], (size,) + x.shape), axis, split_...  57.7 us
    all_to_all x1, blocking collectives, local(): lax.all_to_all(pair.reshape(nx * zh, 2 * n, cols), ('x', 'zh'), split_axi...  32.6 us
    ppermute x2, starting transfers between devices, partner(): return lax.ppermute(part, ('core',) + Z, pairs)  13.1 us
    ppermute x2, starting transfers between devices, swapped(): return lax.ppermute(rows, 'core', [(0, 1), (1, 0)])  7.94 us
    ppermute x2, waiting for transfers between devices, partner(): return lax.ppermute(part, ('core',) + Z, pairs)  7.15 us
    dot_general x4, matrix products, product(): part = jnp.dot(rows, head_weight, preferred_element_type=F32)  5.11 us
  transfers between devices with their start and end apart: 4, of which 1 were waited for; matrix products, arithmetic and copies ran while one was open for 4% of the time, Pallas kernels for 0%

profile of v12, /device:TPU:1, one launch (start us, length us, event | category | flops | bytes accessed | tf_op | source)
XLA Modules:
  0.0 129.0 jit_solution(7333391948572900567)
XLA Ops:
  0.6 0.9 broadcast_in_dim.26
  1.5 16.4 %all_to_all.24 = bf16[4,16,2048]{2,1,0:T(8,128)(2,1)S(1)} all-to-all(bf16[4,16,2048]{2,1,0:T(8,128)(2,1)S(1)} %broadcast_in_dim.26), channel_id=1, replica_groups=mesh['yh'=4,'yl'=2,'core'=2,'zh'=4,'zl'=2,'x'=4] {'yh'}, dimensions={0} | all-to-all | bytes 524288 | tf_op jit(solution)/shard_map/all_to_all | solution.py:13
  17.9 0.2 broadcast_in_dim.27
  18.2 28.1 %all_to_all.25 = bf16[8,4,16,2048]{3,2,1,0:T(8,128)(2,1)S(1)} all-to-all(bf16[8,4,16,2048]{3,2,1,0:T(8,128)(2,1)S(1)} %broadcast_in_dim.27), channel_id=1, replica_groups=mesh['yh'=4,'yl'=2,'core'=2,'zh'=4,'zl'=2,'x'=4] {'x','yl'}, dimensions={0} | all-to-all | bytes 4194304 | tf_op jit(solution)/shard_map/all_to_all | solution.py:13
  46.3 0.1 dynamic-slice_bitcast_fusion
  46.7 6.0 %collective-permute-start.2 = (bf16[256,2048]{1,0:T(8,128)(2,1)S(1)}, bf16[256,2048]{1,0:T(8,128)(2,1)S(1)}, u32[]{:S(2)}, u32[]{:S(2)}) collective-permute-start(bf16[256,2048]{1,0:T(8,128)(2,1)S(1)} %bitcast.37), channel_id=1, source_target_pairs={{0,32},{32,0},{1,33},{33,1},{2,34},{34,2},{3,35},{35,3},{4,36},{36... | collective-permute-start | bytes 3145736 | tf_op jit(solution)/shard_map/ppermute | solution.py:39
  52.7 1.3 %convolution_convert_fusion.1 = f16[256,1024]{1,0:T(8,128)(2,1)S(1)} fusion(bf16[256,2048]{1,0:T(8,128)(2,1)S(1)} %bitcast.38, bf16[2048,1024]{1,0:T(8,128)(2,1)S(1)} %copy-done.1), kind=kOutput, calls=%fused_computation.3 | convolution fusion | flops 1074003968 | bytes 5767168 | tf_op jit(solution)/shard_map/dot_general | solution.py:35
  54.0 10.7 %collective-permute-start.1 = (f16[8,32,1024]{2,1,0:T(8,128)(2,1)S(1)}, f16[8,32,1024]{2,1,0:T(8,128)(2,1)S(1)}, u32[]{:S(2)}, u32[]{:S(2)}) collective-permute-start(f16[8,32,1024]{2,1,0:T(8,128)(2,1)S(1)} %bitcast.43), channel_id=1, source_target_pairs={{0,4},{4,0},{8,12},{12,8},{16,20},{20,16},{24,28},{28,24},{32,60},... | collective-permute-start | bytes 1572872 | tf_op jit(solution)/shard_map/ppermute | solution.py:42
  64.7 1.9 %collective-permute-start = (bf16[256,2048]{1,0:T(8,128)(2,1)S(1)}, bf16[256,2048]{1,0:T(8,128)(2,1)S(1)}, u32[]{:S(2)}, u32[]{:S(2)}) collective-permute-start(bf16[256,2048]{1,0:T(8,128)(2,1)S(1)} %bitcast.35), channel_id=1, source_target_pairs={{0,32},{32,0},{1,33},{33,1},{2,34},{34,2},{3,35},{35,3},{4,36},{36... | collective-permute-start | bytes 3145736 | tf_op jit(solution)/shard_map/ppermute | solution.py:39
  66.7 1.3 fusion.3
  67.9 1.3 convolution_convert_fusion
  69.2 2.5 %collective-permute-start.3 = (f16[8,32,1024]{2,1,0:T(8,128)(2,1)S(1)}, f16[8,32,1024]{2,1,0:T(8,128)(2,1)S(1)}, u32[]{:S(2)}, u32[]{:S(2)}) collective-permute-start(f16[8,32,1024]{2,1,0:T(8,128)(2,1)S(1)} %bitcast.44), channel_id=1, source_target_pairs={{0,4},{4,0},{8,12},{12,8},{16,20},{20,16},{24,28},{28,24},{32,60},... | collective-permute-start | bytes 1572872 | tf_op jit(solution)/shard_map/ppermute | solution.py:42
  71.7 1.3 fusion.4
  73.0 0.2 convert_add_fusion.1
  73.2 7.1 %collective-permute-done.3 = f16[8,32,1024]{2,1,0:T(8,128)(2,1)S(1)} collective-permute-done((f16[8,32,1024]{2,1,0:T(8,128)(2,1)S(1)}, f16[8,32,1024]{2,1,0:T(8,128)(2,1)S(1)}, u32[]{:S(2)}, u32[]{:S(2)}) %collective-permute-start.3) | collective-permute-done | bytes 524320 | tf_op jit(solution)/shard_map/ppermute | solution.py:42
  80.4 0.1 convert_add_fusion
  80.5 0.3 select_convert_fusion
  80.8 32.6 %all_to_all.26 = f16[16,32,1024]{2,1,0:T(8,128)(2,1)S(1)} all-to-all(f16[16,32,1024]{2,1,0:T(8,128)(2,1)S(1)} %bitcast.33), channel_id=1, replica_groups=mesh['yh'=4,'yl'=2,'core'=2,'zh'=4,'zl'=2,'x'=4] {'x','zh'}, dimensions={0} | all-to-all | bytes 2097152 | tf_op jit(solution)/shard_map/all_to_all | solution.py:55
  113.5 0.2 convert_reduce_fusion
  113.8 0.1 reduce_max.18
  113.9 0.3 exponential_reduce_fusion
  114.3 13.1 %all_to_all.27 = f32[16,1,96]{2,1,0:T(1,128)S(1)} all-to-all(f32[16,1,96]{2,1,0:T(1,128)S(1)} %broadcast_in_dim.48), channel_id=1, replica_groups=mesh['yh'=4,'yl'=2,'core'=2,'zh'=4,'zl'=2,'x'=4] {'core','yl','yh'}, dimensions={0} | all-to-all | bytes 12288 | tf_op jit(solution)/shard_map/all_to_all | solution.py:13
  127.6 0.5 subtract_subtract_fusion.1
  128.1 0.9 subtract_subtract_fusion
  (16 shorter events, 0.4 us)
Async XLA Ops:
  46.3 6.4 %copy-start.1 = (bf16[2048,1024]{1,0:T(8,128)(2,1)S(1)}, bf16[2048,1024]{1,0:T(8,128)(2,1)}, u32[]{:S(2)}) copy-start(bf16[2048,1024]{1,0:T(8,128)(2,1)} %param.4) | copy-start | bytes 12582916
  46.7 20.0 %copy-start = (s32[32]{0:T(128)S(1)}, s32[32]{0:T(128)}, u32[]{:S(2)}) copy-start(s32[32]{0:T(128)} %param.5) | copy-start | bytes 388
  46.7 21.3 %collective-permute-start.2 = (bf16[256,2048]{1,0:T(8,128)(2,1)S(1)}, bf16[256,2048]{1,0:T(8,128)(2,1)S(1)}, u32[]{:S(2)}, u32[]{:S(2)}) collective-permute-start(bf16[256,2048]{1,0:T(8,128)(2,1)S(1)} %bitcast.37), channel_id=1, source_target_pairs={{0,32},{32,0},{1,33},{33,1},{2,34},{34,2},{3,35},{35,3},{4,36},{36... | collective-permute-start | bytes 3145736 | tf_op jit(solution)/shard_map/ppermute | solution.py:39
  54.0 19.0 %collective-permute-start.1 = (f16[8,32,1024]{2,1,0:T(8,128)(2,1)S(1)}, f16[8,32,1024]{2,1,0:T(8,128)(2,1)S(1)}, u32[]{:S(2)}, u32[]{:S(2)}) collective-permute-start(f16[8,32,1024]{2,1,0:T(8,128)(2,1)S(1)} %bitcast.43), channel_id=1, source_target_pairs={{0,4},{4,0},{8,12},{12,8},{16,20},{20,16},{24,28},{28,24},{32,60},... | collective-permute-start | bytes 1572872 | tf_op jit(solution)/shard_map/ppermute | solution.py:42
  64.7 7.0 %collective-permute-start = (bf16[256,2048]{1,0:T(8,128)(2,1)S(1)}, bf16[256,2048]{1,0:T(8,128)(2,1)S(1)}, u32[]{:S(2)}, u32[]{:S(2)}) collective-permute-start(bf16[256,2048]{1,0:T(8,128)(2,1)S(1)} %bitcast.35), channel_id=1, source_target_pairs={{0,32},{32,0},{1,33},{33,1},{2,34},{34,2},{3,35},{35,3},{4,36},{36... | collective-permute-start | bytes 3145736 | tf_op jit(solution)/shard_map/ppermute | solution.py:39
  69.2 11.1 %collective-permute-start.3 = (f16[8,32,1024]{2,1,0:T(8,128)(2,1)S(1)}, f16[8,32,1024]{2,1,0:T(8,128)(2,1)S(1)}, u32[]{:S(2)}, u32[]{:S(2)}) collective-permute-start(f16[8,32,1024]{2,1,0:T(8,128)(2,1)S(1)} %bitcast.44), channel_id=1, source_target_pairs={{0,4},{4,0},{8,12},{12,8},{16,20},{20,16},{24,28},{28,24},{32,60},... | collective-permute-start | bytes 1572872 | tf_op jit(solution)/shard_map/ppermute | solution.py:42

commit v13 on v11

--- a/solution.py
+++ b/solution.py
@@ -29,11 +29,11 @@
 
     def parity(which):
         rows = lax.dynamic_index_in_dim(mine, which, 2, keepdims=False)
-        return jnp.swapaxes(rows, 1, 2).reshape(nx * yh * n, k)
+        return jnp.transpose(rows, (2, 0, 1, 3, 4)).reshape(nx * yh * n, k)
 
     def product(rows):
         part = jnp.dot(rows, head_weight, preferred_element_type=F32)
-        return part.reshape(xh * zh, 2 * n, cols)
+        return part.reshape(zh, xh, 2 * n, cols)
 
     def swapped(rows):
         return lax.ppermute(rows, "core", [(0, 1), (1, 0)])
@@ -51,10 +51,10 @@
     kept, kept_far = lax.optimization_barrier((product(keep), product(swapped(keep))))
     own, far = kept + taken, kept_far + taken_far
     place = lax.broadcasted_iota(jnp.int32, (2,) + own.shape, 0)
-    pair = jnp.where(place == core, own[None], far[None]).astype(F16)
+    pair = jnp.swapaxes(jnp.where(place == core, own[None], far[None]).astype(F16), 0, 1)
     pair, token_block, token_column = lax.optimization_barrier((pair, token_block, token_column))
-    part = lax.all_to_all(pair.reshape(nx * zh, 2 * n, cols), ("x", "zh"), split_axis=0, concat_axis=0, tiled=True)
-    logits = jnp.sum(part.reshape(nx, zh, 2 * n, cols).astype(F32), axis=1)
+    part = lax.all_to_all(pair.reshape(zh * nx, 2 * n, cols), ("zh", "x"), split_axis=0, concat_axis=0, tiled=True)
+    logits = jnp.sum(part.reshape(zh, nx, 2 * n, cols).astype(F32), axis=0)
 
     hit = lax.broadcasted_iota(jnp.int32, logits.shape, 0) == token_block[:, None]
     hit &= lax.broadcasted_iota(jnp.int32, logits.shape, 2) == token_column[:, None]

time: 127 us -> 127 us (level)
  the two profiles are of different devices: /device:TPU:2 before, /device:TPU:64 now
where the time goes in v13:
time: 127 us; the launch traced here: 126 us
  blocking collectives  98.9 us (78%)
  starting transfers between devices  10.4 us (8%)
  waiting for transfers between devices  6.72 us (5%)
  matrix products  5.12 us (4%)
  other arithmetic  3.01 us (2%)
  local copies, waits for them, and re-layouts  1.47 us (1%)
    all_to_all x3, blocking collectives, spread(): lax.all_to_all(jnp.broadcast_to(x[None], (size,) + x.shape), axis, split_...  59.3 us
    all_to_all x1, blocking collectives, local(): lax.all_to_all(pair.reshape(zh * nx, 2 * n, cols), ('zh', 'x'), split_axi...  39.6 us
    ppermute x2, waiting for transfers between devices, partner(): return lax.ppermute(part.astype(F16), ('core',) + Z, pairs).astype(F32)  6.72 us
    ppermute x2, starting transfers between devices, partner(): return lax.ppermute(part.astype(F16), ('core',) + Z, pairs).astype(F32)  5.84 us
    dot_general x4, matrix products, product(): part = jnp.dot(rows, head_weight, preferred_element_type=F32)  5.12 us
    ppermute x2, starting transfers between devices, swapped(): return lax.ppermute(rows, 'core', [(0, 1), (1, 0)])  4.59 us
  transfers between devices with their start and end apart: 4, of which 2 were waited for; matrix products, arithmetic and copies ran while one was open for 4% of the time, Pallas kernels for 0%

profile of v13, /device:TPU:64, one launch (start us, length us, event | category | flops | bytes accessed | tf_op | source)
XLA Modules:
  0.0 126.5 jit_solution(9283397992796748228)
XLA Ops:
  0.6 0.9 broadcast_in_dim.26
  1.5 17.7 %all_to_all.24 = bf16[4,16,2048]{2,1,0:T(8,128)(2,1)S(1)} all-to-all(bf16[4,16,2048]{2,1,0:T(8,128)(2,1)S(1)} %broadcast_in_dim.26), channel_id=1, replica_groups=mesh['yh'=4,'yl'=2,'core'=2,'zh'=4,'zl'=2,'x'=4] {'yh'}, dimensions={0} | all-to-all | bytes 524288 | tf_op jit(solution)/shard_map/all_to_all | solution.py:13
  19.2 0.2 broadcast_in_dim.27
  19.5 29.2 %all_to_all.25 = bf16[8,4,16,2048]{3,2,1,0:T(8,128)(2,1)S(1)} all-to-all(bf16[8,4,16,2048]{3,2,1,0:T(8,128)(2,1)S(1)} %broadcast_in_dim.27), channel_id=1, replica_groups=mesh['yh'=4,'yl'=2,'core'=2,'zh'=4,'zl'=2,'x'=4] {'x','yl'}, dimensions={0} | all-to-all | bytes 4194304 | tf_op jit(solution)/shard_map/all_to_all | solution.py:13
  49.0 2.2 %collective-permute-start.1 = (bf16[256,2048]{1,0:T(8,128)(2,1)S(1)}, bf16[256,2048]{1,0:T(8,128)(2,1)S(1)}, u32[]{:S(2)}, u32[]{:S(2)}) collective-permute-start(bf16[256,2048]{1,0:T(8,128)(2,1)S(1)} %bitcast.35), channel_id=1, source_target_pairs={{0,32},{32,0},{1,33},{33,1},{2,34},{34,2},{3,35},{35,3},{4,36},{36... | collective-permute-start | bytes 3145736 | tf_op jit(solution)/shard_map/ppermute | solution.py:39
  51.2 2.4 %collective-permute-start.2 = (bf16[256,2048]{1,0:T(8,128)(2,1)S(1)}, bf16[256,2048]{1,0:T(8,128)(2,1)S(1)}, u32[]{:S(2)}, u32[]{:S(2)}) collective-permute-start(bf16[256,2048]{1,0:T(8,128)(2,1)S(1)} %bitcast.37), channel_id=1, source_target_pairs={{0,32},{32,0},{1,33},{33,1},{2,34},{34,2},{3,35},{35,3},{4,36},{36... | collective-permute-start | bytes 3145736 | tf_op jit(solution)/shard_map/ppermute | solution.py:39
  53.6 1.3 %convolution_convert_fusion.1 = f16[256,1024]{1,0:T(8,128)(2,1)S(1)} fusion(bf16[256,2048]{1,0:T(8,128)(2,1)S(1)} %bitcast.38, bf16[2048,1024]{1,0:T(8,128)(2,1)S(1)} %copy-done.1), kind=kOutput, calls=%fused_computation.3 | convolution fusion | flops 1074003968 | bytes 5767168 | tf_op jit(solution)/shard_map/dot_general | solution.py:35
  54.9 1.9 %collective-permute-start = (f16[4,2,32,1024]{3,2,1,0:T(8,128)(2,1)S(1)}, f16[4,2,32,1024]{3,2,1,0:T(8,128)(2,1)S(1)}, u32[]{:S(2)}, u32[]{:S(2)}) collective-permute-start(f16[4,2,32,1024]{3,2,1,0:T(8,128)(2,1)S(1)} %bitcast.43), channel_id=1, source_target_pairs={{0,4},{4,0},{8,12},{12,8},{16,20},{20,16},{24,28},{28,24},{32,60},... | collective-permute-start | bytes 1572872 | tf_op jit(solution)/shard_map/ppermute | solution.py:42
  56.9 1.3 %fusion.3 = f32[256,1024]{1,0:T(8,128)S(1)} fusion(bf16[256,2048]{1,0:T(8,128)(2,1)S(1)} %bitcast.36, bf16[2048,1024]{1,0:T(8,128)(2,1)S(1)} %copy-done.1), kind=kOutput, calls=%fused_computation.26 | convolution fusion | flops 1073741824 | bytes 6291456 | tf_op jit(solution)/shard_map/dot_general | solution.py:35
  58.2 1.3 %convolution_convert_fusion = f16[256,1024]{1,0:T(8,128)(2,1)S(1)} fusion(bf16[256,2048]{1,0:T(8,128)(2,1)S(1)} %collective-permute-done.2, bf16[2048,1024]{1,0:T(8,128)(2,1)S(1)} %copy-done.1), kind=kOutput, calls=%fused_computation.2 | convolution fusion | flops 1074003968 | bytes 5767168 | tf_op jit(solution)/shard_map/dot_general | solution.py:35
  59.5 3.9 %collective-permute-start.3 = (f16[4,2,32,1024]{3,2,1,0:T(8,128)(2,1)S(1)}, f16[4,2,32,1024]{3,2,1,0:T(8,128)(2,1)S(1)}, u32[]{:S(2)}, u32[]{:S(2)}) collective-permute-start(f16[4,2,32,1024]{3,2,1,0:T(8,128)(2,1)S(1)} %bitcast.44), channel_id=1, source_target_pairs={{0,4},{4,0},{8,12},{12,8},{16,20},{20,16},{24,28},{28,24},{32,60},... | collective-permute-start | bytes 1572872 | tf_op jit(solution)/shard_map/ppermute | solution.py:42
  63.4 1.3 %fusion.4 = f32[256,1024]{1,0:T(8,128)S(1)} fusion(bf16[256,2048]{1,0:T(8,128)(2,1)S(1)} %collective-permute-done.1, bf16[2048,1024]{1,0:T(8,128)(2,1)S(1)} %copy-done.1), kind=kOutput, calls=%fused_computation.27 | convolution fusion | flops 1073741824 | bytes 6291456 | tf_op jit(solution)/shard_map/dot_general | solution.py:35
  64.7 1.3 %collective-permute-done = f16[4,2,32,1024]{3,2,1,0:T(8,128)(2,1)S(1)} collective-permute-done((f16[4,2,32,1024]{3,2,1,0:T(8,128)(2,1)S(1)}, f16[4,2,32,1024]{3,2,1,0:T(8,128)(2,1)S(1)}, u32[]{:S(2)}, u32[]{:S(2)}) %collective-permute-start) | collective-permute-done | bytes 524320 | tf_op jit(solution)/shard_map/ppermute | solution.py:42
  66.0 0.2 convert_add_fusion.1
  66.2 5.4 %collective-permute-done.3 = f16[4,2,32,1024]{3,2,1,0:T(8,128)(2,1)S(1)} collective-permute-done((f16[4,2,32,1024]{3,2,1,0:T(8,128)(2,1)S(1)}, f16[4,2,32,1024]{3,2,1,0:T(8,128)(2,1)S(1)}, u32[]{:S(2)}, u32[]{:S(2)}) %collective-permute-start.3) | collective-permute-done | bytes 524320 | tf_op jit(solution)/shard_map/ppermute | solution.py:42
  71.6 0.1 convert_add_fusion
  71.8 0.3 select_convert_fusion
  72.1 39.6 %all_to_all.26 = f16[16,32,1024]{2,1,0:T(8,128)(2,1)S(1)} all-to-all(f16[16,32,1024]{2,1,0:T(8,128)(2,1)S(1)} %bitcast.32), channel_id=1, replica_groups=mesh['yh'=4,'yl'=2,'core'=2,'zh'=4,'zl'=2,'x'=4] {'zh','x'}, dimensions={0} | all-to-all | bytes 2097152 | tf_op jit(solution)/shard_map/all_to_all | solution.py:56
  111.7 0.2 convert_reduce_fusion
  111.9 0.1 reduce_max.18
  112.1 0.3 exponential_reduce_fusion
  112.5 12.4 %all_to_all.27 = f32[16,1,96]{2,1,0:T(1,128)S(1)} all-to-all(f32[16,1,96]{2,1,0:T(1,128)S(1)} %broadcast_in_dim.48), channel_id=1, replica_groups=mesh['yh'=4,'yl'=2,'core'=2,'zh'=4,'zl'=2,'x'=4] {'core','yl','yh'}, dimensions={0} | all-to-all | bytes 12288 | tf_op jit(solution)/shard_map/all_to_all | solution.py:13
  125.0 0.5 subtract_subtract_fusion.1
  125.6 0.9 subtract_subtract_fusion
  (16 shorter events, 0.6 us)
Async XLA Ops:
  48.7 4.9 %copy-start.1 = (bf16[2048,1024]{1,0:T(8,128)(2,1)S(1)}, bf16[2048,1024]{1,0:T(8,128)(2,1)}, u32[]{:S(2)}) copy-start(bf16[2048,1024]{1,0:T(8,128)(2,1)} %param.4) | copy-start | bytes 12582916
  49.0 7.9 %copy-start = (s32[32]{0:T(128)S(1)}, s32[32]{0:T(128)}, u32[]{:S(2)}) copy-start(s32[32]{0:T(128)} %param.5) | copy-start | bytes 388
  49.0 14.4 %collective-permute-start.1 = (bf16[256,2048]{1,0:T(8,128)(2,1)S(1)}, bf16[256,2048]{1,0:T(8,128)(2,1)S(1)}, u32[]{:S(2)}, u32[]{:S(2)}) collective-permute-start(bf16[256,2048]{1,0:T(8,128)(2,1)S(1)} %bitcast.35), channel_id=1, source_target_pairs={{0,32},{32,0},{1,33},{33,1},{2,34},{34,2},{3,35},{35,3},{4,36},{36... | collective-permute-start | bytes 3145736 | tf_op jit(solution)/shard_map/ppermute | solution.py:39
  51.2 7.0 %collective-permute-start.2 = (bf16[256,2048]{1,0:T(8,128)(2,1)S(1)}, bf16[256,2048]{1,0:T(8,128)(2,1)S(1)}, u32[]{:S(2)}, u32[]{:S(2)}) collective-permute-start(bf16[256,2048]{1,0:T(8,128)(2,1)S(1)} %bitcast.37), channel_id=1, source_target_pairs={{0,32},{32,0},{1,33},{33,1},{2,34},{34,2},{3,35},{35,3},{4,36},{36... | collective-permute-start | bytes 3145736 | tf_op jit(solution)/shard_map/ppermute | solution.py:39
  54.9 11.1 %collective-permute-start = (f16[4,2,32,1024]{3,2,1,0:T(8,128)(2,1)S(1)}, f16[4,2,32,1024]{3,2,1,0:T(8,128)(2,1)S(1)}, u32[]{:S(2)}, u32[]{:S(2)}) collective-permute-start(f16[4,2,32,1024]{3,2,1,0:T(8,128)(2,1)S(1)} %bitcast.43), channel_id=1, source_target_pairs={{0,4},{4,0},{8,12},{12,8},{16,20},{20,16},{24,28},{28,24},{32,60},... | collective-permute-start | bytes 1572872 | tf_op jit(solution)/shard_map/ppermute | solution.py:42
  59.5 12.2 %collective-permute-start.3 = (f16[4,2,32,1024]{3,2,1,0:T(8,128)(2,1)S(1)}, f16[4,2,32,1024]{3,2,1,0:T(8,128)(2,1)S(1)}, u32[]{:S(2)}, u32[]{:S(2)}) collective-permute-start(f16[4,2,32,1024]{3,2,1,0:T(8,128)(2,1)S(1)} %bitcast.44), channel_id=1, source_target_pairs={{0,4},{4,0},{8,12},{12,8},{16,20},{20,16},{24,28},{28,24},{32,60},... | collective-permute-start | bytes 1572872 | tf_op jit(solution)/shard_map/ppermute | solution.py:42

commit v14 on v11

--- a/solution.py
+++ b/solution.py
@@ -22,7 +22,7 @@
     pairs += [(nz + i, nz + ((i + 1) % nz if i % 2 else (i - 1) % nz)) for i in range(nz)]
     hidden, core, odd, block = lax.optimization_barrier((hidden, core, odd, block * nx))
 
-    mine = spread(spread(hidden, "yh", yh), ("x", "yl"), 2 * nx).reshape(xh, 2, 2, yh, n, k)
+    mine = spread(spread(hidden, ("yl", "yh"), ny), "x", nx).reshape(xh, 2, 2, yh, n, k)
     mine, tokens, core, odd, block = lax.optimization_barrier((mine, tokens, core, odd, block))
     token_block = tokens // cols - block
     token_column = lax.rem(tokens, cols)

time: 127 us -> 131 us (1.031)
  blocking collectives: 97.6 us -> 102 us
    all_to_all x3, blocking collectives: 58.1 us -> 62.6 us  [spread(): lax.all_to_all(jnp.broadcast_to(x[None], (size,) + x.shape), axis, split_...]
where the time goes in v14:
time: 131 us
  blocking collectives  102 us (78%)
  starting transfers between devices  10.8 us (8%)
  waiting for transfers between devices  7.64 us (6%)
  matrix products  5.11 us (4%)
  other arithmetic  3 us (2%)
  local copies, waits for them, and re-layouts  1.49 us (1%)
    all_to_all x3, blocking collectives, spread(): lax.all_to_all(jnp.broadcast_to(x[None], (size,) + x.shape), axis, split_...  62.6 us
    all_to_all x1, blocking collectives, local(): lax.all_to_all(pair.reshape(nx * zh, 2 * n, cols), ('x', 'zh'), split_axi...  39.3 us
    ppermute x2, waiting for transfers between devices, partner(): return lax.ppermute(part.astype(F16), ('core',) + Z, pairs).astype(F32)  7.63 us
    ppermute x2, starting transfers between devices, partner(): return lax.ppermute(part.astype(F16), ('core',) + Z, pairs).astype(F32)  6.2 us
    dot_general x4, matrix products, product(): part = jnp.dot(rows, head_weight, preferred_element_type=F32)  5.11 us
    ppermute x2, starting transfers between devices, swapped(): return lax.ppermute(rows, 'core', [(0, 1), (1, 0)])  4.59 us
  transfers between devices with their start and end apart: 4, of which 2 were waited for; matrix products, arithmetic and copies ran while one was open for 4% of the time, Pallas kernels for 0%

profile of v14, /device:TPU:2, one launch (start us, length us, event | category | flops | bytes accessed | tf_op | source)
XLA Modules:
  0.0 130.8 jit_solution(11783496058102995561)
XLA Ops:
  0.6 0.9 broadcast_in_dim.26
  1.5 22.0 %all_to_all.24 = bf16[8,16,2048]{2,1,0:T(8,128)(2,1)S(1)} all-to-all(bf16[8,16,2048]{2,1,0:T(8,128)(2,1)S(1)} %broadcast_in_dim.26), channel_id=1, replica_groups=mesh['yh'=4,'yl'=2,'core'=2,'zh'=4,'zl'=2,'x'=4] {'yl','yh'}, dimensions={0} | all-to-all | bytes 1048576 | tf_op jit(solution)/shard_map/all_to_all | solution.py:13
  23.6 0.2 broadcast_in_dim.27
  23.8 27.0 %all_to_all.25 = bf16[4,8,16,2048]{3,2,1,0:T(8,128)(2,1)S(1)} all-to-all(bf16[4,8,16,2048]{3,2,1,0:T(8,128)(2,1)S(1)} %broadcast_in_dim.27), channel_id=1, replica_groups=mesh['yh'=4,'yl'=2,'core'=2,'zh'=4,'zl'=2,'x'=4] {'x'}, dimensions={0} | all-to-all | bytes 4194304 | tf_op jit(solution)/shard_map/all_to_all | solution.py:13
  51.2 2.2 %collective-permute-start.1 = (bf16[256,2048]{1,0:T(8,128)(2,1)S(1)}, bf16[256,2048]{1,0:T(8,128)(2,1)S(1)}, u32[]{:S(2)}, u32[]{:S(2)}) collective-permute-start(bf16[256,2048]{1,0:T(8,128)(2,1)S(1)} %bitcast.35), channel_id=1, source_target_pairs={{0,32},{32,0},{1,33},{33,1},{2,34},{34,2},{3,35},{35,3},{4,36},{36... | collective-permute-start | bytes 3145736 | tf_op jit(solution)/shard_map/ppermute | solution.py:39
  53.4 2.4 %collective-permute-start.2 = (bf16[256,2048]{1,0:T(8,128)(2,1)S(1)}, bf16[256,2048]{1,0:T(8,128)(2,1)S(1)}, u32[]{:S(2)}, u32[]{:S(2)}) collective-permute-start(bf16[256,2048]{1,0:T(8,128)(2,1)S(1)} %bitcast.37), channel_id=1, source_target_pairs={{0,32},{32,0},{1,33},{33,1},{2,34},{34,2},{3,35},{35,3},{4,36},{36... | collective-permute-start | bytes 3145736 | tf_op jit(solution)/shard_map/ppermute | solution.py:39
  55.8 1.3 convolution_convert_fusion.1
  57.1 4.3 %collective-permute-start = (f16[8,32,1024]{2,1,0:T(8,128)(2,1)S(1)}, f16[8,32,1024]{2,1,0:T(8,128)(2,1)S(1)}, u32[]{:S(2)}, u32[]{:S(2)}) collective-permute-start(f16[8,32,1024]{2,1,0:T(8,128)(2,1)S(1)} %bitcast.43), channel_id=1, source_target_pairs={{0,4},{4,0},{8,12},{12,8},{16,20},{20,16},{24,28},{28,24},{32,60},... | collective-permute-start | bytes 1572872 | tf_op jit(solution)/shard_map/ppermute | solution.py:42
  61.4 1.3 fusion.3
  62.7 1.3 convolution_convert_fusion
  64.0 1.9 %collective-permute-start.3 = (f16[8,32,1024]{2,1,0:T(8,128)(2,1)S(1)}, f16[8,32,1024]{2,1,0:T(8,128)(2,1)S(1)}, u32[]{:S(2)}, u32[]{:S(2)}) collective-permute-start(f16[8,32,1024]{2,1,0:T(8,128)(2,1)S(1)} %bitcast.44), channel_id=1, source_target_pairs={{0,4},{4,0},{8,12},{12,8},{16,20},{20,16},{24,28},{28,24},{32,60},... | collective-permute-start | bytes 1572872 | tf_op jit(solution)/shard_map/ppermute | solution.py:42
  65.9 1.3 fusion.4
  67.2 1.3 %collective-permute-done = f16[8,32,1024]{2,1,0:T(8,128)(2,1)S(1)} collective-permute-done((f16[8,32,1024]{2,1,0:T(8,128)(2,1)S(1)}, f16[8,32,1024]{2,1,0:T(8,128)(2,1)S(1)}, u32[]{:S(2)}, u32[]{:S(2)}) %collective-permute-start) | collective-permute-done | bytes 524320 | tf_op jit(solution)/shard_map/ppermute | solution.py:42
  68.5 0.2 convert_add_fusion.1
  68.7 6.3 %collective-permute-done.3 = f16[8,32,1024]{2,1,0:T(8,128)(2,1)S(1)} collective-permute-done((f16[8,32,1024]{2,1,0:T(8,128)(2,1)S(1)}, f16[8,32,1024]{2,1,0:T(8,128)(2,1)S(1)}, u32[]{:S(2)}, u32[]{:S(2)}) %collective-permute-start.3) | collective-permute-done | bytes 524320 | tf_op jit(solution)/shard_map/ppermute | solution.py:42
  75.1 0.1 convert_add_fusion
  75.2 0.3 select_convert_fusion
  75.5 39.3 %all_to_all.26 = f16[16,32,1024]{2,1,0:T(8,128)(2,1)S(1)} all-to-all(f16[16,32,1024]{2,1,0:T(8,128)(2,1)S(1)} %bitcast.33), channel_id=1, replica_groups=mesh['yh'=4,'yl'=2,'core'=2,'zh'=4,'zl'=2,'x'=4] {'x','zh'}, dimensions={0} | all-to-all | bytes 2097152 | tf_op jit(solution)/shard_map/all_to_all | solution.py:56
  114.8 0.2 convert_reduce_fusion
  115.1 0.1 reduce_max.18
  115.3 0.3 exponential_reduce_fusion
  115.7 13.6 %all_to_all.27 = f32[16,1,96]{2,1,0:T(1,128)S(1)} all-to-all(f32[16,1,96]{2,1,0:T(1,128)S(1)} %broadcast_in_dim.48), channel_id=1, replica_groups=mesh['yh'=4,'yl'=2,'core'=2,'zh'=4,'zl'=2,'x'=4] {'core','yl','yh'}, dimensions={0} | all-to-all | bytes 12288 | tf_op jit(solution)/shard_map/all_to_all | solution.py:13
  129.3 0.5 subtract_subtract_fusion.1
  129.9 0.9 subtract_subtract_fusion
  (16 shorter events, 0.6 us)
Async XLA Ops:
  50.8 4.9 %copy-start.1 = (bf16[2048,1024]{1,0:T(8,128)(2,1)S(1)}, bf16[2048,1024]{1,0:T(8,128)(2,1)}, u32[]{:S(2)}) copy-start(bf16[2048,1024]{1,0:T(8,128)(2,1)} %param.4) | copy-start | bytes 12582916
  51.2 10.2 %copy-start = (s32[32]{0:T(128)S(1)}, s32[32]{0:T(128)}, u32[]{:S(2)}) copy-start(s32[32]{0:T(128)} %param.5) | copy-start | bytes 388
  51.2 14.7 %collective-permute-start.1 = (bf16[256,2048]{1,0:T(8,128)(2,1)S(1)}, bf16[256,2048]{1,0:T(8,128)(2,1)S(1)}, u32[]{:S(2)}, u32[]{:S(2)}) collective-permute-start(bf16[256,2048]{1,0:T(8,128)(2,1)S(1)} %bitcast.35), channel_id=1, source_target_pairs={{0,32},{32,0},{1,33},{33,1},{2,34},{34,2},{3,35},{35,3},{4,36},{36... | collective-permute-start | bytes 3145736 | tf_op jit(solution)/shard_map/ppermute | solution.py:39
  53.4 9.3 %collective-permute-start.2 = (bf16[256,2048]{1,0:T(8,128)(2,1)S(1)}, bf16[256,2048]{1,0:T(8,128)(2,1)S(1)}, u32[]{:S(2)}, u32[]{:S(2)}) collective-permute-start(bf16[256,2048]{1,0:T(8,128)(2,1)S(1)} %bitcast.37), channel_id=1, source_target_pairs={{0,32},{32,0},{1,33},{33,1},{2,34},{34,2},{3,35},{35,3},{4,36},{36... | collective-permute-start | bytes 3145736 | tf_op jit(solution)/shard_map/ppermute | solution.py:39
  57.1 11.4 %collective-permute-start = (f16[8,32,1024]{2,1,0:T(8,128)(2,1)S(1)}, f16[8,32,1024]{2,1,0:T(8,128)(2,1)S(1)}, u32[]{:S(2)}, u32[]{:S(2)}) collective-permute-start(f16[8,32,1024]{2,1,0:T(8,128)(2,1)S(1)} %bitcast.43), channel_id=1, source_target_pairs={{0,4},{4,0},{8,12},{12,8},{16,20},{20,16},{24,28},{28,24},{32,60},... | collective-permute-start | bytes 1572872 | tf_op jit(solution)/shard_map/ppermute | solution.py:42
  64.0 11.1 %collective-permute-start.3 = (f16[8,32,1024]{2,1,0:T(8,128)(2,1)S(1)}, f16[8,32,1024]{2,1,0:T(8,128)(2,1)S(1)}, u32[]{:S(2)}, u32[]{:S(2)}) collective-permute-start(f16[8,32,1024]{2,1,0:T(8,128)(2,1)S(1)} %bitcast.44), channel_id=1, source_target_pairs={{0,4},{4,0},{8,12},{12,8},{16,20},{20,16},{24,28},{28,24},{32,60},... | collective-permute-start | bytes 1572872 | tf_op jit(solution)/shard_map/ppermute | solution.py:42
